TPU v7x, 32 devices: a whole 2x2x4 slice. The times are simulated.
32 devices in a mesh: section: 4 (over y, x), coil: 4 (over z), cuts: 2 (over core).
Axes of the slice: x: 2, y: 2, z: 4, core: 2. Of those that a mesh axis runs over, the one named last changes fastest.
Arguments:
- initial: bfloat16 [2, 32, 80, 2, 128], P(None, 'coil', 'cuts'), may hold values from -6 to 6
- sens: bfloat16 [2, 8, 32, 80, 2, 128], P(None, ('coil', 'cuts')), may hold values from -2.5 to 2.5
- kspace: bfloat16 [2, 8, 32, 80, 2, 128], P(None, ('coil', 'cuts')), may hold values from -6 to 6
- mask: int32 [2, 80, 128], replicated, may hold values 0 or 1
- step_sizes: float32 [4], P('section'), may hold values from 0.3 to 1.5
- conv_in: bfloat16 [4, 128, 18], P('section'), may hold values from -1.5 to 1.5
- bias_in: float32 [4, 128], P('section'), may hold values from -3 to 3
- conv_out: bfloat16 [4, 18, 128], P('section'), may hold values from -0.1875 to 0.1875
Outputs:
- cascade_images: bfloat16 [4, 2, 32, 80, 2, 128], P('section', None, 'coil', 'cuts')
Inputs may be any that keep to these rules, and one draw needn't show every extreme that they name: `mask`: 1 marks a sampled phase-encoding line of the slab, 0 one that was not measured.
All inputs are finite; a program needn't handle non-finite values.
Results may differ from a plain program's by a relative error of at most 0.028.
Values may be sent and summed in bfloat16 or wider, within the bound.
No kernel may reach another device: no remote copies, remote signals or barrier semaphores. Data moves between devices by JAX's collectives and lax.ppermute only.
A program may use at most 128 MiB of HBM per device.

v0:
```python
import functools
import math

import jax
import jax.numpy as jnp
import ml_dtypes
import numpy as np
from jax import lax
from jax.experimental import pallas as pl
from jax.experimental.pallas import tpu as pltpu
from jax.sharding import PartitionSpec as P

INTERPRET = False
BF16, F32 = jnp.bfloat16, jnp.float32
TILE = 8


def dft_table(length, sign):
    ramp = np.arange(length)
    angle = (ramp[:, None] * ramp[None, :] % length) * (2.0 * math.pi / length)
    cosine = np.cos(angle) / math.sqrt(length)
    sine = sign * np.sin(angle) / math.sqrt(length)
    return np.block([[cosine, -sine], [sine, cosine]]).astype(ml_dtypes.bfloat16)


def peers(axis):
    count = lax.axis_size(axis)
    me = lax.axis_index(axis)
    for k in range(1, count):
        if count & (count - 1) == 0:
            yield [(j, j ^ k) for j in range(count)], jnp.bitwise_xor(me, k), jnp.bitwise_xor(me, k)
        else:
            route = [(j, (j + k) % count) for j in range(count)]
            yield route, (me + k) % count, (me - k) % count


def exchange(piece_for, axis):
    arrived = [piece_for(lax.axis_index(axis))]
    for route, target, _ in peers(axis):
        arrived.append(lax.ppermute(piece_for(target), axis, route))
    return arrived


def step_to(index, axis):
    count = lax.axis_size(axis)
    me = lax.axis_index(axis)
    if count & (count - 1) == 0:
        return jnp.bitwise_xor(me, index)
    return (me - index) % count


def conj_product(a, b):
    ar, ai = a[..., 0, :, :].astype(jnp.float32), a[..., 1, :, :].astype(jnp.float32)
    br, bi = b[..., 0, :, :].astype(jnp.float32), b[..., 1, :, :].astype(jnp.float32)
    return jnp.stack([ar * br + ai * bi, ar * bi - ai * br], axis=-3)


def pass_z(v, table):
    length = v.shape[-1]
    split = table.reshape(2, length, 2, length)
    return jnp.einsum("...cyz,czdw->...dyw", v, split, preferred_element_type=jnp.float32).astype(jnp.bfloat16)


def pass_y(v, table):
    length = v.shape[-2]
    split = table.reshape(2, length, 2, length)
    return jnp.einsum("...cyz,cydk->...dkz", v, split, preferred_element_type=jnp.float32).astype(jnp.bfloat16)


def selections():
    chosen = np.zeros((4 * 4 * TILE + TILE, 42), np.float32)
    for dy in range(3):
        for dz in range(3):
            for part in range(2):
                tap = (3 * dy + dz) * 2 + part
                for row in range(2):
                    chosen[row * 32 + (row + dy) * TILE + dz * 2 + part, tap] = 0.5
                    chosen[64 + row * 32 + (row + 2 - dy) * TILE + dz * 2 + part, 21 + tap] = 1.0
    for row in range(2):
        for piece, at in enumerate((TILE + 6, TILE + 7, 2 * TILE + 6)):
            chosen[row * 32 + at, 18 + piece] = 0.5
    for piece in range(3):
        chosen[128 + piece, 39 + piece] = 1.0
    return chosen.astype(ml_dtypes.bfloat16)


def in_three(x):
    high = lax.reduce_precision(x, 8, 7)
    rest = x - high
    mid = lax.reduce_precision(rest, 8, 7)
    return [high, mid, rest - mid]


def pack_weights(conv_in, bias, conv_out, step):
    rows = [conv_in.astype(F32).T] + in_three(bias[None]) + [conv_out.astype(F32)]
    rows += in_three(jnp.broadcast_to(step[None], (1, bias.shape[0])))
    operand = jnp.concatenate(rows, axis=0).astype(BF16)
    return jnp.dot(jnp.asarray(selections()), operand, preferred_element_type=F32).astype(BF16)


def shifted(plane, by, width):
    lane = lax.broadcasted_iota(jnp.int32, (plane.shape[0], width), 1)
    parts = []
    for at in range(0, plane.shape[1], width):
        moved = pltpu.roll(plane[:, at : at + width], (-by) % width, 1)
        parts.append(jnp.where((lane + by >= 0) & (lane + by < width), moved, 0.0))
    return jnp.concatenate(parts, axis=1)


def refine_into(planes, weights, taps_f32, taps, products, result, width):
    rows, lanes = planes[0].shape
    for dz in range(3):
        for part in range(2):
            plane = planes[part] if dz == 1 else shifted(planes[part], dz - 1, width)
            for s in range(lanes // width):
                place = pl.ds(TILE + dz * 2 + part, rows, stride=TILE)
                taps_f32.at[s][place, :] = plane[:, s * width : (s + 1) * width]
    for s in range(lanes // width):
        taps[:, s * width : (s + 1) * width] = taps_f32[s].astype(BF16)
    packed = weights.astype(F32)
    first = jnp.concatenate([packed[0:32].T, packed[32:64].T], axis=0).astype(BF16)
    second = jnp.concatenate([weights[64:96], weights[96:128]], axis=1)

    def pair(i, carry):
        start = pl.multiple_of(i * 2 * TILE, 2 * TILE)
        half = jnp.dot(first, taps[pl.ds(start, 4 * TILE), :], preferred_element_type=F32)
        hidden = (half + half * jnp.tanh(half)).astype(BF16)
        out = jnp.dot(second, hidden, preferred_element_type=F32)
        done = out[: 2 * TILE] + carry
        for s in range(lanes // width):
            products.at[s][pl.ds(start, 2 * TILE), :] = done[:, s * width : (s + 1) * width]
        return out[2 * TILE :]

    last = lax.fori_loop(0, rows // 2, pair, jnp.zeros((2 * TILE, lanes), F32), unroll=4)
    for s in range(lanes // width):
        own = slice(s * width, (s + 1) * width)
        products.at[s][rows * TILE : (rows + 2) * TILE, :] = last[:, own]
        for part in range(2):
            total = products.at[s][pl.ds(TILE + 2 + part, rows, stride=TILE), :]
            for dz in (0, 2):
                total += shifted(products.at[s][pl.ds(TILE + dz * 2 + part, rows, stride=TILE), :], dz - 1, width)
            result[part, :, own] = total


def fill_ones(taps_f32):
    taps_f32[...] = jnp.zeros(taps_f32.shape, F32)
    slices, rows, width = taps_f32.shape
    for s in range(slices):
        for at in (6, 7):
            taps_f32.at[s][pl.ds(at, rows // TILE, stride=TILE), :] = jnp.ones((rows // TILE, width), F32)


def load_planes(image, per):
    return [jnp.concatenate([image[s, part].astype(F32) for s in range(per)], axis=1) for part in range(2)]


def first_refine_kernel(order, image, weights, result, taps_f32, taps, products):
    per, _, _, width = image.shape
    fill_ones(taps_f32)
    refine_into(load_planes(image, per), weights[order[0]], taps_f32, taps, products, result, width)


def cascades_kernel(n_sens, n_data, order, *refs):
    image, first, mask, weights, forward_z, back_z, forward_y, back_y = refs[:8]
    senses, datas = refs[8 : 8 + n_sens], refs[8 + n_sens : 8 + n_sens + n_data]
    out = refs[8 + n_sens + n_data]
    taps_f32, taps, products, refined, planes, gradient, rows_z, rows_y = refs[9 + n_sens + n_data :]
    per, _, height, width = image.shape
    cascades = out.shape[0]
    fill_ones(taps_f32)
    refined[...] = first[...]
    for part, plane in enumerate(load_planes(image, per)):
        planes[part] = plane
    weight_mask = jnp.concatenate([mask[...]] * 2, axis=0)

    def place(piece, q, s):
        before = sum(r.shape[0] for r in senses[:piece])
        return (before + q) * per + s

    def each_coil(step):
        for piece, ref in enumerate(senses):
            if ref.shape[0] <= 8:
                for q in range(ref.shape[0]):
                    step(piece, ref, q)
            else:
                lax.fori_loop(0, ref.shape[0], lambda q, _: step(piece, ref, q), None)

    def aligned(start):
        return start if isinstance(start, int) else pl.multiple_of(start, 16)

    def cascade(c, _):
        def product(piece, ref, q):
            for s in range(per):
                lanes = slice(s * width, (s + 1) * width)
                sr, si = ref[q, s, 0].astype(F32), ref[q, s, 1].astype(F32)
                ir, ii = planes[0, :, lanes], planes[1, :, lanes]
                coil = jnp.concatenate([sr * ir - si * ii, sr * ii + si * ir], axis=1).astype(BF16)
                w = jnp.dot(coil, forward_z[...], preferred_element_type=F32).astype(BF16)
                w = jnp.concatenate([w[:, :width], w[:, width:]], axis=0)
                rows_y[place(piece, q, s)] = w

        each_coil(product)
        planes_count = rows_y.shape[0]

        def line(b, _):
            w = jnp.dot(forward_y[...], rows_y[b], preferred_element_type=F32)
            w = (w * weight_mask).astype(BF16)
            w = jnp.dot(back_y[...], w, preferred_element_type=F32).astype(BF16)
            rows_z[b] = jnp.concatenate([w[:height], w[height:]], axis=1)

        lax.fori_loop(0, planes_count, line, None, unroll=4)
        for s in range(per):
            lanes = slice(s * width, (s + 1) * width)
            for part in range(2):
                gradient[part, :, lanes] = sum(d[s, part].astype(F32) for d in datas)

        def gather(piece, ref, q):
            for s in range(per):
                lanes = slice(s * width, (s + 1) * width)
                sr, si = ref[q, s, 0].astype(F32), ref[q, s, 1].astype(F32)
                w = jnp.dot(rows_z[place(piece, q, s)], back_z[...], preferred_element_type=F32)
                br, bi = w[:, :width], w[:, width:]
                gradient[0, :, lanes] -= sr * br + si * bi
                gradient[1, :, lanes] -= sr * bi - si * br

        each_coil(gather)
        now = weights[order[c]]
        step = sum(now[128 + piece : 129 + piece, 0:1].astype(F32) for piece in range(3))
        for part in range(2):
            new = (planes[part] - step * gradient[part] + refined[part]).astype(BF16)
            for s in range(per):
                out[c, s, part] = new[:, s * width : (s + 1) * width]
            planes[part] = new.astype(F32)

        @pl.when(c + 1 < cascades)
        def _():
            refine_into(
                [planes[0], planes[1]], weights[order[c + 1]], taps_f32, taps, products, refined, width
            )

    lax.fori_loop(0, cascades, cascade, None)


def refine_scratch(height, per, width):
    rows = (height + 2) * TILE
    return [
        pltpu.VMEM((per, rows, width), F32),
        pltpu.VMEM((rows, per * width), BF16),
        pltpu.VMEM((per, rows, width), F32),
    ]


SMEM = pl.BlockSpec(memory_space=pltpu.SMEM)
VMEM = pl.BlockSpec(memory_space=pltpu.VMEM)


def first_refine(order, image, weights):
    per, _, height, width = image.shape
    return pl.pallas_call(
        first_refine_kernel,
        out_shape=jax.ShapeDtypeStruct((2, height, per * width), F32),
        in_specs=[SMEM, VMEM, VMEM],
        out_specs=VMEM,
        scratch_shapes=refine_scratch(height, per, width),
        interpret=INTERPRET,
    )(order, image, weights)


def run_cascades(order, image, first, mask, weights, senses, datas, cascades):
    per, _, height, width = image.shape
    lanes = per * width
    count = sum(s.shape[0] for s in senses) * per
    tables = [
        dft_table(width, 1.0),
        dft_table(width, -1.0),
        dft_table(height, 1.0).T.copy(),
        dft_table(height, -1.0).T.copy(),
    ]
    args = [image, first, mask, weights] + [jnp.asarray(t) for t in tables] + list(senses) + list(datas)
    return pl.pallas_call(
        functools.partial(cascades_kernel, len(senses), len(datas)),
        out_shape=jax.ShapeDtypeStruct((cascades, per, 2, height, width), BF16),
        in_specs=[SMEM] + [VMEM] * len(args),
        out_specs=VMEM,
        scratch_shapes=refine_scratch(height, per, width)
        + [
            pltpu.VMEM((2, height, lanes), F32),
            pltpu.VMEM((2, height, lanes), F32),
            pltpu.VMEM((2, height, lanes), F32),
            pltpu.VMEM((count, height, 2 * width), BF16),
            pltpu.VMEM((count, 2 * height, width), BF16),
        ],
        interpret=INTERPRET,
    )(order, *args)


def body(initial, sens, kspace, mask, step_sizes, conv_in, bias_in, conv_out):
    bf16 = BF16
    slabs, _, size_x, size_y, _, size_z = sens.shape
    sections, cuts, coils = lax.axis_size("section"), lax.axis_size("cuts"), lax.axis_size("coil")
    section, cut = lax.axis_index("section"), lax.axis_index("cuts")
    halves = sections // slabs
    slab, half = section // halves, section % halves
    owned = size_x // coils
    by_half = math.gcd(owned, halves)
    by_cut = math.gcd(owned // by_half, cuts)
    per = owned // (by_half * by_cut)
    run = by_cut * per
    half_block = half * by_half // halves
    rows = size_y // cuts

    def cut_block(which):
        return which * by_cut // cuts

    packed = pack_weights(conv_in[0], bias_in[0], conv_out[0], step_sizes)
    params = jnp.stack(exchange(lambda _: packed, "section"), axis=0)

    cascade_order = jnp.stack([step_to(jnp.int32(c), "section") for c in range(sections)])

    mine = lax.dynamic_index_in_dim(initial, slab, 0, keepdims=False)
    mine = lax.dynamic_slice_in_dim(mine, half_block * run, run, 0)
    mine = jnp.swapaxes(mine, 1, 2)

    halves_of_rows = exchange(
        lambda to: lax.dynamic_slice_in_dim(mine, cut_block(to) * per, per, 0), "cuts"
    )
    order = [step_to(jnp.int32(i), "cuts") for i in range(cuts)]
    stacked_rows = jnp.stack(halves_of_rows, axis=0)
    image = jnp.concatenate(
        [lax.dynamic_index_in_dim(stacked_rows, at, 0, keepdims=False) for at in order], axis=2
    )

    def over_coils(array):
        def for_coil(to):
            return lax.dynamic_slice_in_dim(array, to * run, run, 0)

        columns = jnp.stack(exchange(for_coil, "coil"), axis=0)
        return exchange(
            lambda to: lax.dynamic_slice_in_dim(columns, cut_block(to) * per, per, 1), "cuts"
        )

    def half_slices(array, dim):
        shape = array.shape
        split = array.reshape(shape[:dim] + (coils, by_half, run) + shape[dim + 1 :])
        part = lax.dynamic_index_in_dim(split, half_block, dim + 1, keepdims=False)
        return part.reshape(shape[:dim] + (coils * run,) + shape[dim + 1 :])

    sens_one = lax.dynamic_index_in_dim(sens, slab, 0, keepdims=False)[0]
    sens_half = jnp.swapaxes(half_slices(sens_one, 0), 1, 2)
    senses = over_coils(sens_half)

    data_one = lax.dynamic_index_in_dim(kspace, slab, 0, keepdims=False)[0]
    mask_one = lax.dynamic_index_in_dim(mask, slab, 0, keepdims=False).astype(bf16)
    back_x = half_slices(jnp.asarray(dft_table(size_x, -1.0)).reshape(2, size_x, 2, size_x), 3)
    back_y, back_z = jnp.asarray(dft_table(size_y, -1.0)), jnp.asarray(dft_table(size_z, -1.0))
    spectrum = jnp.einsum("jycz,cjdk->kdyz", data_one, back_x, preferred_element_type=jnp.float32)
    spectrum = spectrum.astype(bf16) * mask_one
    back = pass_z(pass_y(spectrum, back_y), back_z)
    term = conj_product(sens_half, back).reshape((coils, by_cut, per, 2, size_y, size_z))
    pair = exchange(
        lambda to: lax.dynamic_index_in_dim(term, cut_block(to), 1, keepdims=False).astype(bf16), "cuts"
    )
    pair = sum(p.astype(jnp.float32) for p in pair)
    datas = exchange(lambda to: lax.dynamic_index_in_dim(pair, to, 0, keepdims=False).astype(bf16), "coil")

    first = first_refine(cascade_order, image, params)
    images = run_cascades(
        cascade_order, image, first, mask_one.astype(F32), params, senses, datas, sections
    )
    out = images.reshape(sections, per, 2, cuts, rows, size_z)
    out = jnp.transpose(out, (0, 3, 1, 4, 2, 5)).reshape(sections * cuts, per, rows, 2, size_z)
    out = lax.all_to_all(out, ("section", "cuts"), 0, 0, tiled=True)
    out = out.reshape(slabs, halves, cuts, per, rows, 2, size_z)[:, :: halves // by_half, :: cuts // by_cut]
    return out.reshape(1, slabs, owned, rows, 2, size_z)


def solution(mesh):
    return jax.shard_map(
        body,
        mesh=mesh,
        in_specs=(
            P(None, "coil", "cuts", None, None),
            P(None, ("coil", "cuts"), None, None, None, None),
            P(None, ("coil", "cuts"), None, None, None, None),
            P(),
            P("section"),
            P("section", None, None),
            P("section", None),
            P("section", None, None),
        ),
        out_specs=P("section", None, "coil", "cuts", None, None),
        check_vma=False,
    )
```

profile of v0, /device:TPU:0, one launch (start us, length us, event | category | flops | bytes accessed | tf_op | source)
XLA Modules:
  0.0 112.6 jit_solution(9583381496593971669)
XLA Ops:
  4.5 0.7 fusion.37
  5.1 0.7 broadcast_multiply_fusion.2
  5.8 0.7 broadcast_multiply_fusion
  6.5 1.0 fusion.12
  7.5 0.9 fusion.13
  8.4 3.0 %collective-permute-start.1 = (bf16[136,128]{1,0:T(8,128)(2,1)S(1)}, bf16[136,128]{1,0:T(8,128)(2,1)S(1)}, u32[]{:S(2)}, u32[]{:S(2)}) collective-permute-start(bf16[136,128]{1,0:T(8,128)(2,1)S(1)} %bitcast.187), channel_id=1, source_target_pairs={{0,8},{8,0},{16,24},{24,16},{1,9},{9,1},{17,25},{25,17},{2,10},{10... | collective-permute-start | bytes 104456 | tf_op jit(solution)/shard_map/ppermute | solution.py:40
  11.4 1.5 %collective-permute-start.2 = (bf16[136,128]{1,0:T(8,128)(2,1)S(1)}, bf16[136,128]{1,0:T(8,128)(2,1)S(1)}, u32[]{:S(2)}, u32[]{:S(2)}) collective-permute-start(bf16[136,128]{1,0:T(8,128)(2,1)S(1)} %bitcast.188), channel_id=1, source_target_pairs={{0,16},{8,24},{16,0},{24,8},{1,17},{9,25},{17,1},{25,9},{2,18},{10... | collective-permute-start | bytes 104456 | tf_op jit(solution)/shard_map/ppermute | solution.py:40
  13.0 0.0 collective-permute-start.3
  13.0 0.9 constant_dynamic-slice_fusion.4
  13.9 0.0 copy-start.3
  13.9 1.2 %copy.35 = bf16[1,1,32,80,2,128]{5,3,4,2,1,0:T(8,128)(2,1)} copy(bf16[1,1,32,80,2,128]{5,4,3,2,1,0:T(2,128)(2,1)S(1)} %constant_dynamic-slice_fusion.4) | data formatting | bytes 2621440
  15.1 1.0 copy-done.3
  16.1 2.0 %dynamic-slice_bitcast_fusion = bf16[32,80,2,128,1]{3,2,1,0,4:T(2,128)(2,1)} fusion(bf16[2,1,32,80,2,128]{5,4,3,2,1,0:T(2,128)(2,1)S(1)} %copy-done.3, s32[]{:T(128)S(6)} %select_n.98), kind=kLoop, calls=%fused_computation.11 | loop fusion | bytes 2621444 | tf_op jit(solution)/shard_map/squeeze | solution.py:352
  18.1 1.2 %constant_dynamic-slice_fusion.3 = bf16[4,1,4,80,2,128]{5,3,4,2,1,0:T(8,128)(2,1)S(1)} fusion(bf16[4,2,4,80,2,128]{5,3,4,2,1,0:T(8,128)(2,1)} %bitcast.174, s32[]{:T(128)S(6)} %select_n.112), kind=kLoop, calls=%fused_computation.71 | loop fusion | bytes 1310724 | tf_op jit(solution)/shard_map/jit(dynamic_index_in_dim)/dynamic_slice | solution.py:345
  19.4 0.6 fusion.43
  20.0 1.4 %fusion.2 = bf16[2,16,80,128,1]{3,1,4,2,0:T(8,128)(2,1)} fusion(bf16[32,80,2,128,1]{3,2,1,0,4:T(2,128)(2,1)S(1)} %copy-done.1, bf16[2,32,2,16,1]{1,3,2,0,4:T(8,128)(2,1)S(1)} %bitcast.184), kind=kOutput, calls=%fused_computation.9 | convolution fusion | flops 41943040 | bytes 1970176 | tf_op jit(solution)/shard_map/jycz,cjdk->kdyz/dot_general | solution.py:356
  21.4 2.6 %fusion.4 = bf16[16,2,80,128]{3,2,1,0:T(8,128)(2,1)} fusion(bf16[2,128,2,128,1]{3,1,0,2,4:T(8,128)(2,1)} %constant.237, bf16[2,80,2,80,1]{3,1,0,2,4:T(8,128)(2,1)} %constant.236, bf16[2,16,80,128,1]{3,1,4,2,0:T(8,128)(2,1)} %fusion.2, bf16[80,128]{1,0:T(8,128)(2,1)S(1)} %get-tuple-element.6), kind=kOutput, calls=%fused_computation.12 | convolution fusion | flops 273612800 | bytes 1513472 | tf_op jit(solution)/shard_map/...cyz,czdw->...dyw/dot_general | solution.py:61
  24.0 2.2 %fusion.15 = (bf16[16,1,80,128]{3,2,1,0:T(8,128)(2,1)}, bf16[16,1,80,128]{3,2,1,0:T(8,128)(2,1)}) fusion(bf16[16,2,80,128]{3,2,1,0:T(8,128)(2,1)} %fusion.4, bf16[16,2,80,128]{3,2,1,0:T(8,128)(2,1)S(1)} %bitcast.172), kind=kLoop, calls=%fused_computation.29 | loop fusion | flops 1966080 | bytes 1966080 | tf_op jit(solution)/shard_map/sub | solution.py:55
  26.2 1.9 %fusion.19 = (bf16[4,1,2,2,80,128]{5,4,2,1,0,3:T(8,128)(2,1)}, bf16[4,1,2,2,80,128]{5,4,2,1,0,3:T(8,128)(2,1)S(1)}) fusion(s32[]{:T(128)S(6)} %select_n.117, bf16[4,2,2,1,80,128]{5,4,2,1,0,3:T(8,128)(2,1)} %bitcast.179, bf16[4,2,2,1,80,128]{5,4,2,1,0,3:T(8,128)(2,1)} %bitcast.178, s32[]{:T(128)S(6)} %select_n.118), kind=kLoop, calls=%fused_computation.33 | loop fusion | flops 327680 | bytes 1310728 | tf_op jit(solution)/shard_map/stack | solution.py:55
  28.1 0.8 copy.63
  28.9 0.8 dynamic-slice_bitcast_fusion.4
  29.7 2.0 %collective-permute-start.4 = (bf16[4,2,80,128]{3,2,1,0:T(8,128)(2,1)}, bf16[4,2,80,128]{3,2,1,0:T(8,128)(2,1)S(1)}, u32[]{:S(2)}, u32[]{:S(2)}) collective-permute-start(bf16[4,2,80,128]{3,2,1,0:T(8,128)(2,1)} %get-tuple-element.16), channel_id=1, source_target_pairs={{0,2},{2,0},{4,6},{6,4},{1,3},{3,1},{5,7},{7,5},{8,10},{10,8},{12,... | collective-permute-start | bytes 491528 | tf_op jit(solution)/shard_map/ppermute | solution.py:40
  31.7 0.9 constant_dynamic-slice_fusion.5
  32.6 0.7 pad_add_fusion.order
  33.3 2.7 %collective-permute-start.5 = (bf16[4,2,80,128]{3,2,1,0:T(8,128)(2,1)}, bf16[4,2,80,128]{3,2,1,0:T(8,128)(2,1)S(1)}, u32[]{:S(2)}, u32[]{:S(2)}) collective-permute-start(bf16[4,2,80,128]{3,2,1,0:T(8,128)(2,1)} %get-tuple-element.15), channel_id=1, source_target_pairs={{0,4},{2,6},{4,0},{6,2},{1,5},{3,7},{5,1},{7,3},{8,12},{10,14},{12... | collective-permute-start | bytes 491528 | tf_op jit(solution)/shard_map/ppermute | solution.py:40
  35.9 0.0 collective-permute-start.6
  35.9 0.0 collective-permute-done.3
  35.9 0.1 collective-permute-start
  36.0 1.4 %pad_maximum_fusion.1.weights.refs_3_ = bf16[4,136,128]{2,1,0:T(8,128)(2,1)} fusion(bf16[1,136,128]{2,1,0:T(8,128)(2,1)} %bitcast.26, bf16[1,136,128]{2,1,0:T(8,128)(2,1)S(1)} %bitcast.192, bf16[1,136,128]{2,1,0:T(8,128)(2,1)S(1)} %bitcast.191, bf16[1,136,128]{2,1,0:T(8,128)(2,1)S(1)} %bitcast.190), kind=kLoop, calls=%fused_computation.49 | loop fusion | flops 208896 | bytes 278528 | tf_op jit(solution)/shard_map/stack | solution.py:316
  37.5 0.0 collective-permute-done
  37.5 11.0 %collective-permute-done.5 = bf16[4,2,80,128]{3,2,1,0:T(8,128)(2,1)S(1)} collective-permute-done((bf16[4,2,80,128]{3,2,1,0:T(8,128)(2,1)}, bf16[4,2,80,128]{3,2,1,0:T(8,128)(2,1)S(1)}, u32[]{:S(2)}, u32[]{:S(2)}) %collective-permute-start.5) | collective-permute-done | bytes 163872 | tf_op jit(solution)/shard_map/ppermute | solution.py:40
  48.6 0.1 pad_maximum_fusion
  48.6 0.8 constant_dynamic-slice_fusion.1
  49.4 0.1 copy-done.2
  49.5 1.1 convert_add_fusion
  50.6 0.7 fusion.27
  51.3 4.4 %collective-permute-start.10 = (bf16[2,2,80,128]{3,2,1,0:T(8,128)(2,1)}, bf16[2,2,80,128]{3,2,1,0:T(8,128)(2,1)S(1)}, u32[]{:S(2)}, u32[]{:S(2)}) collective-permute-start(bf16[2,2,80,128]{3,2,1,0:T(8,128)(2,1)} %get-tuple-element.18), channel_id=1, source_target_pairs={{0,4},{2,6},{4,0},{6,2},{1,5},{3,7},{5,1},{7,3},{8,12},{10,14},{12... | collective-permute-start | bytes 245768 | tf_op jit(solution)/shard_map/ppermute | solution.py:40
  55.7 1.3 %collective-permute-start.11 = (bf16[2,2,80,128]{3,2,1,0:T(8,128)(2,1)}, bf16[2,2,80,128]{3,2,1,0:T(8,128)(2,1)S(1)}, u32[]{:S(2)}, u32[]{:S(2)}) collective-permute-start(bf16[2,2,80,128]{3,2,1,0:T(8,128)(2,1)} %get-tuple-element.17), channel_id=1, source_target_pairs={{0,6},{2,4},{4,2},{6,0},{1,7},{3,5},{5,3},{7,1},{8,14},{10,12},{12... | collective-permute-start | bytes 245768 | tf_op jit(solution)/shard_map/ppermute | solution.py:40
  57.0 0.6 pad_maximum_fusion.2.image.refs_0_
  57.7 8.0 %shard_map.154.refs_1_ = f32[2,80,256]{2,1,0:T(8,128)} custom-call(s32[4]{0:T(128)} %pad_add_fusion.order, bf16[2,2,80,128]{3,2,1,0:T(8,128)(2,1)} %pad_maximum_fusion.2.image.refs_0_, bf16[4,136,128]{2,1,0:T(8,128)(2,1)} %pad_maximum_fusion.1.weights.refs_3_), custom_call_target="tpu_custom_call" | custom-call | tf_op jit(solution)/shard_map/pallas_call | solution.py:259
  65.7 0.6 copy-done.5
  66.3 0.0 copy-done.6
  66.3 0.0 copy-done.7
  66.4 0.1 copy-done.4
  66.5 33.0 %shard_map.155 = bf16[4,2,2,80,128]{4,3,2,1,0:T(8,128)(2,1)} custom-call(s32[4]{0:T(128)} %pad_add_fusion.order, bf16[2,2,80,128]{3,2,1,0:T(8,128)(2,1)} %pad_maximum_fusion.2.image.refs_0_, f32[2,80,256]{2,1,0:T(8,128)} %shard_map.154.refs_1_, f32[80,128]{1,0:T(8,128)} %get-tuple-element.5.refs_2_, bf16[4,136,128]{2,1,0:T(8,128)(2,1)} %pad_maximum_fusion.1.weights.refs_3_, ...), custom_call_target="tpu_custom_call" | custom-call | tf_op jit(solution)/shard_map/pallas_call | solution.py:280
  99.5 1.0 copy.22
  100.5 11.1 %all_to_all.5 = bf16[8,2,40,2,128]{4,2,3,1,0:T(8,128)(2,1)S(1)} all-to-all(bf16[8,2,40,2,128]{4,2,3,1,0:T(8,128)(2,1)S(1)} %bitcast.176), channel_id=1, replica_groups=mesh['section'=4,'coil'=4,'cuts'=2] {'section','cuts'}, dimensions={0} | all-to-all | bytes 655360 | tf_op jit(solution)/shard_map/all_to_all | solution.py:372
  111.7 1.0 copy.23
  (29 shorter events, 0.1 us)
Async XLA Ops:
  0.0 13.0 %copy-start = (bf16[2,1,32,80,2,128]{5,4,3,2,1,0:T(2,128)(2,1)S(1)}, bf16[2,1,32,80,2,128]{5,4,3,2,1,0:T(2,128)(2,1)}, u32[]{:S(2)}) copy-start(bf16[2,1,32,80,2,128]{5,4,3,2,1,0:T(2,128)(2,1)} %param.17) | copy-start | bytes 7864324
  8.4 24.9 %collective-permute-start.1 = (bf16[136,128]{1,0:T(8,128)(2,1)S(1)}, bf16[136,128]{1,0:T(8,128)(2,1)S(1)}, u32[]{:S(2)}, u32[]{:S(2)}) collective-permute-start(bf16[136,128]{1,0:T(8,128)(2,1)S(1)} %bitcast.187), channel_id=1, source_target_pairs={{0,8},{8,0},{16,24},{24,16},{1,9},{9,1},{17,25},{25,17},{2,10},{10... | collective-permute-start | bytes 104456 | tf_op jit(solution)/shard_map/ppermute | solution.py:40
  11.4 24.5 %collective-permute-start.2 = (bf16[136,128]{1,0:T(8,128)(2,1)S(1)}, bf16[136,128]{1,0:T(8,128)(2,1)S(1)}, u32[]{:S(2)}, u32[]{:S(2)}) collective-permute-start(bf16[136,128]{1,0:T(8,128)(2,1)S(1)} %bitcast.188), channel_id=1, source_target_pairs={{0,16},{8,24},{16,0},{24,8},{1,17},{9,25},{17,1},{25,9},{2,18},{10... | collective-permute-start | bytes 104456 | tf_op jit(solution)/shard_map/ppermute | solution.py:40
  13.0 23.0 %collective-permute-start.3 = (bf16[136,128]{1,0:T(8,128)(2,1)S(1)}, bf16[136,128]{1,0:T(8,128)(2,1)}, u32[]{:S(2)}, u32[]{:S(2)}) collective-permute-start(bf16[136,128]{1,0:T(8,128)(2,1)S(1)} %bitcast.189), channel_id=1, source_target_pairs={{0,24},{8,16},{16,8},{24,0},{1,25},{9,17},{17,9},{25,1},{2,26},{10... | collective-permute-start | bytes 104456 | tf_op jit(solution)/shard_map/ppermute | solution.py:40
  13.9 2.2 %copy-start.3 = (bf16[2,1,32,80,2,128]{5,4,3,2,1,0:T(2,128)(2,1)S(1)}, bf16[2,1,32,80,2,128]{5,4,3,2,1,0:T(2,128)(2,1)}, u32[]{:S(2)}) copy-start(bf16[2,1,32,80,2,128]{5,4,3,2,1,0:T(2,128)(2,1)} %param.18) | copy-start | bytes 7864324
  18.1 1.3 %copy-start.9 = (bf16[2,32,2,4,2,4]{1,5,4,3,2,0:T(4,128)(2,1)S(1)}, bf16[2,32,2,4,2,4]{1,5,4,3,2,0:T(4,128)(2,1)}, u32[]{:S(2)}) copy-start(bf16[2,32,2,4,2,4]{1,5,4,3,2,0:T(4,128)(2,1)} %constant.232) | copy-start | bytes 24580
  18.1 1.3 %copy-start.8 = (s32[2,80,128]{2,1,0:T(8,128)S(1)}, s32[2,80,128]{2,1,0:T(8,128)}, u32[]{:S(2)}) copy-start(s32[2,80,128]{2,1,0:T(8,128)} %param.19) | copy-start | bytes 245764
  18.1 1.9 %copy-start.1 = (bf16[32,80,2,128,1]{3,2,1,0,4:T(2,128)(2,1)S(1)}, bf16[32,80,2,128,1]{3,2,1,0,4:T(2,128)(2,1)}, u32[]{:S(2)}) copy-start(bf16[32,80,2,128,1]{3,2,1,0,4:T(2,128)(2,1)} %dynamic-slice_bitcast_fusion) | copy-start | bytes 3932164
  28.9 20.5 %collective-permute-start.8 = (bf16[4,2,2,80,128]{4,3,2,1,0:T(8,128)(2,1)}, bf16[4,2,2,80,128]{4,3,2,1,0:T(8,128)(2,1)}, u32[]{:S(2)}, u32[]{:S(2)}) collective-permute-start(bf16[4,2,2,80,128]{4,3,2,1,0:T(8,128)(2,1)} %bitcast.169), channel_id=1, source_target_pairs={{0,1},{1,0},{2,3},{3,2},{4,5},{5,4},{6,7},{7,6},{8,9},{9,8},{10,11... | collective-permute-start | bytes 983048 | tf_op jit(solution)/shard_map/ppermute | solution.py:40
  29.7 7.9 %collective-permute-start.4 = (bf16[4,2,80,128]{3,2,1,0:T(8,128)(2,1)}, bf16[4,2,80,128]{3,2,1,0:T(8,128)(2,1)S(1)}, u32[]{:S(2)}, u32[]{:S(2)}) collective-permute-start(bf16[4,2,80,128]{3,2,1,0:T(8,128)(2,1)} %get-tuple-element.16), channel_id=1, source_target_pairs={{0,2},{2,0},{4,6},{6,4},{1,3},{3,1},{5,7},{7,5},{8,10},{10,8},{12,... | collective-permute-start | bytes 491528 | tf_op jit(solution)/shard_map/ppermute | solution.py:40
  33.3 15.3 %collective-permute-start.5 = (bf16[4,2,80,128]{3,2,1,0:T(8,128)(2,1)}, bf16[4,2,80,128]{3,2,1,0:T(8,128)(2,1)S(1)}, u32[]{:S(2)}, u32[]{:S(2)}) collective-permute-start(bf16[4,2,80,128]{3,2,1,0:T(8,128)(2,1)} %get-tuple-element.15), channel_id=1, source_target_pairs={{0,4},{2,6},{4,0},{6,2},{1,5},{3,7},{5,1},{7,3},{8,12},{10,14},{12... | collective-permute-start | bytes 491528 | tf_op jit(solution)/shard_map/ppermute | solution.py:40
  35.9 12.6 %collective-permute-start.6 = (bf16[4,2,80,128]{3,2,1,0:T(8,128)(2,1)}, bf16[4,2,80,128]{3,2,1,0:T(8,128)(2,1)S(1)}, u32[]{:S(2)}, u32[]{:S(2)}) collective-permute-start(bf16[4,2,80,128]{3,2,1,0:T(8,128)(2,1)} %get-tuple-element.14), channel_id=1, source_target_pairs={{0,6},{2,4},{4,2},{6,0},{1,7},{3,5},{5,3},{7,1},{8,14},{10,12},{12... | collective-permute-start | bytes 491528 | tf_op jit(solution)/shard_map/ppermute | solution.py:40
  35.9 1.5 %collective-permute-start = (bf16[2,2,40,128]{3,2,1,0:T(8,128)(2,1)S(1)}, bf16[2,2,40,128]{3,2,1,0:T(8,128)(2,1)S(1)}, u32[]{:S(2)}, u32[]{:S(2)}) collective-permute-start(bf16[2,2,40,128]{3,2,1,0:T(8,128)(2,1)S(1)} %bitcast.186), channel_id=1, source_target_pairs={{0,1},{1,0},{2,3},{3,2},{4,5},{5,4},{6,7},{7,6},{8,9},{9,8},{10,11... | collective-permute-start | bytes 122888 | tf_op jit(solution)/shard_map/ppermute | solution.py:40
  48.6 1.0 copy-start.2
  49.4 16.3 %collective-permute-start.7 = (bf16[4,2,2,80,128]{4,3,2,1,0:T(8,128)(2,1)S(1)}, bf16[4,2,2,80,128]{4,3,2,1,0:T(8,128)(2,1)S(1)}, u32[]{:S(2)}, u32[]{:S(2)}) collective-permute-start(bf16[4,2,2,80,128]{4,3,2,1,0:T(8,128)(2,1)S(1)} %get-tuple-element.11), channel_id=1, source_target_pairs={{0,1},{1,0},{2,3},{3,2},{4,5},{5,4},{6,7},{7,6},{8,9},{9,8},{10,11... | collective-permute-start | bytes 983048 | tf_op jit(solution)/shard_map/ppermute | solution.py:40
  51.3 14.3 %collective-permute-start.10 = (bf16[2,2,80,128]{3,2,1,0:T(8,128)(2,1)}, bf16[2,2,80,128]{3,2,1,0:T(8,128)(2,1)S(1)}, u32[]{:S(2)}, u32[]{:S(2)}) collective-permute-start(bf16[2,2,80,128]{3,2,1,0:T(8,128)(2,1)} %get-tuple-element.18), channel_id=1, source_target_pairs={{0,4},{2,6},{4,0},{6,2},{1,5},{3,7},{5,1},{7,3},{8,12},{10,14},{12... | collective-permute-start | bytes 245768 | tf_op jit(solution)/shard_map/ppermute | solution.py:40
  55.7 10.0 %collective-permute-start.11 = (bf16[2,2,80,128]{3,2,1,0:T(8,128)(2,1)}, bf16[2,2,80,128]{3,2,1,0:T(8,128)(2,1)S(1)}, u32[]{:S(2)}, u32[]{:S(2)}) collective-permute-start(bf16[2,2,80,128]{3,2,1,0:T(8,128)(2,1)} %get-tuple-element.17), channel_id=1, source_target_pairs={{0,6},{2,4},{4,2},{6,0},{1,7},{3,5},{5,3},{7,1},{8,14},{10,12},{12... | collective-permute-start | bytes 245768 | tf_op jit(solution)/shard_map/ppermute | solution.py:40
  57.0 8.7 %collective-permute-start.9 = (bf16[2,2,80,128]{3,2,1,0:T(8,128)(2,1)}, bf16[2,2,80,128]{3,2,1,0:T(8,128)(2,1)S(1)}, u32[]{:S(2)}, u32[]{:S(2)}) collective-permute-start(bf16[2,2,80,128]{3,2,1,0:T(8,128)(2,1)} %get-tuple-element.19), channel_id=1, source_target_pairs={{0,2},{2,0},{4,6},{6,4},{1,3},{3,1},{5,7},{7,5},{8,10},{10,8},{12,... | collective-permute-start | bytes 245768 | tf_op jit(solution)/shard_map/ppermute | solution.py:40
  65.7 0.6 copy-start.5
  65.7 0.6 copy-start.6
  65.7 0.7 copy-start.7
  65.7 0.8 copy-start.4
where the time goes:
time: 113 us
  Pallas kernels  41 us (36%)
  starting transfers between devices  15 us (13%)
  local copies, waits for them, and re-layouts  13.1 us (12%)
  blocking collectives  11.1 us (10%)
  waiting for transfers between devices  11 us (10%)
  other arithmetic  10.7 us (9%)
  matrix products  5.86 us (5%)
  between operations  4.68 us (4%)
    pallas_call x1, Pallas kernels, run_cascades(): pl.pallas_call(functools.partial(cascades_kernel, len(senses), len(datas)...  33 us
    ppermute x12, starting transfers between devices, exchange(): arrived.append(lax.ppermute(piece_for(target), axis, route))  15 us
    all_to_all x1, blocking collectives, body(): out = lax.all_to_all(out, ('section', 'cuts'), 0, 0, tiled=True)  11.1 us
    ppermute x12, waiting for transfers between devices, exchange(): arrived.append(lax.ppermute(piece_for(target), axis, route))  11 us
    pallas_call x1, Pallas kernels, first_refine(): pl.pallas_call(first_refine_kernel, out_shape=jax.ShapeDtypeStruct((2, he...  8.01 us
    unnamed x24, local copies, waits for them, and re-layouts  3.84 us
    dot_general x1, matrix products, pass_z(): jnp.einsum('...cyz,czdw->...dyw', v, split, preferred_element_type=jnp.fl...  2.58 us
  transfers between devices with their start and end apart: 12, of which 1 were waited for; matrix products, arithmetic and copies ran while one was open for 20% of the time, Pallas kernels for 7%

commit v1 on v0

v1 whole, which is shorter than its diff:
```python
import functools
import math

import jax
import jax.numpy as jnp
import ml_dtypes
import numpy as np
from jax import lax
from jax.experimental import pallas as pl
from jax.experimental.pallas import tpu as pltpu
from jax.sharding import PartitionSpec as P

INTERPRET = False
BF16, F32 = jnp.bfloat16, jnp.float32
ACT = F32
GROUP = 4
TILE = 8


def dft_table(length, sign):
    ramp = np.arange(length)
    angle = (ramp[:, None] * ramp[None, :] % length) * (2.0 * math.pi / length)
    cosine = np.cos(angle) / math.sqrt(length)
    sine = sign * np.sin(angle) / math.sqrt(length)
    return np.block([[cosine, -sine], [sine, cosine]]).astype(ml_dtypes.bfloat16)


def peers(axis):
    count = lax.axis_size(axis)
    me = lax.axis_index(axis)
    for k in range(1, count):
        if count & (count - 1) == 0:
            yield [(j, j ^ k) for j in range(count)], jnp.bitwise_xor(me, k), jnp.bitwise_xor(me, k)
        else:
            route = [(j, (j + k) % count) for j in range(count)]
            yield route, (me + k) % count, (me - k) % count


def own_and_peers(axis):
    me = lax.axis_index(axis)
    yield None, me, me
    yield from peers(axis)


def step_to(index, axis):
    count = lax.axis_size(axis)
    me = lax.axis_index(axis)
    if count & (count - 1) == 0:
        return jnp.bitwise_xor(me, index)
    return (me - index) % count


SMEM = pl.BlockSpec(memory_space=pltpu.SMEM)
VMEM = pl.BlockSpec(memory_space=pltpu.VMEM)
ANY = pl.BlockSpec(memory_space=pl.ANY)


def selections():
    chosen = np.zeros((4 * 4 * TILE + TILE, 42), np.float32)
    for dy in range(3):
        for dz in range(3):
            for part in range(2):
                tap = (3 * dy + dz) * 2 + part
                for row in range(2):
                    chosen[row * 32 + (row + dy) * TILE + dz * 2 + part, tap] = 0.5
                    chosen[64 + row * 32 + (row + 2 - dy) * TILE + dz * 2 + part, 21 + tap] = 1.0
    for row in range(2):
        for piece, at in enumerate((TILE + 6, TILE + 7, 2 * TILE + 6)):
            chosen[row * 32 + at, 18 + piece] = 0.5
    for piece in range(3):
        chosen[128 + piece, 39 + piece] = 1.0
    return chosen.astype(ml_dtypes.bfloat16)


def in_three(x):
    high = x.astype(BF16)
    rest = x - high.astype(F32)
    mid = rest.astype(BF16)
    return [high, mid, (rest - mid.astype(F32)).astype(BF16)]


def pack_kernel(chosen, conv_in, bias, conv_out, step, packed):
    def picked(rows, lanes):
        return jnp.dot(chosen[:, lanes], rows, preferred_element_type=F32)

    total = picked(conv_in[...], slice(0, 18)) + picked(conv_out[...], slice(21, 39))
    steps = jnp.full(bias.shape, step[0], F32)
    for at, split in ((18, in_three(bias[...])), (39, in_three(steps))):
        for piece, row in enumerate(split):
            column = chosen[:, at + piece : at + piece + 1].astype(F32)
            total += column * row.astype(F32)
    packed[...] = total.astype(BF16)


def pack_weights(conv_in, bias, conv_out, step):
    chosen = jnp.asarray(selections())
    return pl.pallas_call(
        pack_kernel,
        out_shape=jax.ShapeDtypeStruct((chosen.shape[0], bias.shape[1]), BF16),
        in_specs=[VMEM, VMEM, VMEM, VMEM, SMEM],
        out_specs=VMEM,
        interpret=INTERPRET,
    )(chosen, conv_in.T, bias, conv_out, step)


def shifted(plane, by, width):
    lane = lax.broadcasted_iota(jnp.int32, (plane.shape[0], width), 1)
    parts = []
    for at in range(0, plane.shape[1], width):
        moved = pltpu.roll(plane[:, at : at + width], (-by) % width, 1)
        parts.append(jnp.where((lane + by >= 0) & (lane + by < width), moved, 0.0))
    return jnp.concatenate(parts, axis=1)


def refine_into(planes, weights, scratch, result, width):
    rows, lanes = planes[0].shape
    taps_f32, taps, products, halves, hidden = scratch
    for dz in range(3):
        for part in range(2):
            plane = planes[part] if dz == 1 else shifted(planes[part], dz - 1, width)
            for s in range(lanes // width):
                place = pl.ds(TILE + dz * 2 + part, rows, stride=TILE)
                taps_f32.at[s][place, :] = plane[:, s * width : (s + 1) * width]
    for s in range(lanes // width):
        taps[:, s * width : (s + 1) * width] = taps_f32[s].astype(BF16)
    packed = weights.astype(F32)
    first = jnp.concatenate([packed[0:32].T, packed[32:64].T], axis=0).astype(BF16)
    second = jnp.concatenate([weights[64:96], weights[96:128]], axis=1)

    def start_of(j, g):
        start = (j * GROUP + g) * 2 * TILE
        return start if isinstance(start, int) else pl.multiple_of(start, 2 * TILE)

    def before(j, slot, g):
        window = taps[pl.ds(start_of(j, g), 4 * TILE), :]
        halves[slot, g] = jnp.dot(first, window, preferred_element_type=F32).astype(halves.dtype)

    def activate(slot, g):
        half = halves[slot, g]
        hidden[slot, g] = (half + half * jnp.tanh(half)).astype(BF16)

    def after(j, slot, g, carry):
        out = jnp.dot(second, hidden[slot, g], preferred_element_type=F32)
        done = out[: 2 * TILE] + carry
        for s in range(lanes // width):
            products.at[s][pl.ds(start_of(j, g), 2 * TILE), :] = done[:, s * width : (s + 1) * width]
        return out[2 * TILE :]

    blocks = rows // (2 * GROUP)
    for g in range(GROUP):
        before(0, 0, g)
    for g in range(GROUP):
        activate(0, g)
        before(1, 1, g)

    def two(i, carry):
        for j, slot in ((2 * i + 1, 1), (2 * i + 2, 0)):
            for g in range(GROUP):
                carry = after(j - 1, 1 - slot, g, carry)
                activate(slot, g)
                before(j + 1, 1 - slot, g)
        return carry

    carry = lax.fori_loop(0, (blocks - 2) // 2, two, jnp.zeros((2 * TILE, lanes), F32))
    for g in range(GROUP):
        carry = after(blocks - 2, 0, g, carry)
        activate(1, g)
    for g in range(GROUP):
        carry = after(blocks - 1, 1, g, carry)
    last = carry
    for s in range(lanes // width):
        own = slice(s * width, (s + 1) * width)
        products.at[s][rows * TILE : (rows + 2) * TILE, :] = last[:, own]
        for part in range(2):
            total = products.at[s][pl.ds(TILE + 2 + part, rows, stride=TILE), :]
            for dz in (0, 2):
                total += shifted(products.at[s][pl.ds(TILE + dz * 2 + part, rows, stride=TILE), :], dz - 1, width)
            result[part, :, own] = total


def fill_ones(taps_f32):
    taps_f32[...] = jnp.zeros(taps_f32.shape, F32)
    slices, rows, width = taps_f32.shape
    for s in range(slices):
        for at in (6, 7):
            taps_f32.at[s][pl.ds(at, rows // TILE, stride=TILE), :] = jnp.ones((rows // TILE, width), F32)


def first_refine_kernel(n_rows, n_weights, *refs):
    pieces, weights = refs[:n_rows], refs[n_rows : n_rows + n_weights]
    refined, planes, stage = refs[n_rows + n_weights : n_rows + n_weights + 3]
    scratch = refs[n_rows + n_weights + 3 :]
    per, _, width = pieces[0].shape
    fill_ones(scratch[0])
    for k, (_, _, source) in enumerate(own_and_peers("cuts")):
        block = pieces[k].shape[1]
        for s in range(per):
            stage.at[s][pl.ds(pl.multiple_of(source * block, 16), block), :] = pieces[k][s].astype(F32)
    height = stage.shape[1] // 2
    for s in range(per):
        for part in range(2):
            planes[part, :, s * width : (s + 1) * width] = stage.at[s][pl.ds(part, height, stride=2), :]
    refine_into([planes[0], planes[1]], of_cascade(weights, 0), scratch, refined, width)


def of_cascade(weights, cascade):
    at = step_to(cascade, "section")
    chosen = weights[0][...]
    for k in range(1, len(weights)):
        chosen = jnp.where(at == k, weights[k][...], chosen)
    return chosen


def cascades_kernel(n_weights, n_sens, n_more, n_data, by_cut, *refs):
    planes_in, first, mask, forward_z, back_z, forward_y, back_y = refs[:7]
    at = 7
    weights, at = refs[at : at + n_weights], at + n_weights
    senses, at = refs[at : at + n_sens], at + n_sens
    more, at = refs[at : at + n_more], at + n_more
    datas, at = refs[at : at + n_data], at + n_data
    out = refs[at]
    scratch = refs[at + 1 : -8]
    refined, planes, gradient, coil_planes, rows_z, rows_y, stage, all_weights = refs[-8:]
    per, _, height, width = datas[0].shape
    cascades = len(weights)
    cuts = out.shape[0] // cascades
    slab = lax.axis_index("section") // (lax.axis_size("section") // mask.shape[0])
    fill_ones(scratch[0])
    refined[...] = first[...]
    planes[...] = planes_in[...]
    for k in range(cascades):
        all_weights[k] = weights[k][...]
    weight_mask = mask[slab].astype(F32)
    weight_mask = jnp.concatenate([weight_mask] * 2, axis=0)

    def keep(n, rows):
        stage[n % stage.shape[0]] = rows.astype(F32)
        for part in range(2):
            plane = stage.at[n % stage.shape[0]][pl.ds(part, height, stride=2), :]
            coil_planes[n, part] = plane.astype(BF16)

    run_start = (lax.axis_index("cuts") * by_cut // cuts) * per
    n = 0
    for ref in senses:
        for s in range(per):
            keep(n, ref[run_start + s])
            n += 1
    for ref in more:
        for q in range(ref.shape[0]):
            for s in range(per):
                keep(n, ref[q, s])
                n += 1
    coils = n // per
    unroll = coils <= 8

    def each_coil(step):
        if unroll:
            for q in range(coils):
                step(q)
        else:
            lax.fori_loop(0, coils, lambda q, _: step(q), None)

    def cascade(c, _):
        def product(q):
            for s in range(per):
                lanes = slice(s * width, (s + 1) * width)
                sr, si = coil_planes[q * per + s, 0].astype(F32), coil_planes[q * per + s, 1].astype(F32)
                ir, ii = planes[0, :, lanes], planes[1, :, lanes]
                coil = jnp.concatenate([sr * ir - si * ii, sr * ii + si * ir], axis=1).astype(BF16)
                w = jnp.dot(coil, forward_z[...], preferred_element_type=F32).astype(BF16)
                rows_y[q * per + s] = jnp.concatenate([w[:, :width], w[:, width:]], axis=0)

        each_coil(product)

        def line(b, _):
            w = jnp.dot(forward_y[...], rows_y[b], preferred_element_type=F32)
            w = (w * weight_mask).astype(BF16)
            w = jnp.dot(back_y[...], w, preferred_element_type=F32).astype(BF16)
            rows_z[b] = jnp.concatenate([w[:height], w[height:]], axis=1)

        lax.fori_loop(0, coils * per, line, None, unroll=4)
        for s in range(per):
            lanes = slice(s * width, (s + 1) * width)
            for part in range(2):
                gradient[part, :, lanes] = sum(d[s, part].astype(F32) for d in datas)

        def gather(q):
            for s in range(per):
                lanes = slice(s * width, (s + 1) * width)
                sr, si = coil_planes[q * per + s, 0].astype(F32), coil_planes[q * per + s, 1].astype(F32)
                w = jnp.dot(rows_z[q * per + s], back_z[...], preferred_element_type=F32)
                br, bi = w[:, :width], w[:, width:]
                gradient[0, :, lanes] -= sr * br + si * bi
                gradient[1, :, lanes] -= sr * bi - si * br

        each_coil(gather)
        now = all_weights.at[step_to(c, "section")]
        step = sum(now[128 + piece : 129 + piece, 0:1].astype(F32) for piece in range(3))
        for part in range(2):
            new = (planes[part] - step * gradient[part] + refined[part]).astype(BF16).astype(F32)
            planes[part] = new
            for s in range(per):
                stage.at[s][pl.ds(part, height, stride=2), :] = new[:, s * width : (s + 1) * width]
        block = 2 * height // cuts
        for s in range(per):
            for cut in range(cuts):
                out[c * cuts + cut, s] = stage[s, cut * block : (cut + 1) * block].astype(BF16)

        @pl.when(c + 1 < cascades)
        def _():
            refine_into(
                [planes[0], planes[1]], all_weights[step_to(c + 1, "section")], scratch, refined, width
            )

    lax.fori_loop(0, cascades, cascade, None)


def refine_scratch(height, per, width, hid):
    rows, lanes = (height + 2) * TILE, per * width
    assert height % (4 * GROUP) == 0
    return [
        pltpu.VMEM((per, rows, width), F32),
        pltpu.VMEM((rows, lanes), BF16),
        pltpu.VMEM((per, rows, width), F32),
        pltpu.VMEM((2, GROUP, 2 * hid, lanes), ACT),
        pltpu.VMEM((2, GROUP, 2 * hid, lanes), BF16),
    ]


def first_refine(pieces, weights):
    per, block, width = pieces[0].shape
    rows = block * len(pieces)
    plane = jax.ShapeDtypeStruct((2, rows // 2, per * width), F32)
    return pl.pallas_call(
        functools.partial(first_refine_kernel, len(pieces), len(weights)),
        out_shape=(plane, plane),
        in_specs=[VMEM] * (len(pieces) + len(weights)),
        out_specs=(VMEM, VMEM),
        scratch_shapes=[pltpu.VMEM((per, rows, width), F32)]
        + refine_scratch(rows // 2, per, width, weights[0].shape[-1]),
        interpret=INTERPRET,
    )(*pieces, *weights)


def run_cascades(planes, first, mask, weights, senses, more, datas, cuts, by_cut):
    per, _, height, width = datas[0].shape
    lanes = per * width
    count = per * (len(senses) + sum(m.shape[0] for m in more))
    tables = [
        dft_table(width, 1.0),
        dft_table(width, -1.0),
        dft_table(height, 1.0).T.copy(),
        dft_table(height, -1.0).T.copy(),
    ]
    args = [planes, first, mask] + [jnp.asarray(t) for t in tables]
    args += list(weights) + list(senses) + list(more) + list(datas)
    return pl.pallas_call(
        functools.partial(
            cascades_kernel, len(weights), len(senses), len(more), len(datas), by_cut
        ),
        out_shape=jax.ShapeDtypeStruct((len(weights) * cuts, per, 2 * height // cuts, width), BF16),
        in_specs=[VMEM] * len(args),
        out_specs=VMEM,
        scratch_shapes=refine_scratch(height, per, width, weights[0].shape[-1])
        + [
            pltpu.VMEM((2, height, lanes), F32),
            pltpu.VMEM((2, height, lanes), F32),
            pltpu.VMEM((2, height, lanes), F32),
            pltpu.VMEM((count, 2, height, width), BF16),
            pltpu.VMEM((count, height, 2 * width), BF16),
            pltpu.VMEM((count, 2 * height, width), BF16),
            pltpu.VMEM((max(per, 4), 2 * height, width), F32),
            pltpu.VMEM((len(weights),) + weights[0].shape, BF16),
        ],
        interpret=INTERPRET,
    )(*args)


def copy_all(copies):
    for copy in copies:
        copy.start()
    for copy in copies:
        copy.wait()


def split_kernel(place, sens, initial, *refs):
    coils, cuts = lax.axis_size("coil"), lax.axis_size("cuts")
    sens_out, initial_out, sems = refs[:coils], refs[coils : coils + cuts], refs[-1]
    slab, block = place.slab(), place.half_block()
    copies = []
    for k, (_, target, _) in enumerate(own_and_peers("coil")):
        source = sens.at[slab, 0, pl.ds(target * place.owned + block * place.run, place.run)]
        copies.append(pltpu.make_async_copy(source, sens_out[k], sems.at[k]))
    for k, (_, target, _) in enumerate(own_and_peers("cuts")):
        start = block * place.run + place.cut_block(target) * place.per
        source = initial.at[slab, pl.ds(start, place.per)]
        copies.append(pltpu.make_async_copy(source, initial_out[k], sems.at[coils + k]))
    copy_all(copies)


def split(place, sens, initial):
    coils, cuts = lax.axis_size("coil"), lax.axis_size("cuts")
    outs = [jax.ShapeDtypeStruct((place.run,) + sens.shape[-2:], BF16)] * coils
    outs += [jax.ShapeDtypeStruct((place.per,) + initial.shape[-2:], BF16)] * cuts
    made = pl.pallas_call(
        functools.partial(split_kernel, place),
        out_shape=outs,
        in_specs=[ANY, ANY],
        out_specs=[ANY] * len(outs),
        scratch_shapes=[pltpu.SemaphoreType.DMA((len(outs),))],
        interpret=INTERPRET,
    )(sens, initial)
    return made[:coils], made[coils:]


def partners_kernel(place, *refs):
    coils, cuts = lax.axis_size("coil"), lax.axis_size("cuts")
    senses, outs, sems = refs[:coils], refs[coils : coils + cuts - 1], refs[-1]
    copies = []
    for k, (_, target, _) in enumerate(own_and_peers("cuts")):
        if k:
            for q in range(coils):
                source = senses[q].at[pl.ds(place.cut_block(target) * place.per, place.per)]
                copies.append(pltpu.make_async_copy(source, outs[k - 1].at[q], sems.at[k - 1, q]))
    copy_all(copies)


def for_partners(place, senses):
    coils, cuts = lax.axis_size("coil"), lax.axis_size("cuts")
    outs = [jax.ShapeDtypeStruct((coils, place.per) + senses[0].shape[-2:], BF16)] * (cuts - 1)
    return pl.pallas_call(
        functools.partial(partners_kernel, place),
        out_shape=outs,
        in_specs=[ANY] * coils,
        out_specs=[ANY] * len(outs),
        scratch_shapes=[pltpu.SemaphoreType.DMA((cuts - 1, coils))],
        interpret=INTERPRET,
    )(*senses)


CHUNKS = 4


def adjoint_kernel(place, kspace, sens, mask, table_x, back_y, back_z, *refs):
    coils, cuts = lax.axis_size("coil"), lax.axis_size("cuts")
    outs = refs[:cuts]
    data, own_sens, by_row, by_slice, stage, sems = refs[cuts:]
    size_x, rows, width = data.shape
    height = rows // 2
    kept = coils * place.run
    slab, block = place.slab(), place.half_block()
    chunk = size_x // CHUNKS
    copies = []
    for i in range(CHUNKS):
        at = pl.ds(i * chunk, chunk)
        copies.append(pltpu.make_async_copy(kspace.at[slab, 0, at], data.at[at], sems.at[i]))
    for q in range(coils):
        source = sens.at[slab, 0, pl.ds(q * place.owned + block * place.run, place.run)]
        target = own_sens.at[pl.ds(q * place.run, place.run)]
        copies.append(pltpu.make_async_copy(source, target, sems.at[CHUNKS + q]))
    for copy in copies:
        copy.start()
    for i in range(CHUNKS):
        copies[i].wait()
        for x in range(i * chunk, (i + 1) * chunk):
            by_row[pl.ds(x, rows, stride=size_x), :] = data[x].astype(F32)
    selected = table_x[block]

    def along_x(y, _):
        operand = by_row[pl.ds(pl.multiple_of(y * 2 * size_x, 2 * size_x), 2 * size_x), :].astype(BF16)
        w = jnp.dot(selected, operand, preferred_element_type=F32)
        by_slice[pl.ds(y, 2 * kept, stride=height), :] = w

    lax.fori_loop(0, height, along_x, None, unroll=8)
    for copy in copies[CHUNKS:]:
        copy.wait()
    weight_mask = mask[slab].astype(F32)
    for k, (_, target, _) in enumerate(own_and_peers("cuts")):

        def one(q, _, k=k, target=target):
            for s in range(place.per):
                n = q * place.run + place.cut_block(target) * place.per + s
                parts = []
                for part in range(2):
                    start = pl.multiple_of((part * kept + n) * height, 16)
                    w = by_slice[pl.ds(start, height), :]
                    parts.append((w.astype(BF16).astype(F32) * weight_mask).astype(BF16))
                w = jnp.concatenate(parts, axis=0)
                w = jnp.dot(back_y[...], w, preferred_element_type=F32).astype(BF16)
                w = jnp.concatenate([w[:height], w[height:]], axis=1)
                w = jnp.dot(w, back_z[...], preferred_element_type=F32)
                br, bi = w[:, :width], w[:, width:]
                stage[s] = own_sens[n].astype(F32)
                sr, si = (stage.at[s][pl.ds(part, height, stride=2), :] for part in range(2))
                outs[k][q, s, 0] = (sr * br + si * bi).astype(BF16)
                outs[k][q, s, 1] = (sr * bi - si * br).astype(BF16)

        lax.fori_loop(0, coils, one, None, unroll=4)


def adjoint(place, kspace, sens, mask):
    coils, cuts = lax.axis_size("coil"), lax.axis_size("cuts")
    size_x, rows, width = kspace.shape[-3:]
    height = rows // 2
    kept = coils * place.run
    table = dft_table(size_x, -1.0).reshape(2, size_x, 2, coils, place.by_half, place.run)
    table = table.transpose(4, 2, 3, 5, 0, 1).reshape(place.by_half, 2 * kept, 2 * size_x)
    tables = [table, dft_table(height, -1.0).T.copy(), dft_table(width, -1.0)]
    return pl.pallas_call(
        functools.partial(adjoint_kernel, place),
        out_shape=[jax.ShapeDtypeStruct((coils, place.per, 2, height, width), BF16)] * cuts,
        in_specs=[ANY, ANY] + [VMEM] * 4,
        out_specs=[VMEM] * cuts,
        scratch_shapes=[
            pltpu.VMEM((size_x, rows, width), BF16),
            pltpu.VMEM((kept, rows, width), BF16),
            pltpu.VMEM((rows * size_x, width), F32),
            pltpu.VMEM((2 * kept * height, width), F32),
            pltpu.VMEM((place.per, rows, width), F32),
            pltpu.SemaphoreType.DMA((CHUNKS + coils,)),
        ],
        interpret=INTERPRET,
    )(kspace, sens, mask, *[jnp.asarray(t) for t in tables])


def pair_sum_kernel(n_in, *refs):
    terms, outs = refs[:n_in], refs[n_in:]
    for k, (_, target, _) in enumerate(own_and_peers("coil")):
        outs[k][...] = sum(t[target].astype(F32) for t in terms).astype(BF16)


def pair_sum(terms):
    coils = lax.axis_size("coil")
    return pl.pallas_call(
        functools.partial(pair_sum_kernel, len(terms)),
        out_shape=[jax.ShapeDtypeStruct(terms[0].shape[1:], BF16)] * coils,
        in_specs=[VMEM] * len(terms),
        out_specs=[VMEM] * coils,
        interpret=INTERPRET,
    )(*terms)


class Place:
    def __init__(self, slabs, size_x):
        sections, coils, cuts = (lax.axis_size(a) for a in ("section", "coil", "cuts"))
        self.slabs, self.cuts, self.halves = slabs, cuts, sections // slabs
        self.owned = size_x // coils
        self.by_half = math.gcd(self.owned, self.halves)
        self.by_cut = math.gcd(self.owned // self.by_half, cuts)
        self.per = self.owned // (self.by_half * self.by_cut)
        self.run = self.by_cut * self.per

    def slab(self):
        return lax.axis_index("section") // self.halves

    def half_block(self):
        return lax.axis_index("section") % self.halves * self.by_half // self.halves

    def cut_block(self, cut):
        return cut * self.by_cut // self.cuts


def sent(pieces, axis):
    arrived = [pieces[0]]
    for k, (route, _, _) in enumerate(peers(axis)):
        arrived.append(lax.ppermute(pieces[k + 1], axis, route))
    return arrived


def body(initial, sens, kspace, mask, step_sizes, conv_in, bias_in, conv_out):
    slabs, _, size_x, size_y, _, size_z = sens.shape
    sections, cuts = lax.axis_size("section"), lax.axis_size("cuts")
    place = Place(slabs, size_x)
    rows = size_y // cuts

    def joined(array):
        return array.reshape(array.shape[:-3] + (array.shape[-3] * 2, size_z))

    initial, sens, kspace = joined(initial), joined(sens), joined(kspace)
    sens_pieces, image_pieces = split(place, sens, initial)
    senses = sent(sens_pieces, "coil")

    terms = adjoint(place, kspace, sens, mask)
    terms = [terms[0]] + [
        lax.ppermute(terms[k + 1], "cuts", route) for k, (route, _, _) in enumerate(peers("cuts"))
    ]
    datas = sent(pair_sum(terms), "coil")

    packed = pack_weights(conv_in[0], bias_in, conv_out[0], step_sizes)
    weights = sent([packed] * sections, "section")
    first, planes = first_refine(sent(image_pieces, "cuts"), weights)

    more = [
        lax.ppermute(piece, "cuts", route)
        for piece, (route, _, _) in zip(for_partners(place, senses), peers("cuts"))
    ]
    out = run_cascades(planes, first, mask, weights, senses, more, datas, cuts, place.by_cut)
    out = lax.all_to_all(out, ("section", "cuts"), 0, 0, tiled=True)
    out = out.reshape(slabs, place.halves, cuts, place.per, rows, 2, size_z)
    out = out[:, :: place.halves // place.by_half, :: cuts // place.by_cut]
    return out.reshape(1, slabs, place.owned, rows, 2, size_z)


def solution(mesh):
    return jax.shard_map(
        body,
        mesh=mesh,
        in_specs=(
            P(None, "coil", "cuts", None, None),
            P(None, ("coil", "cuts"), None, None, None, None),
            P(None, ("coil", "cuts"), None, None, None, None),
            P(),
            P("section"),
            P("section", None, None),
            P("section", None),
            P("section", None, None),
        ),
        out_specs=P("section", None, "coil", "cuts", None, None),
        check_vma=False,
    )
```

time: 113 us -> 114 us (level)
  Pallas kernels: 41 us -> 76.4 us
  other arithmetic: 10.7 us -> 0 us
  local copies, waits for them, and re-layouts: 13.1 us -> 3.53 us
  matrix products: 5.86 us -> 0 us
  between operations: 4.68 us -> 0.79 us
  waiting for transfers between devices: 11 us -> 7.44 us
    pallas_call x2 -> x7, Pallas kernels: 41 us -> 76.4 us  [the longest x1 23.8 us: run_cascades(): pl.pallas_call(functools.partial(cascades_kernel, len(weights), len(sense...]
    dot_general x4 -> x0, matrix products: 5.86 us -> none  [the longest x1 2.58 us: pass_z(): jnp.einsum('...cyz,czdw->...dyw', v, split, preferred_element_type=jnp.fl...]
    another operation x4 -> x0, other arithmetic: 4.12 us -> none  [the longest x1 1.94 us: conj_product(): return jnp.stack([ar * br + ai * bi, ar * bi - ai * br], axis=-3)]
    ppermute x12, waiting for transfers between devices: 11 us -> 7.44 us  [the longest x10 7.43 us: sent(): arrived.append(lax.ppermute(pieces[k + 1], axis, route))]
    dynamic_slice x4 -> x0, local copies, waits for them, and re-layouts: 2.94 us -> none  [the longest x2 1.26 us: half_slices(): part = lax.dynamic_index_in_dim(split, half_block, dim + 1, keepdims=False)]
    another operation x3 -> x0, local copies, waits for them, and re-layouts: 2.61 us -> none  [the longest x1 0.98 us: body(): return out.reshape(1, slabs, owned, rows, 2, size_z)]
    sub x1 -> x0, other arithmetic: 2.18 us -> none  [conj_product(): return jnp.stack([ar * br + ai * bi, ar * bi - ai * br], axis=-3)]
    squeeze x1 -> x0, local copies, waits for them, and re-layouts: 1.99 us -> none  [body(): data_one = lax.dynamic_index_in_dim(kspace, slab, 0, keepdims=False)[0]]
  transfers between devices with their start and end apart: 12 -> 12, of which waited for: 1 -> 3; matrix products, arithmetic and copies ran while one was open for 20% -> 0% of each run, Pallas kernels for 7% -> 26%
where the time goes in v1:
time: 114 us
  Pallas kernels  76.4 us (67%)
  starting transfers between devices  14.5 us (13%)
  blocking collectives  10.9 us (10%)
  waiting for transfers between devices  7.44 us (7%)
  local copies, waits for them, and re-layouts  3.53 us (3%)
    pallas_call x1, Pallas kernels, run_cascades(): pl.pallas_call(functools.partial(cascades_kernel, len(weights), len(sense...  23.8 us
    pallas_call x1, Pallas kernels, split(): pl.pallas_call(functools.partial(split_kernel, place), out_shape=outs, in...  23.5 us
    ppermute x10, starting transfers between devices, sent(): arrived.append(lax.ppermute(pieces[k + 1], axis, route))  14.4 us
    pallas_call x1, Pallas kernels, for_partners(): pl.pallas_call(functools.partial(partners_kernel, place), out_shape=outs,...  11.1 us
    all_to_all x1, blocking collectives, body(): out = lax.all_to_all(out, ('section', 'cuts'), 0, 0, tiled=True)  10.9 us
    pallas_call x1, Pallas kernels, adjoint(): pl.pallas_call(functools.partial(adjoint_kernel, place), out_shape=[jax.S...  9.91 us
    ppermute x10, waiting for transfers between devices, sent(): arrived.append(lax.ppermute(pieces[k + 1], axis, route))  7.43 us
    pallas_call x1, Pallas kernels, first_refine(): pl.pallas_call(functools.partial(first_refine_kernel, len(pieces), len(we...  4.76 us
  transfers between devices with their start and end apart: 12, of which 3 were waited for; matrix products, arithmetic and copies ran while one was open for 0% of the time, Pallas kernels for 26%

profile of v1, /device:TPU:0, one launch (start us, length us, event | category | flops | bytes accessed | tf_op | source)
XLA Modules:
  0.0 113.7 jit_solution(13092530001771658873)
XLA Ops:
  0.0 23.5 %shard_map.154 = (bf16[4,160,128]{2,1,0:T(8,128)(2,1)}, bf16[4,160,128]{2,1,0:T(8,128)(2,1)}, bf16[4,160,128]{2,1,0:T(8,128)(2,1)}, bf16[4,160,128]{2,1,0:T(8,12...) custom-call(bf16[2,1,32,160,128]{4,3,2,1,0:T(8,128)(2,1)} %bitcast.8, bf16[2,8,80,128]{3,2,1,0:T(8,128)(2,1)} %bitcast.12), custom_call_target="tpu_custom_call" | custom-call | tf_op jit(solution)/shard_map/pallas_call | solution.py:405
  23.5 3.1 %collective-permute-start.4 = (bf16[4,160,128]{2,1,0:T(8,128)(2,1)}, bf16[4,160,128]{2,1,0:T(8,128)(2,1)S(1)}, u32[]{:S(2)}, u32[]{:S(2)}) collective-permute-start(bf16[4,160,128]{2,1,0:T(8,128)(2,1)} %get-tuple-element.24), channel_id=1, source_target_pairs={{0,2},{2,0},{4,6},{6,4},{1,3},{3,1},{5,7},{7,5},{8,10},{10,8},{12,... | collective-permute-start | bytes 491528 | tf_op jit(solution)/shard_map/ppermute | solution.py:566
  26.6 2.6 %collective-permute-start.5 = (bf16[4,160,128]{2,1,0:T(8,128)(2,1)}, bf16[4,160,128]{2,1,0:T(8,128)(2,1)S(1)}, u32[]{:S(2)}, u32[]{:S(2)}) collective-permute-start(bf16[4,160,128]{2,1,0:T(8,128)(2,1)} %get-tuple-element.25), channel_id=1, source_target_pairs={{0,4},{2,6},{4,0},{6,2},{1,5},{3,7},{5,1},{7,3},{8,12},{10,14},{12... | collective-permute-start | bytes 491528 | tf_op jit(solution)/shard_map/ppermute | solution.py:566
  29.2 0.0 collective-permute-start.6
  29.2 9.9 %shard_map.158 = (bf16[4,2,2,80,128]{4,3,2,1,0:T(8,128)(2,1)}, bf16[4,2,2,80,128]{4,3,2,1,0:T(8,128)(2,1)}) custom-call(bf16[2,1,32,160,128]{4,3,2,1,0:T(8,128)(2,1)} %bitcast.10, bf16[2,1,32,160,128]{4,3,2,1,0:T(8,128)(2,1)} %bitcast.9, s32[2,80,128]{2,1,0:T(8,128)} %refs_2_.1, bf16[2,32,64]{2,1,0:T(8,128)(2,1)} %constant.12.clone.table_x, ...), custom_call_target="tpu_custom_call" | custom-call | tf_op jit(solution)/shard_map/pallas_call | solution.py:509
  39.1 0.1 collective-permute-start.8
  39.2 0.0 collective-permute-done.4.refs_1_.refs_12_
  39.2 0.0 copy-start
  39.2 2.6 %collective-permute-done.5.refs_2_.refs_13_ = bf16[4,160,128]{2,1,0:T(8,128)(2,1)S(1)} collective-permute-done((bf16[4,160,128]{2,1,0:T(8,128)(2,1)}, bf16[4,160,128]{2,1,0:T(8,128)(2,1)S(1)}, u32[]{:S(2)}, u32[]{:S(2)}) %collective-permute-start.5) | collective-permute-done | bytes 163872 | tf_op jit(solution)/shard_map/ppermute | solution.py:566
  41.8 0.0 collective-permute-done.6.refs_3_.refs_14_
  41.8 0.0 copy-done
  41.8 0.7 copy-done.1
  42.5 0.1 copy-done.2
  42.6 11.1 %shard_map.157 = bf16[4,2,160,128]{3,2,1,0:T(8,128)(2,1)} custom-call(bf16[4,160,128]{2,1,0:T(8,128)(2,1)} %get-tuple-element.23.refs_0_.refs_11_, bf16[4,160,128]{2,1,0:T(8,128)(2,1)} %copy-done, bf16[4,160,128]{2,1,0:T(8,128)(2,1)} %copy-done.1, bf16[4,160,128]{2,1,0:T(8,128)(2,1)} %copy-done.2), custom_call_target="tpu_custom_call" | custom-call | tf_op jit(solution)/shard_map/pallas_call | solution.py:431
  53.6 0.1 collective-permute-start.7
  54.3 1.6 %shard_map.155.refs_2_.refs_7_ = bf16[136,128]{1,0:T(8,128)(2,1)} custom-call(bf16[136,42]{1,0:T(8,128)(2,1)} %constant.15.clone.chosen, bf16[18,128]{1,0:T(8,128)(2,1)} %bitcast.13, f32[1,128]{1,0:T(1,128)} %bias.1, bf16[18,128]{1,0:T(8,128)(2,1)} %bitcast.14, f32[1]{0:T(128)S(6)} %copy.18.step), custom_call_target="tpu_custom_call" | custom-call | tf_op jit(solution)/shard_map/pallas_call | solution.py:97
  56.0 2.4 %collective-permute-start.3 = (bf16[136,128]{1,0:T(8,128)(2,1)}, bf16[136,128]{1,0:T(8,128)(2,1)S(1)}, u32[]{:S(2)}, u32[]{:S(2)}) collective-permute-start(bf16[136,128]{1,0:T(8,128)(2,1)} %shard_map.155.refs_2_.refs_7_), channel_id=1, source_target_pairs={{0,24},{8,16},{16,8},{24,0},{1,25},{9,17},{17,9},{25,1},{2,26},{10... | collective-permute-start | bytes 104456 | tf_op jit(solution)/shard_map/ppermute | solution.py:566
  58.4 0.5 collective-permute-start.2
  58.9 0.0 collective-permute-done.8.refs_1_
  58.9 0.7 copy-done.4
  59.7 1.8 %shard_map.159 = (bf16[2,2,80,128]{3,2,1,0:T(8,128)(2,1)}, bf16[2,2,80,128]{3,2,1,0:T(8,128)(2,1)}, bf16[2,2,80,128]{3,2,1,0:T(8,128)(2,1)}, bf16[2,2,80,128]{3,2,1,0:T(8,128)(2,1)}) custom-call(bf16[4,2,2,80,128]{4,3,2,1,0:T(8,128)(2,1)} %get-tuple-element.27.refs_0_, bf16[4,2,2,80,128]{4,3,2,1,0:T(8,128)(2,1)} %copy-done.4), custom_call_target="tpu_custom_call" | custom-call | tf_op jit(solution)/shard_map/pallas_call | solution.py:534
  61.5 2.6 %collective-permute-start.9 = (bf16[2,2,80,128]{3,2,1,0:T(8,128)(2,1)}, bf16[2,2,80,128]{3,2,1,0:T(8,128)(2,1)S(1)}, u32[]{:S(2)}, u32[]{:S(2)}) collective-permute-start(bf16[2,2,80,128]{3,2,1,0:T(8,128)(2,1)} %get-tuple-element.30), channel_id=1, source_target_pairs={{0,2},{2,0},{4,6},{6,4},{1,3},{3,1},{5,7},{7,5},{8,10},{10,8},{12,... | collective-permute-start | bytes 245768 | tf_op jit(solution)/shard_map/ppermute | solution.py:566
  64.1 1.0 collective-permute-start.10
  65.1 0.0 collective-permute-done.3.refs_5_.refs_10_
  65.1 1.5 %collective-permute-start.11 = (bf16[2,2,80,128]{3,2,1,0:T(8,128)(2,1)}, bf16[2,2,80,128]{3,2,1,0:T(8,128)(2,1)S(1)}, u32[]{:S(2)}, u32[]{:S(2)}) collective-permute-start(bf16[2,2,80,128]{3,2,1,0:T(8,128)(2,1)} %get-tuple-element.32), channel_id=1, source_target_pairs={{0,6},{2,4},{4,2},{6,0},{1,7},{3,5},{5,3},{7,1},{8,14},{10,12},{12... | collective-permute-start | bytes 245768 | tf_op jit(solution)/shard_map/ppermute | solution.py:566
  66.7 0.0 collective-permute-done.2.refs_4_.refs_9_
  66.7 0.5 collective-permute-start.1
  67.2 3.6 %collective-permute-done.1.refs_3_.refs_8_ = bf16[136,128]{1,0:T(8,128)(2,1)S(1)} collective-permute-done((bf16[136,128]{1,0:T(8,128)(2,1)}, bf16[136,128]{1,0:T(8,128)(2,1)S(1)}, u32[]{:S(2)}, u32[]{:S(2)}) %collective-permute-start.1) | collective-permute-done | bytes 34848 | tf_op jit(solution)/shard_map/ppermute | solution.py:566
  70.8 0.0 copy-done.12
  70.8 0.0 collective-permute-start
  70.8 1.2 %collective-permute-done.refs_1_ = bf16[2,80,128]{2,1,0:T(8,128)(2,1)S(1)} collective-permute-done((bf16[2,80,128]{2,1,0:T(8,128)(2,1)S(1)}, bf16[2,80,128]{2,1,0:T(8,128)(2,1)S(1)}, u32[]{:S(2)}, u32[]{:S(2)}) %collective-permute-start) | collective-permute-done | bytes 40992 | tf_op jit(solution)/shard_map/ppermute | solution.py:566
  72.1 0.0 copy-done.5
  72.1 0.0 copy-done.6
  72.1 0.6 copy-done.11
  72.7 4.8 %shard_map.156 = (f32[2,80,256]{2,1,0:T(8,128)}, f32[2,80,256]{2,1,0:T(8,128)}) custom-call(bf16[2,80,128]{2,1,0:T(8,128)(2,1)} %get-tuple-element.19.refs_0_, bf16[2,80,128]{2,1,0:T(8,128)(2,1)} %copy-done.11, bf16[136,128]{1,0:T(8,128)(2,1)} %shard_map.155.refs_2_.refs_7_, bf16[136,128]{1,0:T(8,128)(2,1)} %copy-done.7, bf16[136,128]{1,0:T(8,128)(2,1)} %copy-done.6, ...), custom_call_target="tpu_custom_call" | custom-call | tf_op jit(solution)/shard_map/pallas_call | solution.py:334
  77.4 0.0 collective-permute-done.9.refs_17_
  77.4 0.0 collective-permute-done.10.refs_18_
  77.4 0.0 copy-start.9
  77.5 0.0 collective-permute-done.11.refs_19_
  77.5 0.0 collective-permute-done.7.refs_15_
  77.5 0.0 copy-start.3
  77.5 0.6 copy-done.8
  78.1 0.0 copy-done.9
  78.1 0.0 copy-done.10
  78.1 0.1 copy-done.3
  78.2 23.8 %shard_map.160 = bf16[8,2,80,128]{3,2,1,0:T(8,128)(2,1)} custom-call(f32[2,80,256]{2,1,0:T(8,128)} %get-tuple-element.21.refs_0_, f32[2,80,256]{2,1,0:T(8,128)} %get-tuple-element.22.refs_1_, s32[2,80,128]{2,1,0:T(8,128)} %refs_2_.1, bf16[256,256]{1,0:T(8,128)(2,1)} %constant.16.clone.refs_3_, bf16[256,256]{1,0:T(8,128)(2,1)} %constant.14.clone.back_z.refs_4_, ...), custom_call_target="tpu_custom_call" | custom-call | tf_op jit(solution)/shard_map/pallas_call | solution.py:357
  102.0 10.9 %all_to_all.5 = bf16[8,2,80,128]{3,2,1,0:T(8,128)(2,1)S(1)} all-to-all(bf16[8,2,80,128]{3,2,1,0:T(8,128)(2,1)} %shard_map.160), channel_id=1, replica_groups=mesh['section'=4,'coil'=4,'cuts'=2] {'section','cuts'}, dimensions={0} | all-to-all | bytes 655360 | tf_op jit(solution)/shard_map/all_to_all | solution.py:598
  113.0 0.7 copy.19
  (11 shorter events, 0.0 us)
Async XLA Ops:
  23.5 15.7 %collective-permute-start.4 = (bf16[4,160,128]{2,1,0:T(8,128)(2,1)}, bf16[4,160,128]{2,1,0:T(8,128)(2,1)S(1)}, u32[]{:S(2)}, u32[]{:S(2)}) collective-permute-start(bf16[4,160,128]{2,1,0:T(8,128)(2,1)} %get-tuple-element.24), channel_id=1, source_target_pairs={{0,2},{2,0},{4,6},{6,4},{1,3},{3,1},{5,7},{7,5},{8,10},{10,8},{12,... | collective-permute-start | bytes 491528 | tf_op jit(solution)/shard_map/ppermute | solution.py:566
  26.6 15.2 %collective-permute-start.5 = (bf16[4,160,128]{2,1,0:T(8,128)(2,1)}, bf16[4,160,128]{2,1,0:T(8,128)(2,1)S(1)}, u32[]{:S(2)}, u32[]{:S(2)}) collective-permute-start(bf16[4,160,128]{2,1,0:T(8,128)(2,1)} %get-tuple-element.25), channel_id=1, source_target_pairs={{0,4},{2,6},{4,0},{6,2},{1,5},{3,7},{5,1},{7,3},{8,12},{10,14},{12... | collective-permute-start | bytes 491528 | tf_op jit(solution)/shard_map/ppermute | solution.py:566
  29.2 12.6 %collective-permute-start.6 = (bf16[4,160,128]{2,1,0:T(8,128)(2,1)}, bf16[4,160,128]{2,1,0:T(8,128)(2,1)S(1)}, u32[]{:S(2)}, u32[]{:S(2)}) collective-permute-start(bf16[4,160,128]{2,1,0:T(8,128)(2,1)} %get-tuple-element.26), channel_id=1, source_target_pairs={{0,6},{2,4},{4,2},{6,0},{1,7},{3,5},{5,3},{7,1},{8,14},{10,12},{12... | collective-permute-start | bytes 491528 | tf_op jit(solution)/shard_map/ppermute | solution.py:566
  29.2 41.6 %copy-start.12 = (bf16[2,80,128]{2,1,0:T(8,128)(2,1)S(1)}, bf16[2,80,128]{2,1,0:T(8,128)(2,1)}, u32[]{:S(2)}) copy-start(bf16[2,80,128]{2,1,0:T(8,128)(2,1)} %get-tuple-element.20) | copy-start | bytes 122884
  39.1 19.8 %collective-permute-start.8 = (bf16[4,2,2,80,128]{4,3,2,1,0:T(8,128)(2,1)}, bf16[4,2,2,80,128]{4,3,2,1,0:T(8,128)(2,1)S(1)}, u32[]{:S(2)}, u32[]{:S(2)}) collective-permute-start(bf16[4,2,2,80,128]{4,3,2,1,0:T(8,128)(2,1)} %get-tuple-element.28), channel_id=1, source_target_pairs={{0,1},{1,0},{2,3},{3,2},{4,5},{5,4},{6,7},{7,6},{8,9},{9,8},{10,11... | collective-permute-start | bytes 983048 | tf_op jit(solution)/shard_map/ppermute | solution.py:585
  39.2 2.6 %copy-start = (bf16[4,160,128]{2,1,0:T(8,128)(2,1)}, bf16[4,160,128]{2,1,0:T(8,128)(2,1)S(1)}, u32[]{:S(2)}) copy-start(bf16[4,160,128]{2,1,0:T(8,128)(2,1)S(1)} %collective-permute-done.4.refs_1_.refs_12_) | copy-start | bytes 491524
  41.8 0.7 copy-start.1
  41.8 0.7 copy-start.2
  53.6 23.9 %collective-permute-start.7 = (bf16[4,2,160,128]{3,2,1,0:T(8,128)(2,1)}, bf16[4,2,160,128]{3,2,1,0:T(8,128)(2,1)S(1)}, u32[]{:S(2)}, u32[]{:S(2)}) collective-permute-start(bf16[4,2,160,128]{3,2,1,0:T(8,128)(2,1)} %shard_map.157), channel_id=1, source_target_pairs={{0,1},{1,0},{2,3},{3,2},{4,5},{5,4},{6,7},{7,6},{8,9},{9,8},{10,11... | collective-permute-start | bytes 983048 | tf_op jit(solution)/shard_map/ppermute | solution.py:594
  56.0 9.2 %collective-permute-start.3 = (bf16[136,128]{1,0:T(8,128)(2,1)}, bf16[136,128]{1,0:T(8,128)(2,1)S(1)}, u32[]{:S(2)}, u32[]{:S(2)}) collective-permute-start(bf16[136,128]{1,0:T(8,128)(2,1)} %shard_map.155.refs_2_.refs_7_), channel_id=1, source_target_pairs={{0,24},{8,16},{16,8},{24,0},{1,25},{9,17},{17,9},{25,1},{2,26},{10... | collective-permute-start | bytes 104456 | tf_op jit(solution)/shard_map/ppermute | solution.py:566
  58.4 8.3 %collective-permute-start.2 = (bf16[136,128]{1,0:T(8,128)(2,1)}, bf16[136,128]{1,0:T(8,128)(2,1)S(1)}, u32[]{:S(2)}, u32[]{:S(2)}) collective-permute-start(bf16[136,128]{1,0:T(8,128)(2,1)} %shard_map.155.refs_2_.refs_7_), channel_id=1, source_target_pairs={{0,16},{8,24},{16,0},{24,8},{1,17},{9,25},{17,1},{25,9},{2,18},{10... | collective-permute-start | bytes 104456 | tf_op jit(solution)/shard_map/ppermute | solution.py:566
  58.9 0.7 copy-start.4
  61.5 15.9 %collective-permute-start.9 = (bf16[2,2,80,128]{3,2,1,0:T(8,128)(2,1)}, bf16[2,2,80,128]{3,2,1,0:T(8,128)(2,1)S(1)}, u32[]{:S(2)}, u32[]{:S(2)}) collective-permute-start(bf16[2,2,80,128]{3,2,1,0:T(8,128)(2,1)} %get-tuple-element.30), channel_id=1, source_target_pairs={{0,2},{2,0},{4,6},{6,4},{1,3},{3,1},{5,7},{7,5},{8,10},{10,8},{12,... | collective-permute-start | bytes 245768 | tf_op jit(solution)/shard_map/ppermute | solution.py:566
  64.1 13.3 %collective-permute-start.10 = (bf16[2,2,80,128]{3,2,1,0:T(8,128)(2,1)}, bf16[2,2,80,128]{3,2,1,0:T(8,128)(2,1)S(1)}, u32[]{:S(2)}, u32[]{:S(2)}) collective-permute-start(bf16[2,2,80,128]{3,2,1,0:T(8,128)(2,1)} %get-tuple-element.31), channel_id=1, source_target_pairs={{0,4},{2,6},{4,0},{6,2},{1,5},{3,7},{5,1},{7,3},{8,12},{10,14},{12... | collective-permute-start | bytes 245768 | tf_op jit(solution)/shard_map/ppermute | solution.py:566
  65.1 6.9 %copy-start.5 = (bf16[136,128]{1,0:T(8,128)(2,1)}, bf16[136,128]{1,0:T(8,128)(2,1)S(1)}, u32[]{:S(2)}) copy-start(bf16[136,128]{1,0:T(8,128)(2,1)S(1)} %collective-permute-done.3.refs_5_.refs_10_) | copy-start | bytes 104452
  65.1 12.3 %collective-permute-start.11 = (bf16[2,2,80,128]{3,2,1,0:T(8,128)(2,1)}, bf16[2,2,80,128]{3,2,1,0:T(8,128)(2,1)S(1)}, u32[]{:S(2)}, u32[]{:S(2)}) collective-permute-start(bf16[2,2,80,128]{3,2,1,0:T(8,128)(2,1)} %get-tuple-element.32), channel_id=1, source_target_pairs={{0,6},{2,4},{4,2},{6,0},{1,7},{3,5},{5,3},{7,1},{8,14},{10,12},{12... | collective-permute-start | bytes 245768 | tf_op jit(solution)/shard_map/ppermute | solution.py:566
  66.7 5.4 %copy-start.6 = (bf16[136,128]{1,0:T(8,128)(2,1)}, bf16[136,128]{1,0:T(8,128)(2,1)S(1)}, u32[]{:S(2)}) copy-start(bf16[136,128]{1,0:T(8,128)(2,1)S(1)} %collective-permute-done.2.refs_4_.refs_9_) | copy-start | bytes 104452
  66.7 4.1 %collective-permute-start.1 = (bf16[136,128]{1,0:T(8,128)(2,1)}, bf16[136,128]{1,0:T(8,128)(2,1)S(1)}, u32[]{:S(2)}, u32[]{:S(2)}) collective-permute-start(bf16[136,128]{1,0:T(8,128)(2,1)} %shard_map.155.refs_2_.refs_7_), channel_id=1, source_target_pairs={{0,8},{8,0},{16,24},{24,16},{1,9},{9,1},{17,25},{25,17},{2,10},{10... | collective-permute-start | bytes 104456 | tf_op jit(solution)/shard_map/ppermute | solution.py:566
  70.8 1.2 %copy-start.7 = (bf16[136,128]{1,0:T(8,128)(2,1)}, bf16[136,128]{1,0:T(8,128)(2,1)S(1)}, u32[]{:S(2)}) copy-start(bf16[136,128]{1,0:T(8,128)(2,1)S(1)} %collective-permute-done.1.refs_3_.refs_8_) | copy-start | bytes 104452
  70.8 1.2 %collective-permute-start = (bf16[2,80,128]{2,1,0:T(8,128)(2,1)S(1)}, bf16[2,80,128]{2,1,0:T(8,128)(2,1)S(1)}, u32[]{:S(2)}, u32[]{:S(2)}) collective-permute-start(bf16[2,80,128]{2,1,0:T(8,128)(2,1)S(1)} %copy-done.12), channel_id=1, source_target_pairs={{0,1},{1,0},{2,3},{3,2},{4,5},{5,4},{6,7},{7,6},{8,9},{9,8},{10,11... | collective-permute-start | bytes 122888 | tf_op jit(solution)/shard_map/ppermute | solution.py:566
  72.1 0.6 copy-start.11
  77.4 0.6 copy-start.8
  77.4 0.7 copy-start.9
  77.5 0.7 copy-start.10
  77.5 0.7 copy-start.3

commit v2 on v1

--- a/solution.py
+++ b/solution.py
@@ -9,6 +9,7 @@
 from jax.experimental import pallas as pl
 from jax.experimental.pallas import tpu as pltpu
 from jax.sharding import PartitionSpec as P
+
 
 INTERPRET = False
 BF16, F32 = jnp.bfloat16, jnp.float32
@@ -53,6 +54,18 @@
 SMEM = pl.BlockSpec(memory_space=pltpu.SMEM)
 VMEM = pl.BlockSpec(memory_space=pltpu.VMEM)
 ANY = pl.BlockSpec(memory_space=pl.ANY)
+
+
+def far():
+    return INTERPRET or lax.axis_size("coil") > 8
+
+
+def near(x):
+    return x if far() else pltpu.with_memory_space_constraint(x, pltpu.VMEM)
+
+
+def near_out(shape, dtype):
+    return jax.ShapeDtypeStruct(shape, dtype) if far() else pltpu.VMEM(shape, dtype)
 
 
 def selections():
@@ -79,7 +92,7 @@
     return [high, mid, (rest - mid.astype(F32)).astype(BF16)]
 
 
-def pack_kernel(chosen, conv_in, bias, conv_out, step, packed):
+def pack_into(packed, chosen, conv_in, bias, conv_out, step):
     def picked(rows, lanes):
         return jnp.dot(chosen[:, lanes], rows, preferred_element_type=F32)
 
@@ -90,17 +103,6 @@
             column = chosen[:, at + piece : at + piece + 1].astype(F32)
             total += column * row.astype(F32)
     packed[...] = total.astype(BF16)
-
-
-def pack_weights(conv_in, bias, conv_out, step):
-    chosen = jnp.asarray(selections())
-    return pl.pallas_call(
-        pack_kernel,
-        out_shape=jax.ShapeDtypeStruct((chosen.shape[0], bias.shape[1]), BF16),
-        in_specs=[VMEM, VMEM, VMEM, VMEM, SMEM],
-        out_specs=VMEM,
-        interpret=INTERPRET,
-    )(chosen, conv_in.T, bias, conv_out, step)
 
 
 def shifted(plane, by, width):
@@ -330,7 +332,7 @@
 def first_refine(pieces, weights):
     per, block, width = pieces[0].shape
     rows = block * len(pieces)
-    plane = jax.ShapeDtypeStruct((2, rows // 2, per * width), F32)
+    plane = near_out((2, rows // 2, per * width), F32)
     return pl.pallas_call(
         functools.partial(first_refine_kernel, len(pieces), len(weights)),
         out_shape=(plane, plane),
@@ -339,7 +341,7 @@
         scratch_shapes=[pltpu.VMEM((per, rows, width), F32)]
         + refine_scratch(rows // 2, per, width, weights[0].shape[-1]),
         interpret=INTERPRET,
-    )(*pieces, *weights)
+    )(*[near(x) for x in [*pieces, *weights]])
 
 
 def run_cascades(planes, first, mask, weights, senses, more, datas, cuts, by_cut):
@@ -373,19 +375,12 @@
             pltpu.VMEM((len(weights),) + weights[0].shape, BF16),
         ],
         interpret=INTERPRET,
-    )(*args)
-
-
-def copy_all(copies):
-    for copy in copies:
-        copy.start()
-    for copy in copies:
-        copy.wait()
-
-
-def split_kernel(place, sens, initial, *refs):
+    )(*[near(x) for x in args])
+
+
+def split_kernel(place, sens, initial, chosen, conv_in, bias, conv_out, step, *refs):
     coils, cuts = lax.axis_size("coil"), lax.axis_size("cuts")
-    sens_out, initial_out, sems = refs[:coils], refs[coils : coils + cuts], refs[-1]
+    sens_out, initial_out, packed, sems = refs[:coils], refs[coils : coils + cuts], refs[-2], refs[-1]
     slab, block = place.slab(), place.half_block()
     copies = []
     for k, (_, target, _) in enumerate(own_and_peers("coil")):
@@ -395,107 +390,109 @@
         start = block * place.run + place.cut_block(target) * place.per
         source = initial.at[slab, pl.ds(start, place.per)]
         copies.append(pltpu.make_async_copy(source, initial_out[k], sems.at[coils + k]))
-    copy_all(copies)
-
-
-def split(place, sens, initial):
+    for copy in copies:
+        copy.start()
+    pack_into(packed, chosen, conv_in, bias, conv_out, step)
+    for copy in copies:
+        copy.wait()
+
+
+def split(place, sens, initial, conv_in, bias, conv_out, step):
     coils, cuts = lax.axis_size("coil"), lax.axis_size("cuts")
-    outs = [jax.ShapeDtypeStruct((place.run,) + sens.shape[-2:], BF16)] * coils
-    outs += [jax.ShapeDtypeStruct((place.per,) + initial.shape[-2:], BF16)] * cuts
+    chosen = jnp.asarray(selections())
+    outs = [near_out((place.run,) + sens.shape[-2:], BF16)] * coils
+    outs += [near_out((place.per,) + initial.shape[-2:], BF16)] * cuts
+    outs += [near_out((chosen.shape[0], bias.shape[1]), BF16)]
     made = pl.pallas_call(
         functools.partial(split_kernel, place),
         out_shape=outs,
-        in_specs=[ANY, ANY],
-        out_specs=[ANY] * len(outs),
-        scratch_shapes=[pltpu.SemaphoreType.DMA((len(outs),))],
+        in_specs=[ANY, ANY, VMEM, VMEM, VMEM, VMEM, SMEM],
+        out_specs=[VMEM] * len(outs),
+        scratch_shapes=[pltpu.SemaphoreType.DMA((coils + cuts,))],
         interpret=INTERPRET,
-    )(sens, initial)
-    return made[:coils], made[coils:]
+    )(sens, initial, chosen, conv_in.T, bias, conv_out, step)
+    return made[:coils], made[coils:-1], made[-1]
 
 
 def partners_kernel(place, *refs):
-    coils, cuts = lax.axis_size("coil"), lax.axis_size("cuts")
-    senses, outs, sems = refs[:coils], refs[coils : coils + cuts - 1], refs[-1]
-    copies = []
-    for k, (_, target, _) in enumerate(own_and_peers("cuts")):
-        if k:
-            for q in range(coils):
-                source = senses[q].at[pl.ds(place.cut_block(target) * place.per, place.per)]
-                copies.append(pltpu.make_async_copy(source, outs[k - 1].at[q], sems.at[k - 1, q]))
-    copy_all(copies)
+    coils = lax.axis_size("coil")
+    senses, outs = refs[:coils], refs[coils:]
+    for k, (_, target, _) in enumerate(peers("cuts")):
+        for q in range(coils):
+            outs[k][q] = senses[q][pl.ds(place.cut_block(target) * place.per, place.per)]
 
 
 def for_partners(place, senses):
     coils, cuts = lax.axis_size("coil"), lax.axis_size("cuts")
-    outs = [jax.ShapeDtypeStruct((coils, place.per) + senses[0].shape[-2:], BF16)] * (cuts - 1)
+    outs = [near_out((coils, place.per) + senses[0].shape[-2:], BF16)] * (cuts - 1)
     return pl.pallas_call(
         functools.partial(partners_kernel, place),
         out_shape=outs,
-        in_specs=[ANY] * coils,
-        out_specs=[ANY] * len(outs),
-        scratch_shapes=[pltpu.SemaphoreType.DMA((cuts - 1, coils))],
+        in_specs=[VMEM] * coils,
+        out_specs=[VMEM] * len(outs),
         interpret=INTERPRET,
-    )(*senses)
+    )(*[near(x) for x in senses])
 
 
 CHUNKS = 4
 
 
-def adjoint_kernel(place, kspace, sens, mask, table_x, back_y, back_z, *refs):
+def adjoint_kernel(place, kspace, sens, mask, tables_x, back_y, back_z, *refs):
     coils, cuts = lax.axis_size("coil"), lax.axis_size("cuts")
     outs = refs[:cuts]
-    data, own_sens, by_row, by_slice, stage, sems = refs[cuts:]
+    data, own_sens, table_x, planes, rows_z, stage, sems = refs[cuts:]
     size_x, rows, width = data.shape
     height = rows // 2
     kept = coils * place.run
     slab, block = place.slab(), place.half_block()
     chunk = size_x // CHUNKS
-    copies = []
+    copies = [pltpu.make_async_copy(tables_x.at[block], table_x, sems.at[0])]
     for i in range(CHUNKS):
         at = pl.ds(i * chunk, chunk)
-        copies.append(pltpu.make_async_copy(kspace.at[slab, 0, at], data.at[at], sems.at[i]))
+        copies.append(pltpu.make_async_copy(kspace.at[slab, 0, at], data.at[at], sems.at[1 + i]))
+    first_sens = len(copies)
     for q in range(coils):
         source = sens.at[slab, 0, pl.ds(q * place.owned + block * place.run, place.run)]
         target = own_sens.at[pl.ds(q * place.run, place.run)]
-        copies.append(pltpu.make_async_copy(source, target, sems.at[CHUNKS + q]))
+        copies.append(pltpu.make_async_copy(source, target, sems.at[first_sens + q]))
     for copy in copies:
         copy.start()
-    for i in range(CHUNKS):
-        copies[i].wait()
-        for x in range(i * chunk, (i + 1) * chunk):
-            by_row[pl.ds(x, rows, stride=size_x), :] = data[x].astype(F32)
-    selected = table_x[block]
-
-    def along_x(y, _):
-        operand = by_row[pl.ds(pl.multiple_of(y * 2 * size_x, 2 * size_x), 2 * size_x), :].astype(BF16)
-        w = jnp.dot(selected, operand, preferred_element_type=F32)
-        by_slice[pl.ds(y, 2 * kept, stride=height), :] = w
-
-    lax.fori_loop(0, height, along_x, None, unroll=8)
-    for copy in copies[CHUNKS:]:
+    for copy in copies[:first_sens]:
         copy.wait()
     weight_mask = mask[slab].astype(F32)
+    groups = rows // (2 * TILE)
+    for g in range(0, groups, 2):
+        both = [
+            data[:, (g + i) * 2 * TILE : (g + i + 1) * 2 * TILE, :].reshape(size_x * 2 * TILE, width)
+            for i in range(2)
+        ]
+        w = jnp.dot(table_x[...], jnp.concatenate(both, axis=1), preferred_element_type=F32)
+        for i in range(2):
+            at = slice((g + i) * TILE, (g + i + 1) * TILE)
+            part = w[:, i * width : (i + 1) * width].reshape(2 * kept, TILE, width)
+            planes[:, at, :] = part * weight_mask[at][None]
+    for n in range(0, kept, 2):
+        pair = [
+            jnp.concatenate([planes[2 * (n + i)], planes[2 * (n + i) + 1]], axis=0).astype(BF16)
+            for i in range(2)
+        ]
+        w = jnp.dot(back_y[...], jnp.concatenate(pair, axis=1), preferred_element_type=F32).astype(BF16)
+        for i in range(2):
+            lanes = slice(i * width, (i + 1) * width)
+            rows_z[n + i] = jnp.concatenate([w[:height, lanes], w[height:, lanes]], axis=1)
+    for copy in copies[first_sens:]:
+        copy.wait()
     for k, (_, target, _) in enumerate(own_and_peers("cuts")):
-
-        def one(q, _, k=k, target=target):
+        for q in range(coils):
             for s in range(place.per):
                 n = q * place.run + place.cut_block(target) * place.per + s
-                parts = []
-                for part in range(2):
-                    start = pl.multiple_of((part * kept + n) * height, 16)
-                    w = by_slice[pl.ds(start, height), :]
-                    parts.append((w.astype(BF16).astype(F32) * weight_mask).astype(BF16))
-                w = jnp.concatenate(parts, axis=0)
-                w = jnp.dot(back_y[...], w, preferred_element_type=F32).astype(BF16)
-                w = jnp.concatenate([w[:height], w[height:]], axis=1)
-                w = jnp.dot(w, back_z[...], preferred_element_type=F32)
+                w = jnp.dot(rows_z[n], back_z[...], preferred_element_type=F32)
                 br, bi = w[:, :width], w[:, width:]
-                stage[s] = own_sens[n].astype(F32)
-                sr, si = (stage.at[s][pl.ds(part, height, stride=2), :] for part in range(2))
+                slot = stage.at[(q * place.per + s) % stage.shape[0]]
+                slot[...] = own_sens[n].astype(F32)
+                sr, si = (slot[pl.ds(part, height, stride=2), :] for part in range(2))
                 outs[k][q, s, 0] = (sr * br + si * bi).astype(BF16)
                 outs[k][q, s, 1] = (sr * bi - si * br).astype(BF16)
-
-        lax.fori_loop(0, coils, one, None, unroll=4)
 
 
 def adjoint(place, kspace, sens, mask):
@@ -504,23 +501,25 @@
     height = rows // 2
     kept = coils * place.run
     table = dft_table(size_x, -1.0).reshape(2, size_x, 2, coils, place.by_half, place.run)
-    table = table.transpose(4, 2, 3, 5, 0, 1).reshape(place.by_half, 2 * kept, 2 * size_x)
-    tables = [table, dft_table(height, -1.0).T.copy(), dft_table(width, -1.0)]
+    table = np.einsum("cxdqbr,uv->bqrduxvc", table.astype(np.float32), np.eye(TILE, dtype=np.float32))
+    table = table.reshape(place.by_half, 2 * kept * TILE, 2 * size_x * TILE).astype(ml_dtypes.bfloat16)
+    tables = [jnp.asarray(t) for t in (table, dft_table(height, -1.0).T.copy(), dft_table(width, -1.0))]
     return pl.pallas_call(
         functools.partial(adjoint_kernel, place),
-        out_shape=[jax.ShapeDtypeStruct((coils, place.per, 2, height, width), BF16)] * cuts,
-        in_specs=[ANY, ANY] + [VMEM] * 4,
+        out_shape=[near_out((coils, place.per, 2, height, width), BF16)] * cuts,
+        in_specs=[ANY, ANY, VMEM, ANY, VMEM, VMEM],
         out_specs=[VMEM] * cuts,
         scratch_shapes=[
             pltpu.VMEM((size_x, rows, width), BF16),
             pltpu.VMEM((kept, rows, width), BF16),
-            pltpu.VMEM((rows * size_x, width), F32),
-            pltpu.VMEM((2 * kept * height, width), F32),
-            pltpu.VMEM((place.per, rows, width), F32),
-            pltpu.SemaphoreType.DMA((CHUNKS + coils,)),
+            pltpu.VMEM(table.shape[1:], BF16),
+            pltpu.VMEM((2 * kept, height, width), F32),
+            pltpu.VMEM((kept, height, 2 * width), BF16),
+            pltpu.VMEM((4, rows, width), F32),
+            pltpu.SemaphoreType.DMA((1 + CHUNKS + coils,)),
         ],
         interpret=INTERPRET,
-    )(kspace, sens, mask, *[jnp.asarray(t) for t in tables])
+    )(kspace, sens, near(mask), tables[0], near(tables[1]), near(tables[2]))
 
 
 def pair_sum_kernel(n_in, *refs):
@@ -533,11 +532,11 @@
     coils = lax.axis_size("coil")
     return pl.pallas_call(
         functools.partial(pair_sum_kernel, len(terms)),
-        out_shape=[jax.ShapeDtypeStruct(terms[0].shape[1:], BF16)] * coils,
+        out_shape=[near_out(terms[0].shape[1:], BF16)] * coils,
         in_specs=[VMEM] * len(terms),
         out_specs=[VMEM] * coils,
         interpret=INTERPRET,
-    )(*terms)
+    )(*[near(t) for t in terms])
 
 
 class Place:
@@ -577,23 +576,17 @@
         return array.reshape(array.shape[:-3] + (array.shape[-3] * 2, size_z))
 
     initial, sens, kspace = joined(initial), joined(sens), joined(kspace)
-    sens_pieces, image_pieces = split(place, sens, initial)
+    sens_pieces, image_pieces, packed = split(place, sens, initial, conv_in[0], bias_in, conv_out[0], step_sizes)
     senses = sent(sens_pieces, "coil")
-
+    weights = sent([packed] * sections, "section")
+    image_pieces = sent(image_pieces, "cuts")
     terms = adjoint(place, kspace, sens, mask)
-    terms = [terms[0]] + [
-        lax.ppermute(terms[k + 1], "cuts", route) for k, (route, _, _) in enumerate(peers("cuts"))
-    ]
-    datas = sent(pair_sum(terms), "coil")
-
-    packed = pack_weights(conv_in[0], bias_in, conv_out[0], step_sizes)
-    weights = sent([packed] * sections, "section")
-    first, planes = first_refine(sent(image_pieces, "cuts"), weights)
-
-    more = [
-        lax.ppermute(piece, "cuts", route)
-        for piece, (route, _, _) in zip(for_partners(place, senses), peers("cuts"))
-    ]
+    terms = sent(terms, "cuts")
+    sums = pair_sum(terms)
+    datas = sent(sums, "coil")
+    given = for_partners(place, senses)
+    more = sent([None] + list(given), "cuts")[1:]
+    first, planes = first_refine(image_pieces, weights)
     out = run_cascades(planes, first, mask, weights, senses, more, datas, cuts, place.by_cut)
     out = lax.all_to_all(out, ("section", "cuts"), 0, 0, tiled=True)
     out = out.reshape(slabs, place.halves, cuts, place.per, rows, 2, size_z)

time: 114 us -> 72 us (0.63)
  Pallas kernels: 76.4 us -> 30.5 us
  waiting for transfers between devices: 7.44 us -> 14 us
  local copies, waits for them, and re-layouts: 3.53 us -> 0.75 us
    pallas_call x1, Pallas kernels: 23.5 us -> 2.02 us  [split(): pl.pallas_call(functools.partial(split_kernel, place), out_shape=outs, in...]
    pallas_call x1, Pallas kernels: 11.1 us -> 0.02 us  [for_partners(): pl.pallas_call(functools.partial(partners_kernel, place), out_shape=outs,...]
    pallas_call x2 -> x1, Pallas kernels: 11.5 us -> 2.95 us  [adjoint(): pl.pallas_call(functools.partial(adjoint_kernel, place), out_shape=[near_...]
    ppermute x10 -> x12, waiting for transfers between devices: 7.43 us -> 14 us  [sent(): arrived.append(lax.ppermute(pieces[k + 1], axis, route))]
    unnamed x27 -> x11, local copies, waits for them, and re-layouts: 3.53 us -> 0.75 us
    pallas_call x1, Pallas kernels: 1.82 us -> 0.08 us  [pair_sum(): pl.pallas_call(functools.partial(pair_sum_kernel, len(terms)), out_shape=...]
    pallas_call x1, Pallas kernels: 23.8 us -> 22.2 us  [run_cascades(): pl.pallas_call(functools.partial(cascades_kernel, len(weights), len(sense...]
    pallas_call x1, Pallas kernels: 4.76 us -> 3.22 us  [first_refine(): pl.pallas_call(functools.partial(first_refine_kernel, len(pieces), len(we...]
  transfers between devices with their start and end apart: 12 -> 12, of which waited for: 3 -> 4; matrix products, arithmetic and copies ran while one was open for 0% -> 0% of each run, Pallas kernels for 26% -> 9%
where the time goes in v2:
time: 72 us; the launch traced here: 71.7 us
  Pallas kernels  30.5 us (42%)
  starting transfers between devices  14.6 us (20%)
  waiting for transfers between devices  14 us (19%)
  blocking collectives  10.9 us (15%)
  between operations  0.83 us (1%)
  local copies, waits for them, and re-layouts  0.75 us (1%)
    pallas_call x1, Pallas kernels, run_cascades(): pl.pallas_call(functools.partial(cascades_kernel, len(weights), len(sense...  22.2 us
    ppermute x12, starting transfers between devices, sent(): arrived.append(lax.ppermute(pieces[k + 1], axis, route))  14.6 us
    ppermute x12, waiting for transfers between devices, sent(): arrived.append(lax.ppermute(pieces[k + 1], axis, route))  14 us
    all_to_all x1, blocking collectives, body(): out = lax.all_to_all(out, ('section', 'cuts'), 0, 0, tiled=True)  10.9 us
    pallas_call x1, Pallas kernels, first_refine(): pl.pallas_call(functools.partial(first_refine_kernel, len(pieces), len(we...  3.22 us
    pallas_call x1, Pallas kernels, adjoint(): pl.pallas_call(functools.partial(adjoint_kernel, place), out_shape=[near_...  2.95 us
    pallas_call x1, Pallas kernels, split(): pl.pallas_call(functools.partial(split_kernel, place), out_shape=outs, in...  2.02 us
  transfers between devices with their start and end apart: 12, of which 4 were waited for; matrix products, arithmetic and copies ran while one was open for 0% of the time, Pallas kernels for 9%

profile of v2, /device:TPU:0, one launch (start us, length us, event | category | flops | bytes accessed | tf_op | source)
XLA Modules:
  0.0 71.7 jit_solution(9306825547669709175)
XLA Ops:
  0.0 0.0 copy-start
  0.0 0.0 copy-start.2
  0.0 0.0 copy-start.1
  0.7 2.0 %shard_map.154 = (bf16[4,160,128]{2,1,0:T(8,128)(2,1)S(1)}, bf16[4,160,128]{2,1,0:T(8,128)(2,1)S(1)}, bf16[4,160,128]{2,1,0:T(8,128)(2,1)S(1)}, bf16[4,160,128]{...) custom-call(bf16[2,1,32,160,128]{4,3,2,1,0:T(8,128)(2,1)} %bitcast.8, ...), custom_call_target="tpu_custom_call" | custom-call | tf_op jit(solution)/shard_map/pallas_call | solution.py:406
  2.7 3.1 %collective-permute-start.4 = (bf16[4,160,128]{2,1,0:T(8,128)(2,1)S(1)}, bf16[4,160,128]{2,1,0:T(8,128)(2,1)S(1)}, u32[]{:S(2)}, u32[]{:S(2)}) collective-permute-start(bf16[4,160,128]{2,1,0:T(8,128)(2,1)S(1)} %get-tuple-element.26), channel_id=1, source_target_pairs={{0,2},{2,0},{4,6},{6,4},{1,3},{3,1},{5,7},{7,5},{8,10},{10,8},{12,... | collective-permute-start | bytes 491528 | tf_op jit(solution)/shard_map/ppermute | solution.py:565
  5.9 2.6 %collective-permute-start.5 = (bf16[4,160,128]{2,1,0:T(8,128)(2,1)S(1)}, bf16[4,160,128]{2,1,0:T(8,128)(2,1)S(1)}, u32[]{:S(2)}, u32[]{:S(2)}) collective-permute-start(bf16[4,160,128]{2,1,0:T(8,128)(2,1)S(1)} %get-tuple-element.27), channel_id=1, source_target_pairs={{0,4},{2,6},{4,0},{6,2},{1,5},{3,7},{5,1},{7,3},{8,12},{10,14},{12... | collective-permute-start | bytes 491528 | tf_op jit(solution)/shard_map/ppermute | solution.py:565
  8.4 0.0 collective-permute-start.6
  8.4 0.0 copy-done
  8.4 0.0 copy-done.2
  8.5 0.0 copy-done.1
  8.5 0.0 copy-start.3
  8.5 0.0 copy-start.4
  8.5 2.9 %shard_map.157 = (bf16[4,2,2,80,128]{4,3,2,1,0:T(8,128)(2,1)S(1)}, bf16[4,2,2,80,128]{4,3,2,1,0:T(8,128)(2,1)S(1)}) custom-call(bf16[2,1,32,160,128]{4,3,2,1,0:T(8,128)(2,1)} %bitcast.10, bf16[2,1,32,160,128]{4,3,2,1,0:T(8,128)(2,1)} %bitcast.9, s32[2,80,128]{2,1,0:T(8,128)S(1)} %copy-done.1, bf16[2,256,512]{2,1,0:T(8,128)(2,1)} %constant.13.clone.tables_x, ...), custom_call_target="tpu_custom_call" | custom-call | tf_op jit(solution)/shard_map/pallas_call | solution.py:507
  11.4 0.1 collective-permute-start.8
  11.5 1.0 %collective-permute-done.4.refs_1_.refs_12_ = bf16[4,160,128]{2,1,0:T(8,128)(2,1)S(1)} collective-permute-done((bf16[4,160,128]{2,1,0:T(8,128)(2,1)S(1)}, bf16[4,160,128]{2,1,0:T(8,128)(2,1)S(1)}, u32[]{:S(2)}, u32[]{:S(2)}) %collective-permute-start.4) | collective-permute-done | bytes 163872 | tf_op jit(solution)/shard_map/ppermute | solution.py:565
  12.6 8.3 %collective-permute-done.5.refs_2_.refs_13_ = bf16[4,160,128]{2,1,0:T(8,128)(2,1)S(1)} collective-permute-done((bf16[4,160,128]{2,1,0:T(8,128)(2,1)S(1)}, bf16[4,160,128]{2,1,0:T(8,128)(2,1)S(1)}, u32[]{:S(2)}, u32[]{:S(2)}) %collective-permute-start.5) | collective-permute-done | bytes 163872 | tf_op jit(solution)/shard_map/ppermute | solution.py:565
  20.8 0.0 collective-permute-done.6.refs_3_.refs_14_
  20.9 0.1 collective-permute-start.7
  21.0 2.5 %collective-permute-start.3 = (bf16[136,128]{1,0:T(8,128)(2,1)S(1)}, bf16[136,128]{1,0:T(8,128)(2,1)S(1)}, u32[]{:S(2)}, u32[]{:S(2)}) collective-permute-start(bf16[136,128]{1,0:T(8,128)(2,1)S(1)} %get-tuple-element.22.refs_2_.refs_7_), channel_id=1, source_target_pairs={{0,24},{8,16},{16,8},{24,0},{1,25},{9,17},{17,9},{25,1},{2,26},{10... | collective-permute-start | bytes 104456 | tf_op jit(solution)/shard_map/ppermute | solution.py:565
  23.5 0.5 collective-permute-start.2
  24.0 0.0 collective-permute-done.8.refs_1_
  24.0 0.1 shard_map.158
  24.1 2.8 %collective-permute-start.9 = (bf16[2,2,80,128]{3,2,1,0:T(8,128)(2,1)S(1)}, bf16[2,2,80,128]{3,2,1,0:T(8,128)(2,1)S(1)}, u32[]{:S(2)}, u32[]{:S(2)}) collective-permute-start(bf16[2,2,80,128]{3,2,1,0:T(8,128)(2,1)S(1)} %get-tuple-element.32), channel_id=1, source_target_pairs={{0,2},{2,0},{4,6},{6,4},{1,3},{3,1},{5,7},{7,5},{8,10},{10,8},{12,... | collective-permute-start | bytes 245768 | tf_op jit(solution)/shard_map/ppermute | solution.py:565
  26.8 1.1 %collective-permute-start.10 = (bf16[2,2,80,128]{3,2,1,0:T(8,128)(2,1)S(1)}, bf16[2,2,80,128]{3,2,1,0:T(8,128)(2,1)S(1)}, u32[]{:S(2)}, u32[]{:S(2)}) collective-permute-start(bf16[2,2,80,128]{3,2,1,0:T(8,128)(2,1)S(1)} %get-tuple-element.33), channel_id=1, source_target_pairs={{0,4},{2,6},{4,0},{6,2},{1,5},{3,7},{5,1},{7,3},{8,12},{10,14},{12... | collective-permute-start | bytes 245768 | tf_op jit(solution)/shard_map/ppermute | solution.py:565
  27.9 0.0 collective-permute-done.3.refs_5_.refs_10_
  27.9 1.4 %collective-permute-start.11 = (bf16[2,2,80,128]{3,2,1,0:T(8,128)(2,1)S(1)}, bf16[2,2,80,128]{3,2,1,0:T(8,128)(2,1)S(1)}, u32[]{:S(2)}, u32[]{:S(2)}) collective-permute-start(bf16[2,2,80,128]{3,2,1,0:T(8,128)(2,1)S(1)} %get-tuple-element.34), channel_id=1, source_target_pairs={{0,6},{2,4},{4,2},{6,0},{1,7},{3,5},{5,3},{7,1},{8,14},{10,12},{12... | collective-permute-start | bytes 245768 | tf_op jit(solution)/shard_map/ppermute | solution.py:565
  29.3 0.0 collective-permute-done.2.refs_4_.refs_9_
  29.3 0.5 collective-permute-start.1
  29.8 3.4 %collective-permute-done.1.refs_3_.refs_8_ = bf16[136,128]{1,0:T(8,128)(2,1)S(1)} collective-permute-done((bf16[136,128]{1,0:T(8,128)(2,1)S(1)}, bf16[136,128]{1,0:T(8,128)(2,1)S(1)}, u32[]{:S(2)}, u32[]{:S(2)}) %collective-permute-start.1) | collective-permute-done | bytes 34848 | tf_op jit(solution)/shard_map/ppermute | solution.py:565
  33.2 0.0 collective-permute-start
  33.3 1.2 %collective-permute-done.refs_1_ = bf16[2,80,128]{2,1,0:T(8,128)(2,1)S(1)} collective-permute-done((bf16[2,80,128]{2,1,0:T(8,128)(2,1)S(1)}, bf16[2,80,128]{2,1,0:T(8,128)(2,1)S(1)}, u32[]{:S(2)}, u32[]{:S(2)}) %collective-permute-start) | collective-permute-done | bytes 40992 | tf_op jit(solution)/shard_map/ppermute | solution.py:565
  34.5 3.2 %shard_map.155 = (f32[2,80,256]{2,1,0:T(8,128)S(1)}, f32[2,80,256]{2,1,0:T(8,128)S(1)}) custom-call(bf16[2,80,128]{2,1,0:T(8,128)(2,1)S(1)} %get-tuple-element.20.refs_0_, bf16[2,80,128]{2,1,0:T(8,128)(2,1)S(1)} %collective-permute-done.refs_1_, bf16[136,128]{1,0:T(8,128)(2,1)S(1)} %get-tuple-element.22.refs_2_.refs_7_, ...), custom_call_target="tpu_custom_call" | custom-call | tf_op jit(solution)/shard_map/pallas_call | solution.py:336
  37.7 0.0 collective-permute-done.9.refs_17_
  37.7 0.0 collective-permute-done.10.refs_18_
  37.7 0.0 collective-permute-done.11.refs_19_
  37.7 0.0 collective-permute-done.7.refs_15_
  37.7 0.0 copy-done.3
  37.7 0.0 copy-done.4
  37.8 22.2 %shard_map.159 = bf16[8,2,80,128]{3,2,1,0:T(8,128)(2,1)} custom-call(f32[2,80,256]{2,1,0:T(8,128)S(1)} %get-tuple-element.23.refs_0_, f32[2,80,256]{2,1,0:T(8,128)S(1)} %get-tuple-element.24.refs_1_, s32[2,80,128]{2,1,0:T(8,128)S(1)} %copy-done.1, bf16[256,256]{1,0:T(8,128)(2,1)S(1)} %copy-done.3, bf16[256,256]{1,0:T(8,128)(2,1)S(1)} %copy-done, ...), custom_call_target="tpu_custom_call" | custom-call | tf_op jit(solution)/shard_map/pallas_call | solution.py:359
  60.0 10.9 %all_to_all.5 = bf16[8,2,80,128]{3,2,1,0:T(8,128)(2,1)S(1)} all-to-all(bf16[8,2,80,128]{3,2,1,0:T(8,128)(2,1)} %shard_map.159), channel_id=1, replica_groups=mesh['section'=4,'coil'=4,'cuts'=2] {'section','cuts'}, dimensions={0} | all-to-all | bytes 655360 | tf_op jit(solution)/shard_map/all_to_all | solution.py:591
  70.9 0.7 %copy.19 = bf16[1,2,8,40,2,128]{5,4,3,2,1,0:T(2,128)(2,1)} copy(bf16[1,2,8,40,2,128]{5,4,3,2,1,0:T(2,128)(2,1)S(1)} %bitcast.11) | data formatting | bytes 655360
  (1 shorter events, 0.0 us)
Async XLA Ops:
  0.0 8.4 %copy-start = (bf16[256,256]{1,0:T(8,128)(2,1)S(1)}, bf16[256,256]{1,0:T(8,128)(2,1)}, u32[]{:S(2)}) copy-start(bf16[256,256]{1,0:T(8,128)(2,1)} %constant.15.clone.back_z.refs_4_) | copy-start | bytes 393220
  0.0 8.4 %copy-start.2 = (bf16[160,160]{1,0:T(8,128)(2,1)S(1)}, bf16[160,160]{1,0:T(8,128)(2,1)}, u32[]{:S(2)}) copy-start(bf16[160,160]{1,0:T(8,128)(2,1)} %constant.14.clone.back_y.refs_6_) | copy-start | bytes 153604
  0.0 8.5 %copy-start.1 = (s32[2,80,128]{2,1,0:T(8,128)S(1)}, s32[2,80,128]{2,1,0:T(8,128)}, u32[]{:S(2)}) copy-start(s32[2,80,128]{2,1,0:T(8,128)} %refs_2_.1) | copy-start | bytes 245764
  2.7 9.8 %collective-permute-start.4 = (bf16[4,160,128]{2,1,0:T(8,128)(2,1)S(1)}, bf16[4,160,128]{2,1,0:T(8,128)(2,1)S(1)}, u32[]{:S(2)}, u32[]{:S(2)}) collective-permute-start(bf16[4,160,128]{2,1,0:T(8,128)(2,1)S(1)} %get-tuple-element.26), channel_id=1, source_target_pairs={{0,2},{2,0},{4,6},{6,4},{1,3},{3,1},{5,7},{7,5},{8,10},{10,8},{12,... | collective-permute-start | bytes 491528 | tf_op jit(solution)/shard_map/ppermute | solution.py:565
  5.9 15.0 %collective-permute-start.5 = (bf16[4,160,128]{2,1,0:T(8,128)(2,1)S(1)}, bf16[4,160,128]{2,1,0:T(8,128)(2,1)S(1)}, u32[]{:S(2)}, u32[]{:S(2)}) collective-permute-start(bf16[4,160,128]{2,1,0:T(8,128)(2,1)S(1)} %get-tuple-element.27), channel_id=1, source_target_pairs={{0,4},{2,6},{4,0},{6,2},{1,5},{3,7},{5,1},{7,3},{8,12},{10,14},{12... | collective-permute-start | bytes 491528 | tf_op jit(solution)/shard_map/ppermute | solution.py:565
  8.4 12.4 %collective-permute-start.6 = (bf16[4,160,128]{2,1,0:T(8,128)(2,1)S(1)}, bf16[4,160,128]{2,1,0:T(8,128)(2,1)S(1)}, u32[]{:S(2)}, u32[]{:S(2)}) collective-permute-start(bf16[4,160,128]{2,1,0:T(8,128)(2,1)S(1)} %get-tuple-element.28), channel_id=1, source_target_pairs={{0,6},{2,4},{4,2},{6,0},{1,7},{3,5},{5,3},{7,1},{8,14},{10,12},{12... | collective-permute-start | bytes 491528 | tf_op jit(solution)/shard_map/ppermute | solution.py:565
  8.5 29.3 %copy-start.3 = (bf16[256,256]{1,0:T(8,128)(2,1)S(1)}, bf16[256,256]{1,0:T(8,128)(2,1)}, u32[]{:S(2)}) copy-start(bf16[256,256]{1,0:T(8,128)(2,1)} %constant.16.clone.refs_3_) | copy-start | bytes 393220
  8.5 29.3 %copy-start.4 = (bf16[160,160]{1,0:T(8,128)(2,1)S(1)}, bf16[160,160]{1,0:T(8,128)(2,1)}, u32[]{:S(2)}) copy-start(bf16[160,160]{1,0:T(8,128)(2,1)} %constant.17.clone.refs_5_) | copy-start | bytes 153604
  11.4 12.5 %collective-permute-start.8 = (bf16[4,2,2,80,128]{4,3,2,1,0:T(8,128)(2,1)S(1)}, bf16[4,2,2,80,128]{4,3,2,1,0:T(8,128)(2,1)S(1)}, u32[]{:S(2)}, u32[]{:S(2)}) collective-permute-start(bf16[4,2,2,80,128]{4,3,2,1,0:T(8,128)(2,1)S(1)} %get-tuple-element.30), channel_id=1, source_target_pairs={{0,1},{1,0},{2,3},{3,2},{4,5},{5,4},{6,7},{7,6},{8,9},{9,8},{10,11... | collective-permute-start | bytes 983048 | tf_op jit(solution)/shard_map/ppermute | solution.py:565
  20.9 16.9 %collective-permute-start.7 = (bf16[4,2,160,128]{3,2,1,0:T(8,128)(2,1)S(1)}, bf16[4,2,160,128]{3,2,1,0:T(8,128)(2,1)S(1)}, u32[]{:S(2)}, u32[]{:S(2)}) collective-permute-start(bf16[4,2,160,128]{3,2,1,0:T(8,128)(2,1)S(1)} %shard_map.156), channel_id=1, source_target_pairs={{0,1},{1,0},{2,3},{3,2},{4,5},{5,4},{6,7},{7,6},{8,9},{9,8},{10,11... | collective-permute-start | bytes 983048 | tf_op jit(solution)/shard_map/ppermute | solution.py:565
  21.0 7.0 %collective-permute-start.3 = (bf16[136,128]{1,0:T(8,128)(2,1)S(1)}, bf16[136,128]{1,0:T(8,128)(2,1)S(1)}, u32[]{:S(2)}, u32[]{:S(2)}) collective-permute-start(bf16[136,128]{1,0:T(8,128)(2,1)S(1)} %get-tuple-element.22.refs_2_.refs_7_), channel_id=1, source_target_pairs={{0,24},{8,16},{16,8},{24,0},{1,25},{9,17},{17,9},{25,1},{2,26},{10... | collective-permute-start | bytes 104456 | tf_op jit(solution)/shard_map/ppermute | solution.py:565
  23.5 5.8 %collective-permute-start.2 = (bf16[136,128]{1,0:T(8,128)(2,1)S(1)}, bf16[136,128]{1,0:T(8,128)(2,1)S(1)}, u32[]{:S(2)}, u32[]{:S(2)}) collective-permute-start(bf16[136,128]{1,0:T(8,128)(2,1)S(1)} %get-tuple-element.22.refs_2_.refs_7_), channel_id=1, source_target_pairs={{0,16},{8,24},{16,0},{24,8},{1,17},{9,25},{17,1},{25,9},{2,18},{10... | collective-permute-start | bytes 104456 | tf_op jit(solution)/shard_map/ppermute | solution.py:565
  24.1 13.6 %collective-permute-start.9 = (bf16[2,2,80,128]{3,2,1,0:T(8,128)(2,1)S(1)}, bf16[2,2,80,128]{3,2,1,0:T(8,128)(2,1)S(1)}, u32[]{:S(2)}, u32[]{:S(2)}) collective-permute-start(bf16[2,2,80,128]{3,2,1,0:T(8,128)(2,1)S(1)} %get-tuple-element.32), channel_id=1, source_target_pairs={{0,2},{2,0},{4,6},{6,4},{1,3},{3,1},{5,7},{7,5},{8,10},{10,8},{12,... | collective-permute-start | bytes 245768 | tf_op jit(solution)/shard_map/ppermute | solution.py:565
  26.8 10.9 %collective-permute-start.10 = (bf16[2,2,80,128]{3,2,1,0:T(8,128)(2,1)S(1)}, bf16[2,2,80,128]{3,2,1,0:T(8,128)(2,1)S(1)}, u32[]{:S(2)}, u32[]{:S(2)}) collective-permute-start(bf16[2,2,80,128]{3,2,1,0:T(8,128)(2,1)S(1)} %get-tuple-element.33), channel_id=1, source_target_pairs={{0,4},{2,6},{4,0},{6,2},{1,5},{3,7},{5,1},{7,3},{8,12},{10,14},{12... | collective-permute-start | bytes 245768 | tf_op jit(solution)/shard_map/ppermute | solution.py:565
  27.9 9.8 %collective-permute-start.11 = (bf16[2,2,80,128]{3,2,1,0:T(8,128)(2,1)S(1)}, bf16[2,2,80,128]{3,2,1,0:T(8,128)(2,1)S(1)}, u32[]{:S(2)}, u32[]{:S(2)}) collective-permute-start(bf16[2,2,80,128]{3,2,1,0:T(8,128)(2,1)S(1)} %get-tuple-element.34), channel_id=1, source_target_pairs={{0,6},{2,4},{4,2},{6,0},{1,7},{3,5},{5,3},{7,1},{8,14},{10,12},{12... | collective-permute-start | bytes 245768 | tf_op jit(solution)/shard_map/ppermute | solution.py:565
  29.3 3.9 %collective-permute-start.1 = (bf16[136,128]{1,0:T(8,128)(2,1)S(1)}, bf16[136,128]{1,0:T(8,128)(2,1)S(1)}, u32[]{:S(2)}, u32[]{:S(2)}) collective-permute-start(bf16[136,128]{1,0:T(8,128)(2,1)S(1)} %get-tuple-element.22.refs_2_.refs_7_), channel_id=1, source_target_pairs={{0,8},{8,0},{16,24},{24,16},{1,9},{9,1},{17,25},{25,17},{2,10},{10... | collective-permute-start | bytes 104456 | tf_op jit(solution)/shard_map/ppermute | solution.py:565
  33.2 1.2 %collective-permute-start = (bf16[2,80,128]{2,1,0:T(8,128)(2,1)S(1)}, bf16[2,80,128]{2,1,0:T(8,128)(2,1)S(1)}, u32[]{:S(2)}, u32[]{:S(2)}) collective-permute-start(bf16[2,80,128]{2,1,0:T(8,128)(2,1)S(1)} %get-tuple-element.21), channel_id=1, source_target_pairs={{0,1},{1,0},{2,3},{3,2},{4,5},{5,4},{6,7},{7,6},{8,9},{9,8},{10,11... | collective-permute-start | bytes 122888 | tf_op jit(solution)/shard_map/ppermute | solution.py:565

commit v3 on v2

--- a/solution.py
+++ b/solution.py
@@ -64,8 +64,16 @@
     return x if far() else pltpu.with_memory_space_constraint(x, pltpu.VMEM)
 
 
+def away(x):
+    return x if INTERPRET else pltpu.with_memory_space_constraint(x, pltpu.HBM)
+
+
 def near_out(shape, dtype):
     return jax.ShapeDtypeStruct(shape, dtype) if far() else pltpu.VMEM(shape, dtype)
+
+
+def kernel_params():
+    return None if far() else pltpu.CompilerParams(vmem_limit_bytes=20 << 20)
 
 
 def selections():
@@ -213,89 +221,118 @@
     return chosen
 
 
-def cascades_kernel(n_weights, n_sens, n_more, n_data, by_cut, *refs):
-    planes_in, first, mask, forward_z, back_z, forward_y, back_y = refs[:7]
-    at = 7
+def subtract_normal(planes, coil_planes, weight_mask, tables, gradient, rows_y, rows_z):
+    forward_z, back_z, forward_y, back_y = tables
+    count, _, height, width = coil_planes.shape
+    per = planes.shape[2] // width
+    assert per <= 2
+    pairs = count // 2
+
+    def each_pair(step):
+        if pairs <= 8:
+            for m in range(pairs):
+                step(m)
+        else:
+            lax.fori_loop(0, pairs, lambda m, _: step(m), None)
+
+    def sens_and_lanes(m, i):
+        n, s = 2 * m + i, i % per
+        sens = coil_planes[n, 0].astype(F32), coil_planes[n, 1].astype(F32)
+        return *sens, slice(s * width, (s + 1) * width)
+
+    def product(m):
+        coils = []
+        for i in range(2):
+            sr, si, lanes = sens_and_lanes(m, i)
+            ir, ii = planes[0, :, lanes], planes[1, :, lanes]
+            coils.append(jnp.concatenate([sr * ir - si * ii, sr * ii + si * ir], axis=1).astype(BF16))
+        w = jnp.dot(jnp.concatenate(coils, axis=0), forward_z[...], preferred_element_type=F32)
+        w = w.astype(BF16)
+        for i in range(2):
+            for part in range(2):
+                block = w[i * height : (i + 1) * height, part * width : (part + 1) * width]
+                rows_y[m, part * height : (part + 1) * height, i * width : (i + 1) * width] = block
+
+    def forward(m):
+        w = jnp.dot(forward_y[...], rows_y[m], preferred_element_type=F32)
+        for i in range(2):
+            lanes = slice(i * width, (i + 1) * width)
+            rows_y[m, :, lanes] = (w[:, lanes] * weight_mask).astype(BF16)
+
+    def back(m):
+        w = jnp.dot(back_y[...], rows_y[m], preferred_element_type=F32).astype(BF16)
+        for i in range(2):
+            for part in range(2):
+                block = w[part * height : (part + 1) * height, i * width : (i + 1) * width]
+                rows_z[m, i * height : (i + 1) * height, part * width : (part + 1) * width] = block
+
+    def gather(m):
+        w = jnp.dot(rows_z[m], back_z[...], preferred_element_type=F32)
+        for i in range(2):
+            sr, si, lanes = sens_and_lanes(m, i)
+            br = w[i * height : (i + 1) * height, :width]
+            bi = w[i * height : (i + 1) * height, width:]
+            gradient[0, :, lanes] -= sr * br + si * bi
+            gradient[1, :, lanes] -= sr * bi - si * br
+
+    for stage in (product, forward, back, gather):
+        each_pair(stage)
+
+
+def mask_of(place, mask):
+    weight_mask = mask[place.slab()].astype(F32)
+    return jnp.concatenate([weight_mask] * 2, axis=0)
+
+
+def first_normal_kernel(place, n_sens, planes, mask, *refs):
+    tables, senses, more = refs[:4], refs[4 : 4 + n_sens], refs[4 + n_sens : -5]
+    coil_planes, normal, rows_y, rows_z, stage = refs[-5:]
+    height = coil_planes.shape[2]
+
+    def keep(n, rows):
+        slot = stage.at[n % stage.shape[0]]
+        slot[...] = rows.astype(F32)
+        for part in range(2):
+            coil_planes[n, part] = slot[pl.ds(part, height, stride=2), :].astype(BF16)
+
+    start = place.cut_block(lax.axis_index("cuts")) * place.per
+    n = 0
+    for ref in senses:
+        for s in range(place.per):
+            keep(n, ref[start + s])
+            n += 1
+    for ref in more:
+        for q in range(ref.shape[0]):
+            for s in range(place.per):
+                keep(n, ref[q, s])
+                n += 1
+    normal[...] = jnp.zeros(normal.shape, F32)
+    subtract_normal(planes, coil_planes, mask_of(place, mask), tables, normal, rows_y, rows_z)
+
+
+def cascades_kernel(place, n_weights, n_data, *refs):
+    planes_in, first, normal, coil_planes, mask = refs[:5]
+    tables, at = refs[5:9], 9
     weights, at = refs[at : at + n_weights], at + n_weights
-    senses, at = refs[at : at + n_sens], at + n_sens
-    more, at = refs[at : at + n_more], at + n_more
     datas, at = refs[at : at + n_data], at + n_data
     out = refs[at]
     scratch = refs[at + 1 : -8]
-    refined, planes, gradient, coil_planes, rows_z, rows_y, stage, all_weights = refs[-8:]
+    refined, planes, data, gradient, rows_y, rows_z, stage, all_weights = refs[-8:]
     per, _, height, width = datas[0].shape
     cascades = len(weights)
     cuts = out.shape[0] // cascades
-    slab = lax.axis_index("section") // (lax.axis_size("section") // mask.shape[0])
     fill_ones(scratch[0])
     refined[...] = first[...]
     planes[...] = planes_in[...]
     for k in range(cascades):
         all_weights[k] = weights[k][...]
-    weight_mask = mask[slab].astype(F32)
-    weight_mask = jnp.concatenate([weight_mask] * 2, axis=0)
-
-    def keep(n, rows):
-        stage[n % stage.shape[0]] = rows.astype(F32)
+    for s in range(per):
         for part in range(2):
-            plane = stage.at[n % stage.shape[0]][pl.ds(part, height, stride=2), :]
-            coil_planes[n, part] = plane.astype(BF16)
-
-    run_start = (lax.axis_index("cuts") * by_cut // cuts) * per
-    n = 0
-    for ref in senses:
-        for s in range(per):
-            keep(n, ref[run_start + s])
-            n += 1
-    for ref in more:
-        for q in range(ref.shape[0]):
-            for s in range(per):
-                keep(n, ref[q, s])
-                n += 1
-    coils = n // per
-    unroll = coils <= 8
-
-    def each_coil(step):
-        if unroll:
-            for q in range(coils):
-                step(q)
-        else:
-            lax.fori_loop(0, coils, lambda q, _: step(q), None)
+            data[part, :, s * width : (s + 1) * width] = sum(d[s, part].astype(F32) for d in datas)
+    gradient[...] = data[...] + normal[...]
+    weight_mask = mask_of(place, mask)
 
     def cascade(c, _):
-        def product(q):
-            for s in range(per):
-                lanes = slice(s * width, (s + 1) * width)
-                sr, si = coil_planes[q * per + s, 0].astype(F32), coil_planes[q * per + s, 1].astype(F32)
-                ir, ii = planes[0, :, lanes], planes[1, :, lanes]
-                coil = jnp.concatenate([sr * ir - si * ii, sr * ii + si * ir], axis=1).astype(BF16)
-                w = jnp.dot(coil, forward_z[...], preferred_element_type=F32).astype(BF16)
-                rows_y[q * per + s] = jnp.concatenate([w[:, :width], w[:, width:]], axis=0)
-
-        each_coil(product)
-
-        def line(b, _):
-            w = jnp.dot(forward_y[...], rows_y[b], preferred_element_type=F32)
-            w = (w * weight_mask).astype(BF16)
-            w = jnp.dot(back_y[...], w, preferred_element_type=F32).astype(BF16)
-            rows_z[b] = jnp.concatenate([w[:height], w[height:]], axis=1)
-
-        lax.fori_loop(0, coils * per, line, None, unroll=4)
-        for s in range(per):
-            lanes = slice(s * width, (s + 1) * width)
-            for part in range(2):
-                gradient[part, :, lanes] = sum(d[s, part].astype(F32) for d in datas)
-
-        def gather(q):
-            for s in range(per):
-                lanes = slice(s * width, (s + 1) * width)
-                sr, si = coil_planes[q * per + s, 0].astype(F32), coil_planes[q * per + s, 1].astype(F32)
-                w = jnp.dot(rows_z[q * per + s], back_z[...], preferred_element_type=F32)
-                br, bi = w[:, :width], w[:, width:]
-                gradient[0, :, lanes] -= sr * br + si * bi
-                gradient[1, :, lanes] -= sr * bi - si * br
-
-        each_coil(gather)
         now = all_weights.at[step_to(c, "section")]
         step = sum(now[128 + piece : 129 + piece, 0:1].astype(F32) for piece in range(3))
         for part in range(2):
@@ -313,6 +350,8 @@
             refine_into(
                 [planes[0], planes[1]], all_weights[step_to(c + 1, "section")], scratch, refined, width
             )
+            gradient[...] = data[...]
+            subtract_normal(planes, coil_planes, weight_mask, tables, gradient, rows_y, rows_z)
 
     lax.fori_loop(0, cascades, cascade, None)
 
@@ -340,47 +379,72 @@
         out_specs=(VMEM, VMEM),
         scratch_shapes=[pltpu.VMEM((per, rows, width), F32)]
         + refine_scratch(rows // 2, per, width, weights[0].shape[-1]),
+        compiler_params=kernel_params(),
         interpret=INTERPRET,
     )(*[near(x) for x in [*pieces, *weights]])
 
 
-def run_cascades(planes, first, mask, weights, senses, more, datas, cuts, by_cut):
-    per, _, height, width = datas[0].shape
-    lanes = per * width
-    count = per * (len(senses) + sum(m.shape[0] for m in more))
+def pass_tables(height, width):
     tables = [
         dft_table(width, 1.0),
         dft_table(width, -1.0),
         dft_table(height, 1.0).T.copy(),
         dft_table(height, -1.0).T.copy(),
     ]
-    args = [planes, first, mask] + [jnp.asarray(t) for t in tables]
-    args += list(weights) + list(senses) + list(more) + list(datas)
+    return [near(jnp.asarray(t)) for t in tables]
+
+
+def pass_scratch(count, height, width):
+    return [
+        pltpu.VMEM((count // 2, 2 * height, 2 * width), BF16),
+        pltpu.VMEM((count // 2, 2 * height, 2 * width), BF16),
+    ]
+
+
+def first_normal(place, planes, mask, senses, more):
+    _, height, lanes = planes.shape
+    width = senses[0].shape[-1]
+    count = place.per * (len(senses) + sum(m.shape[0] for m in more))
+    args = [planes, mask] + pass_tables(height, width) + list(senses) + list(more)
     return pl.pallas_call(
-        functools.partial(
-            cascades_kernel, len(weights), len(senses), len(more), len(datas), by_cut
-        ),
+        functools.partial(first_normal_kernel, place, len(senses)),
+        out_shape=[near_out((count, 2, height, width), BF16), near_out((2, height, lanes), F32)],
+        in_specs=[VMEM] * len(args),
+        out_specs=[VMEM] * 2,
+        scratch_shapes=pass_scratch(count, height, width) + [pltpu.VMEM((4, 2 * height, width), F32)],
+        compiler_params=kernel_params(),
+        interpret=INTERPRET,
+    )(*[near(x) for x in args])
+
+
+def run_cascades(place, planes, first, normal, coil_planes, mask, weights, datas, cuts):
+    per, _, height, width = datas[0].shape
+    lanes = per * width
+    count = coil_planes.shape[0]
+    args = [planes, first, normal, coil_planes, mask] + pass_tables(height, width)
+    args += list(weights) + list(datas)
+    return pl.pallas_call(
+        functools.partial(cascades_kernel, place, len(weights), len(datas)),
         out_shape=jax.ShapeDtypeStruct((len(weights) * cuts, per, 2 * height // cuts, width), BF16),
         in_specs=[VMEM] * len(args),
         out_specs=VMEM,
         scratch_shapes=refine_scratch(height, per, width, weights[0].shape[-1])
+        + [pltpu.VMEM((2, height, lanes), F32)] * 4
+        + pass_scratch(count, height, width)
         + [
-            pltpu.VMEM((2, height, lanes), F32),
-            pltpu.VMEM((2, height, lanes), F32),
-            pltpu.VMEM((2, height, lanes), F32),
-            pltpu.VMEM((count, 2, height, width), BF16),
-            pltpu.VMEM((count, height, 2 * width), BF16),
-            pltpu.VMEM((count, 2 * height, width), BF16),
-            pltpu.VMEM((max(per, 4), 2 * height, width), F32),
+            pltpu.VMEM((per, 2 * height, width), F32),
             pltpu.VMEM((len(weights),) + weights[0].shape, BF16),
         ],
+        compiler_params=kernel_params(),
         interpret=INTERPRET,
     )(*[near(x) for x in args])
 
 
-def split_kernel(place, sens, initial, chosen, conv_in, bias, conv_out, step, *refs):
+def split_kernel(place, sens, initial, *refs):
     coils, cuts = lax.axis_size("coil"), lax.axis_size("cuts")
-    sens_out, initial_out, packed, sems = refs[:coils], refs[coils : coils + cuts], refs[-2], refs[-1]
+    small, step, refs = refs[:4], refs[4], refs[5:]
+    sens_out, initial_out, packed = refs[:coils], refs[coils : coils + cuts], refs[coils + cuts]
+    held, sems = refs[coils + cuts + 1 : -1], refs[-1]
     slab, block = place.slab(), place.half_block()
     copies = []
     for k, (_, target, _) in enumerate(own_and_peers("coil")):
@@ -390,27 +454,34 @@
         start = block * place.run + place.cut_block(target) * place.per
         source = initial.at[slab, pl.ds(start, place.per)]
         copies.append(pltpu.make_async_copy(source, initial_out[k], sems.at[coils + k]))
+    for k, (source, target) in enumerate(zip(small, held)):
+        copies.append(pltpu.make_async_copy(source, target, sems.at[coils + cuts + k]))
     for copy in copies:
         copy.start()
-    pack_into(packed, chosen, conv_in, bias, conv_out, step)
-    for copy in copies:
+    for copy in copies[coils + cuts :]:
+        copy.wait()
+    pack_into(packed, *held, step)
+    for copy in copies[: coils + cuts]:
         copy.wait()
 
 
 def split(place, sens, initial, conv_in, bias, conv_out, step):
     coils, cuts = lax.axis_size("coil"), lax.axis_size("cuts")
     chosen = jnp.asarray(selections())
+    small = [chosen, conv_in.T, bias, conv_out]
     outs = [near_out((place.run,) + sens.shape[-2:], BF16)] * coils
     outs += [near_out((place.per,) + initial.shape[-2:], BF16)] * cuts
     outs += [near_out((chosen.shape[0], bias.shape[1]), BF16)]
     made = pl.pallas_call(
         functools.partial(split_kernel, place),
         out_shape=outs,
-        in_specs=[ANY, ANY, VMEM, VMEM, VMEM, VMEM, SMEM],
+        in_specs=[ANY] * 6 + [SMEM],
         out_specs=[VMEM] * len(outs),
-        scratch_shapes=[pltpu.SemaphoreType.DMA((coils + cuts,))],
+        scratch_shapes=[pltpu.VMEM(x.shape, x.dtype) for x in small]
+        + [pltpu.SemaphoreType.DMA((coils + cuts + len(small),))],
+        compiler_params=kernel_params(),
         interpret=INTERPRET,
-    )(sens, initial, chosen, conv_in.T, bias, conv_out, step)
+    )(*[away(x) for x in [sens, initial] + small], step)
     return made[:coils], made[coils:-1], made[-1]
 
 
@@ -430,6 +501,7 @@
         out_shape=outs,
         in_specs=[VMEM] * coils,
         out_specs=[VMEM] * len(outs),
+        compiler_params=kernel_params(),
         interpret=INTERPRET,
     )(*[near(x) for x in senses])
 
@@ -518,8 +590,9 @@
             pltpu.VMEM((4, rows, width), F32),
             pltpu.SemaphoreType.DMA((1 + CHUNKS + coils,)),
         ],
+        compiler_params=kernel_params(),
         interpret=INTERPRET,
-    )(kspace, sens, near(mask), tables[0], near(tables[1]), near(tables[2]))
+    )(away(kspace), away(sens), near(mask), away(tables[0]), near(tables[1]), near(tables[2]))
 
 
 def pair_sum_kernel(n_in, *refs):
@@ -535,6 +608,7 @@
         out_shape=[near_out(terms[0].shape[1:], BF16)] * coils,
         in_specs=[VMEM] * len(terms),
         out_specs=[VMEM] * coils,
+        compiler_params=kernel_params(),
         interpret=INTERPRET,
     )(*[near(t) for t in terms])
 
@@ -587,7 +661,8 @@
     given = for_partners(place, senses)
     more = sent([None] + list(given), "cuts")[1:]
     first, planes = first_refine(image_pieces, weights)
-    out = run_cascades(planes, first, mask, weights, senses, more, datas, cuts, place.by_cut)
+    coil_planes, normal = first_normal(place, planes, mask, senses, more)
+    out = run_cascades(place, planes, first, normal, coil_planes, mask, weights, datas, cuts)
     out = lax.all_to_all(out, ("section", "cuts"), 0, 0, tiled=True)
     out = out.reshape(slabs, place.halves, cuts, place.per, rows, 2, size_z)
     out = out[:, :: place.halves // place.by_half, :: cuts // place.by_cut]

time: 72 us -> 62.7 us (0.87)
  Pallas kernels: 30.5 us -> 21.3 us
  blocking collectives: 10.9 us -> 9.99 us
  waiting for transfers between devices: 14 us -> 14.9 us
    pallas_call x1 -> x2, Pallas kernels: 22.2 us -> 13.6 us  [the longest x1 12.5 us: run_cascades(): pl.pallas_call(functools.partial(cascades_kernel, place, len(weights), le...]
    ppermute x12, waiting for transfers between devices: 14 us -> 14.9 us  [sent(): arrived.append(lax.ppermute(pieces[k + 1], axis, route))]
    all_to_all x1, blocking collectives: 10.9 us -> 9.99 us  [body(): out = lax.all_to_all(out, ('section', 'cuts'), 0, 0, tiled=True)]
  transfers between devices with their start and end apart: 12 -> 12, of which waited for: 4 -> 4; matrix products, arithmetic and copies ran while one was open for 0% -> 0% of each run, Pallas kernels for 9% -> 12%
where the time goes in v3:
time: 62.7 us; the launch traced here: 62.5 us
  Pallas kernels  21.3 us (34%)
  waiting for transfers between devices  14.9 us (24%)
  starting transfers between devices  14.7 us (23%)
  blocking collectives  9.99 us (16%)
  between operations  0.85 us (1%)
  local copies, waits for them, and re-layouts  0.75 us (1%)
    ppermute x12, waiting for transfers between devices, sent(): arrived.append(lax.ppermute(pieces[k + 1], axis, route))  14.9 us
    ppermute x12, starting transfers between devices, sent(): arrived.append(lax.ppermute(pieces[k + 1], axis, route))  14.7 us
    pallas_call x1, Pallas kernels, run_cascades(): pl.pallas_call(functools.partial(cascades_kernel, place, len(weights), le...  12.5 us
    all_to_all x1, blocking collectives, body(): out = lax.all_to_all(out, ('section', 'cuts'), 0, 0, tiled=True)  9.99 us
    pallas_call x1, Pallas kernels, first_refine(): pl.pallas_call(functools.partial(first_refine_kernel, len(pieces), len(we...  3.24 us
    pallas_call x1, Pallas kernels, adjoint(): pl.pallas_call(functools.partial(adjoint_kernel, place), out_shape=[near_...  2.92 us
    pallas_call x1, Pallas kernels, split(): pl.pallas_call(functools.partial(split_kernel, place), out_shape=outs, in...  1.47 us
  transfers between devices with their start and end apart: 12, of which 4 were waited for; matrix products, arithmetic and copies ran while one was open for 0% of the time, Pallas kernels for 12%

profile of v3, /device:TPU:0, one launch (start us, length us, event | category | flops | bytes accessed | tf_op | source)
XLA Modules:
  0.0 62.5 jit_solution(3072660263981102282)
XLA Ops:
  0.0 0.0 copy-start
  0.0 0.0 copy-start.2
  0.0 0.0 copy-start.1
  0.7 1.5 %shard_map.190 = (bf16[4,160,128]{2,1,0:T(8,128)(2,1)S(1)}, bf16[4,160,128]{2,1,0:T(8,128)(2,1)S(1)}, bf16[4,160,128]{2,1,0:T(8,128)(2,1)S(1)}, bf16[4,160,128]{...) custom-call(bf16[2,1,32,160,128]{4,3,2,1,0:T(8,128)(2,1)} %bitcast.8, ...), custom_call_target="tpu_custom_call" | custom-call | tf_op jit(solution)/shard_map/pallas_call | solution.py:475
  2.2 3.1 %collective-permute-start.4 = (bf16[4,160,128]{2,1,0:T(8,128)(2,1)S(1)}, bf16[4,160,128]{2,1,0:T(8,128)(2,1)S(1)}, u32[]{:S(2)}, u32[]{:S(2)}) collective-permute-start(bf16[4,160,128]{2,1,0:T(8,128)(2,1)S(1)} %get-tuple-element.28), channel_id=1, source_target_pairs={{0,2},{2,0},{4,6},{6,4},{1,3},{3,1},{5,7},{7,5},{8,10},{10,8},{12,... | collective-permute-start | bytes 491528 | tf_op jit(solution)/shard_map/ppermute | solution.py:639
  5.3 2.6 %collective-permute-start.5 = (bf16[4,160,128]{2,1,0:T(8,128)(2,1)S(1)}, bf16[4,160,128]{2,1,0:T(8,128)(2,1)S(1)}, u32[]{:S(2)}, u32[]{:S(2)}) collective-permute-start(bf16[4,160,128]{2,1,0:T(8,128)(2,1)S(1)} %get-tuple-element.29), channel_id=1, source_target_pairs={{0,4},{2,6},{4,0},{6,2},{1,5},{3,7},{5,1},{7,3},{8,12},{10,14},{12... | collective-permute-start | bytes 491528 | tf_op jit(solution)/shard_map/ppermute | solution.py:639
  7.9 0.0 collective-permute-start.6
  7.9 0.0 copy-done
  7.9 0.0 copy-done.2
  7.9 0.0 copy-done.1
  7.9 0.0 copy-start.3
  7.9 0.0 copy-start.4
  7.9 2.9 %shard_map.194 = (bf16[4,2,2,80,128]{4,3,2,1,0:T(8,128)(2,1)S(1)}, bf16[4,2,2,80,128]{4,3,2,1,0:T(8,128)(2,1)S(1)}) custom-call(bf16[2,1,32,160,128]{4,3,2,1,0:T(8,128)(2,1)} %bitcast.10, bf16[2,1,32,160,128]{4,3,2,1,0:T(8,128)(2,1)} %bitcast.9, s32[2,80,128]{2,1,0:T(8,128)S(1)} %copy-done.1, bf16[2,256,512]{2,1,0:T(8,128)(2,1)} %constant.13.clone.tables_x, ...), custom_call_target="tpu_custom_call" | custom-call | tf_op jit(solution)/shard_map/pallas_call | solution.py:579
  10.9 0.1 collective-permute-start.8
  10.9 1.1 %collective-permute-done.4.refs_1_.refs_5_ = bf16[4,160,128]{2,1,0:T(8,128)(2,1)S(1)} collective-permute-done((bf16[4,160,128]{2,1,0:T(8,128)(2,1)S(1)}, bf16[4,160,128]{2,1,0:T(8,128)(2,1)S(1)}, u32[]{:S(2)}, u32[]{:S(2)}) %collective-permute-start.4) | collective-permute-done | bytes 163872 | tf_op jit(solution)/shard_map/ppermute | solution.py:639
  12.0 8.3 %collective-permute-done.5.refs_2_.refs_6_ = bf16[4,160,128]{2,1,0:T(8,128)(2,1)S(1)} collective-permute-done((bf16[4,160,128]{2,1,0:T(8,128)(2,1)S(1)}, bf16[4,160,128]{2,1,0:T(8,128)(2,1)S(1)}, u32[]{:S(2)}, u32[]{:S(2)}) %collective-permute-start.5) | collective-permute-done | bytes 163872 | tf_op jit(solution)/shard_map/ppermute | solution.py:639
  20.3 0.0 collective-permute-done.6.refs_3_.refs_7_
  20.3 0.1 collective-permute-start.7
  20.4 1.6 %collective-permute-start.1 = (bf16[136,128]{1,0:T(8,128)(2,1)S(1)}, bf16[136,128]{1,0:T(8,128)(2,1)S(1)}, u32[]{:S(2)}, u32[]{:S(2)}) collective-permute-start(bf16[136,128]{1,0:T(8,128)(2,1)S(1)} %get-tuple-element.24.refs_2_.refs_9_), channel_id=1, source_target_pairs={{0,8},{8,0},{16,24},{24,16},{1,9},{9,1},{17,25},{25,17},{2,10},{10... | collective-permute-start | bytes 104456 | tf_op jit(solution)/shard_map/ppermute | solution.py:639
  22.0 1.5 %collective-permute-start.2 = (bf16[136,128]{1,0:T(8,128)(2,1)S(1)}, bf16[136,128]{1,0:T(8,128)(2,1)S(1)}, u32[]{:S(2)}, u32[]{:S(2)}) collective-permute-start(bf16[136,128]{1,0:T(8,128)(2,1)S(1)} %get-tuple-element.24.refs_2_.refs_9_), channel_id=1, source_target_pairs={{0,16},{8,24},{16,0},{24,8},{1,17},{9,25},{17,1},{25,9},{2,18},{10... | collective-permute-start | bytes 104456 | tf_op jit(solution)/shard_map/ppermute | solution.py:639
  23.5 0.0 collective-permute-done.8.refs_1_
  23.5 0.1 shard_map.195
  23.6 2.8 %collective-permute-start.9 = (bf16[2,2,80,128]{3,2,1,0:T(8,128)(2,1)S(1)}, bf16[2,2,80,128]{3,2,1,0:T(8,128)(2,1)S(1)}, u32[]{:S(2)}, u32[]{:S(2)}) collective-permute-start(bf16[2,2,80,128]{3,2,1,0:T(8,128)(2,1)S(1)} %get-tuple-element.36), channel_id=1, source_target_pairs={{0,2},{2,0},{4,6},{6,4},{1,3},{3,1},{5,7},{7,5},{8,10},{10,8},{12,... | collective-permute-start | bytes 245768 | tf_op jit(solution)/shard_map/ppermute | solution.py:639
  26.3 1.1 %collective-permute-start.10 = (bf16[2,2,80,128]{3,2,1,0:T(8,128)(2,1)S(1)}, bf16[2,2,80,128]{3,2,1,0:T(8,128)(2,1)S(1)}, u32[]{:S(2)}, u32[]{:S(2)}) collective-permute-start(bf16[2,2,80,128]{3,2,1,0:T(8,128)(2,1)S(1)} %get-tuple-element.37), channel_id=1, source_target_pairs={{0,4},{2,6},{4,0},{6,2},{1,5},{3,7},{5,1},{7,3},{8,12},{10,14},{12... | collective-permute-start | bytes 245768 | tf_op jit(solution)/shard_map/ppermute | solution.py:639
  27.4 0.0 collective-permute-done.1.refs_3_.refs_10_
  27.4 1.4 %collective-permute-start.11 = (bf16[2,2,80,128]{3,2,1,0:T(8,128)(2,1)S(1)}, bf16[2,2,80,128]{3,2,1,0:T(8,128)(2,1)S(1)}, u32[]{:S(2)}, u32[]{:S(2)}) collective-permute-start(bf16[2,2,80,128]{3,2,1,0:T(8,128)(2,1)S(1)} %get-tuple-element.38), channel_id=1, source_target_pairs={{0,6},{2,4},{4,2},{6,0},{1,7},{3,5},{5,3},{7,1},{8,14},{10,12},{12... | collective-permute-start | bytes 245768 | tf_op jit(solution)/shard_map/ppermute | solution.py:639
  28.8 0.0 collective-permute-done.2.refs_4_.refs_11_
  28.8 0.5 collective-permute-start.3
  29.3 4.4 %collective-permute-done.3.refs_5_.refs_12_ = bf16[136,128]{1,0:T(8,128)(2,1)S(1)} collective-permute-done((bf16[136,128]{1,0:T(8,128)(2,1)S(1)}, bf16[136,128]{1,0:T(8,128)(2,1)S(1)}, u32[]{:S(2)}, u32[]{:S(2)}) %collective-permute-start.3) | collective-permute-done | bytes 34848 | tf_op jit(solution)/shard_map/ppermute | solution.py:639
  33.7 0.0 collective-permute-start
  33.7 1.2 %collective-permute-done.refs_1_ = bf16[2,80,128]{2,1,0:T(8,128)(2,1)S(1)} collective-permute-done((bf16[2,80,128]{2,1,0:T(8,128)(2,1)S(1)}, bf16[2,80,128]{2,1,0:T(8,128)(2,1)S(1)}, u32[]{:S(2)}, u32[]{:S(2)}) %collective-permute-start) | collective-permute-done | bytes 40992 | tf_op jit(solution)/shard_map/ppermute | solution.py:639
  34.9 3.2 %shard_map.191 = (f32[2,80,256]{2,1,0:T(8,128)S(1)}, f32[2,80,256]{2,1,0:T(8,128)S(1)}) custom-call(bf16[2,80,128]{2,1,0:T(8,128)(2,1)S(1)} %get-tuple-element.22.refs_0_, bf16[2,80,128]{2,1,0:T(8,128)(2,1)S(1)} %collective-permute-done.refs_1_, bf16[136,128]{1,0:T(8,128)(2,1)S(1)} %get-tuple-element.24.refs_2_.refs_9_, ...), custom_call_target="tpu_custom_call" | custom-call | tf_op jit(solution)/shard_map/pallas_call | solution.py:375
  38.1 0.0 collective-permute-done.7.refs_8_
  38.1 0.0 copy-done.3
  38.1 0.0 copy-done.4
  38.1 1.1 %shard_map.193 = (bf16[16,2,80,128]{3,2,1,0:T(8,128)(2,1)S(1)}, f32[2,80,256]{2,1,0:T(8,128)S(1)}) custom-call(f32[2,80,256]{2,1,0:T(8,128)S(1)} %get-tuple-element.25.planes.refs_0_, s32[2,80,128]{2,1,0:T(8,128)S(1)} %copy-done.1, bf16[256,256]{1,0:T(8,128)(2,1)S(1)} %copy-done.3, bf16[256,256]{1,0:T(8,128)(2,1)S(1)} %copy-done, ...), custom_call_target="tpu_custom_call" | custom-call | tf_op jit(solution)/shard_map/pallas_call | solution.py:409
  39.3 0.0 collective-permute-done.9.refs_14_
  39.3 0.0 collective-permute-done.10.refs_15_
  39.3 0.0 collective-permute-done.11.refs_16_
  39.3 12.5 %shard_map.196 = bf16[8,2,80,128]{3,2,1,0:T(8,128)(2,1)S(1)} custom-call(f32[2,80,256]{2,1,0:T(8,128)S(1)} %get-tuple-element.25.planes.refs_0_, f32[2,80,256]{2,1,0:T(8,128)S(1)} %get-tuple-element.26.refs_1_, f32[2,80,256]{2,1,0:T(8,128)S(1)} %get-tuple-element.31.refs_2_, bf16[16,2,80,128]{3,2,1,0:T(8,128)(2,1)S(1)} %get-tuple-element.32.refs_3_, ...), custom_call_target="tpu_custom_call" | custom-call | tf_op jit(solution)/shard_map/pallas_call | solution.py:426
  51.8 10.0 %all_to_all.5 = bf16[8,2,80,128]{3,2,1,0:T(8,128)(2,1)S(1)} all-to-all(bf16[8,2,80,128]{3,2,1,0:T(8,128)(2,1)S(1)} %shard_map.196), channel_id=1, replica_groups=mesh['section'=4,'coil'=4,'cuts'=2] {'section','cuts'}, dimensions={0} | all-to-all | bytes 655360 | tf_op jit(solution)/shard_map/all_to_all | solution.py:666
  61.8 0.7 %copy.23 = bf16[1,2,8,40,2,128]{5,4,3,2,1,0:T(2,128)(2,1)} copy(bf16[1,2,8,40,2,128]{5,4,3,2,1,0:T(2,128)(2,1)S(1)} %bitcast.11) | data formatting | bytes 655360
  (1 shorter events, 0.0 us)
Async XLA Ops:
  0.0 7.9 %copy-start = (bf16[256,256]{1,0:T(8,128)(2,1)S(1)}, bf16[256,256]{1,0:T(8,128)(2,1)}, u32[]{:S(2)}) copy-start(bf16[256,256]{1,0:T(8,128)(2,1)} %constant.15.clone.refs_1_.back_z.refs_6_) | copy-start | bytes 393220
  0.0 7.9 %copy-start.2 = (bf16[160,160]{1,0:T(8,128)(2,1)S(1)}, bf16[160,160]{1,0:T(8,128)(2,1)}, u32[]{:S(2)}) copy-start(bf16[160,160]{1,0:T(8,128)(2,1)} %constant.14.clone.refs_3_.back_y.refs_8_) | copy-start | bytes 153604
  0.0 7.9 %copy-start.1 = (s32[2,80,128]{2,1,0:T(8,128)S(1)}, s32[2,80,128]{2,1,0:T(8,128)}, u32[]{:S(2)}) copy-start(s32[2,80,128]{2,1,0:T(8,128)} %refs_4_.2) | copy-start | bytes 245764
  2.2 9.8 %collective-permute-start.4 = (bf16[4,160,128]{2,1,0:T(8,128)(2,1)S(1)}, bf16[4,160,128]{2,1,0:T(8,128)(2,1)S(1)}, u32[]{:S(2)}, u32[]{:S(2)}) collective-permute-start(bf16[4,160,128]{2,1,0:T(8,128)(2,1)S(1)} %get-tuple-element.28), channel_id=1, source_target_pairs={{0,2},{2,0},{4,6},{6,4},{1,3},{3,1},{5,7},{7,5},{8,10},{10,8},{12,... | collective-permute-start | bytes 491528 | tf_op jit(solution)/shard_map/ppermute | solution.py:639
  5.3 15.0 %collective-permute-start.5 = (bf16[4,160,128]{2,1,0:T(8,128)(2,1)S(1)}, bf16[4,160,128]{2,1,0:T(8,128)(2,1)S(1)}, u32[]{:S(2)}, u32[]{:S(2)}) collective-permute-start(bf16[4,160,128]{2,1,0:T(8,128)(2,1)S(1)} %get-tuple-element.29), channel_id=1, source_target_pairs={{0,4},{2,6},{4,0},{6,2},{1,5},{3,7},{5,1},{7,3},{8,12},{10,14},{12... | collective-permute-start | bytes 491528 | tf_op jit(solution)/shard_map/ppermute | solution.py:639
  7.9 12.4 %collective-permute-start.6 = (bf16[4,160,128]{2,1,0:T(8,128)(2,1)S(1)}, bf16[4,160,128]{2,1,0:T(8,128)(2,1)S(1)}, u32[]{:S(2)}, u32[]{:S(2)}) collective-permute-start(bf16[4,160,128]{2,1,0:T(8,128)(2,1)S(1)} %get-tuple-element.30), channel_id=1, source_target_pairs={{0,6},{2,4},{4,2},{6,0},{1,7},{3,5},{5,3},{7,1},{8,14},{10,12},{12... | collective-permute-start | bytes 491528 | tf_op jit(solution)/shard_map/ppermute | solution.py:639
  7.9 30.2 %copy-start.3 = (bf16[256,256]{1,0:T(8,128)(2,1)S(1)}, bf16[256,256]{1,0:T(8,128)(2,1)}, u32[]{:S(2)}) copy-start(bf16[256,256]{1,0:T(8,128)(2,1)} %constant.16.clone.refs_0_.refs_5_) | copy-start | bytes 393220
  7.9 30.2 %copy-start.4 = (bf16[160,160]{1,0:T(8,128)(2,1)S(1)}, bf16[160,160]{1,0:T(8,128)(2,1)}, u32[]{:S(2)}) copy-start(bf16[160,160]{1,0:T(8,128)(2,1)} %constant.17.clone.refs_2_.refs_7_) | copy-start | bytes 153604
  10.9 12.6 %collective-permute-start.8 = (bf16[4,2,2,80,128]{4,3,2,1,0:T(8,128)(2,1)S(1)}, bf16[4,2,2,80,128]{4,3,2,1,0:T(8,128)(2,1)S(1)}, u32[]{:S(2)}, u32[]{:S(2)}) collective-permute-start(bf16[4,2,2,80,128]{4,3,2,1,0:T(8,128)(2,1)S(1)} %get-tuple-element.34), channel_id=1, source_target_pairs={{0,1},{1,0},{2,3},{3,2},{4,5},{5,4},{6,7},{7,6},{8,9},{9,8},{10,11... | collective-permute-start | bytes 983048 | tf_op jit(solution)/shard_map/ppermute | solution.py:639
  20.3 17.8 %collective-permute-start.7 = (bf16[4,2,160,128]{3,2,1,0:T(8,128)(2,1)S(1)}, bf16[4,2,160,128]{3,2,1,0:T(8,128)(2,1)S(1)}, u32[]{:S(2)}, u32[]{:S(2)}) collective-permute-start(bf16[4,2,160,128]{3,2,1,0:T(8,128)(2,1)S(1)} %shard_map.192), channel_id=1, source_target_pairs={{0,1},{1,0},{2,3},{3,2},{4,5},{5,4},{6,7},{7,6},{8,9},{9,8},{10,11... | collective-permute-start | bytes 983048 | tf_op jit(solution)/shard_map/ppermute | solution.py:639
  20.4 7.0 %collective-permute-start.1 = (bf16[136,128]{1,0:T(8,128)(2,1)S(1)}, bf16[136,128]{1,0:T(8,128)(2,1)S(1)}, u32[]{:S(2)}, u32[]{:S(2)}) collective-permute-start(bf16[136,128]{1,0:T(8,128)(2,1)S(1)} %get-tuple-element.24.refs_2_.refs_9_), channel_id=1, source_target_pairs={{0,8},{8,0},{16,24},{24,16},{1,9},{9,1},{17,25},{25,17},{2,10},{10... | collective-permute-start | bytes 104456 | tf_op jit(solution)/shard_map/ppermute | solution.py:639
  22.0 6.9 %collective-permute-start.2 = (bf16[136,128]{1,0:T(8,128)(2,1)S(1)}, bf16[136,128]{1,0:T(8,128)(2,1)S(1)}, u32[]{:S(2)}, u32[]{:S(2)}) collective-permute-start(bf16[136,128]{1,0:T(8,128)(2,1)S(1)} %get-tuple-element.24.refs_2_.refs_9_), channel_id=1, source_target_pairs={{0,16},{8,24},{16,0},{24,8},{1,17},{9,25},{17,1},{25,9},{2,18},{10... | collective-permute-start | bytes 104456 | tf_op jit(solution)/shard_map/ppermute | solution.py:639
  23.6 15.7 %collective-permute-start.9 = (bf16[2,2,80,128]{3,2,1,0:T(8,128)(2,1)S(1)}, bf16[2,2,80,128]{3,2,1,0:T(8,128)(2,1)S(1)}, u32[]{:S(2)}, u32[]{:S(2)}) collective-permute-start(bf16[2,2,80,128]{3,2,1,0:T(8,128)(2,1)S(1)} %get-tuple-element.36), channel_id=1, source_target_pairs={{0,2},{2,0},{4,6},{6,4},{1,3},{3,1},{5,7},{7,5},{8,10},{10,8},{12,... | collective-permute-start | bytes 245768 | tf_op jit(solution)/shard_map/ppermute | solution.py:639
  26.3 13.0 %collective-permute-start.10 = (bf16[2,2,80,128]{3,2,1,0:T(8,128)(2,1)S(1)}, bf16[2,2,80,128]{3,2,1,0:T(8,128)(2,1)S(1)}, u32[]{:S(2)}, u32[]{:S(2)}) collective-permute-start(bf16[2,2,80,128]{3,2,1,0:T(8,128)(2,1)S(1)} %get-tuple-element.37), channel_id=1, source_target_pairs={{0,4},{2,6},{4,0},{6,2},{1,5},{3,7},{5,1},{7,3},{8,12},{10,14},{12... | collective-permute-start | bytes 245768 | tf_op jit(solution)/shard_map/ppermute | solution.py:639
  27.4 11.9 %collective-permute-start.11 = (bf16[2,2,80,128]{3,2,1,0:T(8,128)(2,1)S(1)}, bf16[2,2,80,128]{3,2,1,0:T(8,128)(2,1)S(1)}, u32[]{:S(2)}, u32[]{:S(2)}) collective-permute-start(bf16[2,2,80,128]{3,2,1,0:T(8,128)(2,1)S(1)} %get-tuple-element.38), channel_id=1, source_target_pairs={{0,6},{2,4},{4,2},{6,0},{1,7},{3,5},{5,3},{7,1},{8,14},{10,12},{12... | collective-permute-start | bytes 245768 | tf_op jit(solution)/shard_map/ppermute | solution.py:639
  28.8 4.8 %collective-permute-start.3 = (bf16[136,128]{1,0:T(8,128)(2,1)S(1)}, bf16[136,128]{1,0:T(8,128)(2,1)S(1)}, u32[]{:S(2)}, u32[]{:S(2)}) collective-permute-start(bf16[136,128]{1,0:T(8,128)(2,1)S(1)} %get-tuple-element.24.refs_2_.refs_9_), channel_id=1, source_target_pairs={{0,24},{8,16},{16,8},{24,0},{1,25},{9,17},{17,9},{25,1},{2,26},{10... | collective-permute-start | bytes 104456 | tf_op jit(solution)/shard_map/ppermute | solution.py:639
  33.7 1.2 %collective-permute-start = (bf16[2,80,128]{2,1,0:T(8,128)(2,1)S(1)}, bf16[2,80,128]{2,1,0:T(8,128)(2,1)S(1)}, u32[]{:S(2)}, u32[]{:S(2)}) collective-permute-start(bf16[2,80,128]{2,1,0:T(8,128)(2,1)S(1)} %get-tuple-element.23), channel_id=1, source_target_pairs={{0,1},{1,0},{2,3},{3,2},{4,5},{5,4},{6,7},{7,6},{8,9},{9,8},{10,11... | collective-permute-start | bytes 122888 | tf_op jit(solution)/shard_map/ppermute | solution.py:639

commit v4 on v3

--- a/solution.py
+++ b/solution.py
@@ -163,20 +163,14 @@
         activate(0, g)
         before(1, 1, g)
 
-    def two(i, carry):
-        for j, slot in ((2 * i + 1, 1), (2 * i + 2, 0)):
-            for g in range(GROUP):
-                carry = after(j - 1, 1 - slot, g, carry)
-                activate(slot, g)
-                before(j + 1, 1 - slot, g)
-        return carry
-
-    carry = lax.fori_loop(0, (blocks - 2) // 2, two, jnp.zeros((2 * TILE, lanes), F32))
-    for g in range(GROUP):
-        carry = after(blocks - 2, 0, g, carry)
-        activate(1, g)
-    for g in range(GROUP):
-        carry = after(blocks - 1, 1, g, carry)
+    carry = jnp.zeros((2 * TILE, lanes), F32)
+    for j in range(1, blocks + 1):
+        for g in range(GROUP):
+            carry = after(j - 1, (j - 1) % 2, g, carry)
+            if j < blocks:
+                activate(j % 2, g)
+            if j + 1 < blocks:
+                before(j + 1, (j + 1) % 2, g)
     last = carry
     for s in range(lanes // width):
         own = slice(s * width, (s + 1) * width)
@@ -200,12 +194,12 @@
     pieces, weights = refs[:n_rows], refs[n_rows : n_rows + n_weights]
     refined, planes, stage = refs[n_rows + n_weights : n_rows + n_weights + 3]
     scratch = refs[n_rows + n_weights + 3 :]
-    per, _, width = pieces[0].shape
+    last, (per, _, block, width) = pieces[0].shape[0] - 1, pieces[0].shape[1:]
     fill_ones(scratch[0])
     for k, (_, _, source) in enumerate(own_and_peers("cuts")):
-        block = pieces[k].shape[1]
         for s in range(per):
-            stage.at[s][pl.ds(pl.multiple_of(source * block, 16), block), :] = pieces[k][s].astype(F32)
+            rows = pl.ds(pl.multiple_of(source * block, 16), block)
+            stage.at[s][rows, :] = pieces[k][last, s, 0].astype(F32)
     height = stage.shape[1] // 2
     for s in range(per):
         for part in range(2):
@@ -369,7 +363,7 @@
 
 
 def first_refine(pieces, weights):
-    per, block, width = pieces[0].shape
+    per, _, block, width = pieces[0].shape[1:]
     rows = block * len(pieces)
     plane = near_out((2, rows // 2, per * width), F32)
     return pl.pallas_call(
@@ -440,49 +434,30 @@
     )(*[near(x) for x in args])
 
 
-def split_kernel(place, sens, initial, *refs):
-    coils, cuts = lax.axis_size("coil"), lax.axis_size("cuts")
-    small, step, refs = refs[:4], refs[4], refs[5:]
-    sens_out, initial_out, packed = refs[:coils], refs[coils : coils + cuts], refs[coils + cuts]
-    held, sems = refs[coils + cuts + 1 : -1], refs[-1]
-    slab, block = place.slab(), place.half_block()
+def split_kernel(place, sens, *refs):
+    outs, sems = refs[:-1], refs[-1]
+    start = place.half_block() * place.run
     copies = []
     for k, (_, target, _) in enumerate(own_and_peers("coil")):
-        source = sens.at[slab, 0, pl.ds(target * place.owned + block * place.run, place.run)]
-        copies.append(pltpu.make_async_copy(source, sens_out[k], sems.at[k]))
-    for k, (_, target, _) in enumerate(own_and_peers("cuts")):
-        start = block * place.run + place.cut_block(target) * place.per
-        source = initial.at[slab, pl.ds(start, place.per)]
-        copies.append(pltpu.make_async_copy(source, initial_out[k], sems.at[coils + k]))
-    for k, (source, target) in enumerate(zip(small, held)):
-        copies.append(pltpu.make_async_copy(source, target, sems.at[coils + cuts + k]))
+        source = sens.at[place.slab(), 0, pl.ds(target * place.owned + start, place.run)]
+        copies.append(pltpu.make_async_copy(source, outs[k], sems.at[k]))
     for copy in copies:
         copy.start()
-    for copy in copies[coils + cuts :]:
+    for copy in copies:
         copy.wait()
-    pack_into(packed, *held, step)
-    for copy in copies[: coils + cuts]:
-        copy.wait()
-
-
-def split(place, sens, initial, conv_in, bias, conv_out, step):
-    coils, cuts = lax.axis_size("coil"), lax.axis_size("cuts")
-    chosen = jnp.asarray(selections())
-    small = [chosen, conv_in.T, bias, conv_out]
-    outs = [near_out((place.run,) + sens.shape[-2:], BF16)] * coils
-    outs += [near_out((place.per,) + initial.shape[-2:], BF16)] * cuts
-    outs += [near_out((chosen.shape[0], bias.shape[1]), BF16)]
-    made = pl.pallas_call(
+
+
+def split(place, sens):
+    coils = lax.axis_size("coil")
+    return pl.pallas_call(
         functools.partial(split_kernel, place),
-        out_shape=outs,
-        in_specs=[ANY] * 6 + [SMEM],
-        out_specs=[VMEM] * len(outs),
-        scratch_shapes=[pltpu.VMEM(x.shape, x.dtype) for x in small]
-        + [pltpu.SemaphoreType.DMA((coils + cuts + len(small),))],
+        out_shape=[near_out((place.run,) + sens.shape[-2:], BF16)] * coils,
+        in_specs=[ANY],
+        out_specs=[VMEM] * coils,
+        scratch_shapes=[pltpu.SemaphoreType.DMA((coils,))],
         compiler_params=kernel_params(),
         interpret=INTERPRET,
-    )(*[away(x) for x in [sens, initial] + small], step)
-    return made[:coils], made[coils:-1], made[-1]
+    )(away(sens))
 
 
 def partners_kernel(place, *refs):
@@ -509,15 +484,22 @@
 CHUNKS = 4
 
 
-def adjoint_kernel(place, kspace, sens, mask, tables_x, back_y, back_z, *refs):
+def adjoint_kernel(place, n_small, kspace, sens, initial, mask, tables_x, back_y, back_z, *refs):
     coils, cuts = lax.axis_size("coil"), lax.axis_size("cuts")
-    outs = refs[:cuts]
-    data, own_sens, table_x, planes, rows_z, stage, sems = refs[cuts:]
+    small, step, refs = refs[:n_small], refs[n_small], refs[n_small + 1 :]
+    outs, packed, refs = refs[:cuts], refs[cuts], refs[cuts + 1 :]
+    held, refs = refs[:n_small], refs[n_small:]
+    data, own_sens, table_x, planes, rows_z, stage, sems = refs
     size_x, rows, width = data.shape
     height = rows // 2
     kept = coils * place.run
     slab, block = place.slab(), place.half_block()
     chunk = size_x // CHUNKS
+    first_small = 1 + CHUNKS + coils + cuts * place.per
+    packing = [
+        pltpu.make_async_copy(source, target, sems.at[first_small + k])
+        for k, (source, target) in enumerate(zip(small, held))
+    ]
     copies = [pltpu.make_async_copy(tables_x.at[block], table_x, sems.at[0])]
     for i in range(CHUNKS):
         at = pl.ds(i * chunk, chunk)
@@ -527,8 +509,16 @@
         source = sens.at[slab, 0, pl.ds(q * place.owned + block * place.run, place.run)]
         target = own_sens.at[pl.ds(q * place.run, place.run)]
         copies.append(pltpu.make_async_copy(source, target, sems.at[first_sens + q]))
-    for copy in copies:
+    for k, (_, target, _) in enumerate(own_and_peers("cuts")):
+        for s in range(place.per):
+            n = block * place.run + place.cut_block(target) * place.per + s
+            sem = sems.at[first_sens + coils + k * place.per + s]
+            copies.append(pltpu.make_async_copy(initial.at[slab, n], outs[k].at[coils, s, 0], sem))
+    for copy in packing + copies:
         copy.start()
+    for copy in packing:
+        copy.wait()
+    pack_into(packed, *held, step)
     for copy in copies[:first_sens]:
         copy.wait()
     weight_mask = mask[slab].astype(F32)
@@ -555,6 +545,7 @@
     for copy in copies[first_sens:]:
         copy.wait()
     for k, (_, target, _) in enumerate(own_and_peers("cuts")):
+        outs[k][coils, :, 1] = jnp.zeros((place.per, height, width), BF16)
         for q in range(coils):
             for s in range(place.per):
                 n = q * place.run + place.cut_block(target) * place.per + s
@@ -567,50 +558,75 @@
                 outs[k][q, s, 1] = (sr * bi - si * br).astype(BF16)
 
 
-def adjoint(place, kspace, sens, mask):
+def adjoint(place, kspace, sens, initial, mask, conv_in, bias, conv_out, step):
     coils, cuts = lax.axis_size("coil"), lax.axis_size("cuts")
     size_x, rows, width = kspace.shape[-3:]
     height = rows // 2
     kept = coils * place.run
+    assert initial.shape[-2] == height
+    chosen = jnp.asarray(selections())
+    small = [chosen, conv_in.T, bias, conv_out]
     table = dft_table(size_x, -1.0).reshape(2, size_x, 2, coils, place.by_half, place.run)
     table = np.einsum("cxdqbr,uv->bqrduxvc", table.astype(np.float32), np.eye(TILE, dtype=np.float32))
     table = table.reshape(place.by_half, 2 * kept * TILE, 2 * size_x * TILE).astype(ml_dtypes.bfloat16)
     tables = [jnp.asarray(t) for t in (table, dft_table(height, -1.0).T.copy(), dft_table(width, -1.0))]
     return pl.pallas_call(
-        functools.partial(adjoint_kernel, place),
-        out_shape=[near_out((coils, place.per, 2, height, width), BF16)] * cuts,
-        in_specs=[ANY, ANY, VMEM, ANY, VMEM, VMEM],
-        out_specs=[VMEM] * cuts,
-        scratch_shapes=[
+        functools.partial(adjoint_kernel, place, len(small)),
+        out_shape=[near_out((coils + 1, place.per, 2, height, width), BF16)] * cuts
+        + [near_out((chosen.shape[0], bias.shape[1]), BF16)],
+        in_specs=[ANY, ANY, ANY, VMEM, ANY, VMEM, VMEM] + [ANY] * len(small) + [SMEM],
+        out_specs=[VMEM] * (cuts + 1),
+        scratch_shapes=[pltpu.VMEM(x.shape, x.dtype) for x in small]
+        + [
             pltpu.VMEM((size_x, rows, width), BF16),
             pltpu.VMEM((kept, rows, width), BF16),
             pltpu.VMEM(table.shape[1:], BF16),
             pltpu.VMEM((2 * kept, height, width), F32),
             pltpu.VMEM((kept, height, 2 * width), BF16),
             pltpu.VMEM((4, rows, width), F32),
-            pltpu.SemaphoreType.DMA((1 + CHUNKS + coils,)),
+            pltpu.SemaphoreType.DMA((1 + CHUNKS + coils + cuts * place.per + len(small),)),
         ],
         compiler_params=kernel_params(),
         interpret=INTERPRET,
-    )(away(kspace), away(sens), near(mask), away(tables[0]), near(tables[1]), near(tables[2]))
-
-
-def pair_sum_kernel(n_in, *refs):
-    terms, outs = refs[:n_in], refs[n_in:]
-    for k, (_, target, _) in enumerate(own_and_peers("coil")):
-        outs[k][...] = sum(t[target].astype(F32) for t in terms).astype(BF16)
-
-
-def pair_sum(terms):
-    coils = lax.axis_size("coil")
+    )(
+        *[away(x) for x in (kspace, sens, initial)],
+        near(mask),
+        away(tables[0]),
+        near(tables[1]),
+        near(tables[2]),
+        *[away(x) for x in small],
+        step,
+    )
+
+
+def halve_kernel(n_in, bit, *refs):
+    terms, (kept, given) = refs[:n_in], refs[n_in:]
+    mine = lax.axis_index("coil") // (1 << bit) % 2
+    for j in range(kept.shape[0]):
+        for out, target in ((kept, 2 * j + mine), (given, 2 * j + 1 - mine)):
+            out[j] = sum(t[target].astype(F32) for t in terms).astype(BF16)
+
+
+def halve(terms, bit):
+    count = terms[0].shape[0] // 2 * 2
     return pl.pallas_call(
-        functools.partial(pair_sum_kernel, len(terms)),
-        out_shape=[near_out(terms[0].shape[1:], BF16)] * coils,
+        functools.partial(halve_kernel, len(terms), bit),
+        out_shape=[near_out((count // 2,) + terms[0].shape[1:], BF16)] * 2,
         in_specs=[VMEM] * len(terms),
-        out_specs=[VMEM] * coils,
+        out_specs=[VMEM] * 2,
         compiler_params=kernel_params(),
         interpret=INTERPRET,
     )(*[near(t) for t in terms])
+
+
+def sum_over_coils(terms):
+    coils = lax.axis_size("coil")
+    assert coils & (coils - 1) == 0
+    for bit in range(coils.bit_length() - 1):
+        kept, given = halve(terms, bit)
+        route = [(j, j ^ (1 << bit)) for j in range(coils)]
+        terms = [kept, lax.ppermute(given, "coil", route)]
+    return [t[0] for t in terms]
 
 
 class Place:
@@ -650,17 +666,17 @@
         return array.reshape(array.shape[:-3] + (array.shape[-3] * 2, size_z))
 
     initial, sens, kspace = joined(initial), joined(sens), joined(kspace)
-    sens_pieces, image_pieces, packed = split(place, sens, initial, conv_in[0], bias_in, conv_out[0], step_sizes)
+    sens_pieces = split(place, sens)
     senses = sent(sens_pieces, "coil")
+    *terms, packed = adjoint(
+        place, kspace, sens, initial, mask, conv_in[0], bias_in, conv_out[0], step_sizes
+    )
     weights = sent([packed] * sections, "section")
-    image_pieces = sent(image_pieces, "cuts")
-    terms = adjoint(place, kspace, sens, mask)
     terms = sent(terms, "cuts")
-    sums = pair_sum(terms)
-    datas = sent(sums, "coil")
+    datas = sum_over_coils(terms)
     given = for_partners(place, senses)
     more = sent([None] + list(given), "cuts")[1:]
-    first, planes = first_refine(image_pieces, weights)
+    first, planes = first_refine(terms, weights)
     coil_planes, normal = first_normal(place, planes, mask, senses, more)
     out = run_cascades(place, planes, first, normal, coil_planes, mask, weights, datas, cuts)
     out = lax.all_to_all(out, ("section", "cuts"), 0, 0, tiled=True)

time: 62.7 us -> 69 us (1.10)
  waiting for transfers between devices: 14.9 us -> 20.7 us
  Pallas kernels: 21.3 us -> 18 us
  local copies, waits for them, and re-layouts: 0.75 us -> 3.43 us
  starting transfers between devices: 14.7 us -> 15.5 us
    ppermute x0 -> x2, starting transfers between devices: none -> 6.09 us  [sum_over_coils(): terms = [kept, lax.ppermute(given, 'coil', route)]]
    ppermute x12 -> x8, starting transfers between devices: 14.7 us -> 9.45 us  [sent(): arrived.append(lax.ppermute(pieces[k + 1], axis, route))]
    ppermute x0 -> x2, waiting for transfers between devices: none -> 4.84 us  [sum_over_coils(): terms = [kept, lax.ppermute(given, 'coil', route)]]
    unnamed x11 -> x17, local copies, waits for them, and re-layouts: 0.75 us -> 3.43 us
    pallas_call x1, Pallas kernels: 12.5 us -> 9.99 us  [run_cascades(): pl.pallas_call(functools.partial(cascades_kernel, place, len(weights), le...]
    ppermute x12 -> x8, waiting for transfers between devices: 14.9 us -> 15.9 us  [sent(): arrived.append(lax.ppermute(pieces[k + 1], axis, route))]
    pallas_call x1, Pallas kernels: 3.24 us -> 2.52 us  [first_refine(): pl.pallas_call(functools.partial(first_refine_kernel, len(pieces), len(we...]
    pallas_call x3 -> x4, Pallas kernels: 4.47 us -> 4.36 us  [the longest x1 3.05 us: adjoint(): pl.pallas_call(functools.partial(adjoint_kernel, place, len(small)), out_...]
  transfers between devices with their start and end apart: 12 -> 10, of which waited for: 4 -> 6; matrix products, arithmetic and copies ran while one was open for 0% -> 0% of each run, Pallas kernels for 12% -> 7%
where the time goes in v4:
time: 69 us; the launch traced here: 68.7 us
  waiting for transfers between devices  20.7 us (30%)
  Pallas kernels  18 us (26%)
  starting transfers between devices  15.5 us (22%)
  blocking collectives  10.2 us (15%)
  local copies, waits for them, and re-layouts  3.43 us (5%)
  between operations  0.83 us (1%)
    ppermute x8, waiting for transfers between devices, sent(): arrived.append(lax.ppermute(pieces[k + 1], axis, route))  15.9 us
    all_to_all x1, blocking collectives, body(): out = lax.all_to_all(out, ('section', 'cuts'), 0, 0, tiled=True)  10.2 us
    pallas_call x1, Pallas kernels, run_cascades(): pl.pallas_call(functools.partial(cascades_kernel, place, len(weights), le...  9.99 us
    ppermute x8, starting transfers between devices, sent(): arrived.append(lax.ppermute(pieces[k + 1], axis, route))  9.45 us
    ppermute x2, starting transfers between devices, sum_over_coils(): terms = [kept, lax.ppermute(given, 'coil', route)]  6.09 us
    ppermute x2, waiting for transfers between devices, sum_over_coils(): terms = [kept, lax.ppermute(given, 'coil', route)]  4.84 us
    unnamed x17, local copies, waits for them, and re-layouts  3.43 us
    pallas_call x1, Pallas kernels, adjoint(): pl.pallas_call(functools.partial(adjoint_kernel, place, len(small)), out_...  3.05 us
  transfers between devices with their start and end apart: 10, of which 6 were waited for; matrix products, arithmetic and copies ran while one was open for 0% of the time, Pallas kernels for 7%

profile of v4, /device:TPU:0, one launch (start us, length us, event | category | flops | bytes accessed | tf_op | source)
XLA Modules:
  0.0 68.7 jit_solution(17560967868842661501)
XLA Ops:
  0.7 0.0 copy-start
  0.7 0.9 %copy-done = bf16[256,256]{1,0:T(8,128)(2,1)S(1)} copy-done((bf16[256,256]{1,0:T(8,128)(2,1)S(1)}, bf16[256,256]{1,0:T(8,128)(2,1)}, u32[]{:S(2)}) %copy-start) | copy-done | bytes 131096
  1.6 0.0 copy-start.2
  1.6 0.9 %copy-done.2 = s32[2,80,128]{2,1,0:T(8,128)S(1)} copy-done((s32[2,80,128]{2,1,0:T(8,128)S(1)}, s32[2,80,128]{2,1,0:T(8,128)}, u32[]{:S(2)}) %copy-start.2) | copy-done | bytes 81944
  2.4 0.0 copy-start.4
  2.4 0.9 %copy-done.4 = bf16[160,160]{1,0:T(8,128)(2,1)S(1)} copy-done((bf16[160,160]{1,0:T(8,128)(2,1)S(1)}, bf16[160,160]{1,0:T(8,128)(2,1)}, u32[]{:S(2)}) %copy-start.4) | copy-done | bytes 51224
  3.3 3.0 %shard_map.190 = (bf16[5,2,2,80,128]{4,3,2,1,0:T(8,128)(2,1)S(1)}, bf16[5,2,2,80,128]{4,3,2,1,0:T(8,128)(2,1)S(1)}, bf16[136,128]{1,0:T(8,128)(2,1)S(1)}) custom-call(bf16[2,1,32,160,128]{4,3,2,1,0:T(8,128)(2,1)} %bitcast.14, bf16[2,1,32,160,128]{4,3,2,1,0:T(8,128)(2,1)} %bitcast.12, bf16[2,8,80,128]{3,2,1,0:T(8,128)(2,1)} %bitcast.16, ...), custom_call_target="tpu_custom_call" | custom-call | tf_op jit(solution)/shard_map/pallas_call | solution.py:573
  6.4 0.0 copy-start.1
  6.4 0.0 copy-start.3
  6.4 0.0 copy-start.5
  6.4 0.0 copy-start.6
  6.4 0.0 copy-start.7
  6.5 0.6 collective-permute-start
  7.0 1.2 %shard_map.192 = (bf16[4,160,128]{2,1,0:T(8,128)(2,1)S(1)}, bf16[4,160,128]{2,1,0:T(8,128)(2,1)S(1)}, bf16[4,160,128]{2,1,0:T(8,128)(2,1)S(1)}, bf16[4,160,128]{2,1,0:T(8,128)(2,1)S(1)}) custom-call(bf16[2,1,32,160,128]{4,3,2,1,0:T(8,128)(2,1)} %bitcast.13), custom_call_target="tpu_custom_call" | custom-call | tf_op jit(solution)/shard_map/pallas_call | solution.py:452
  8.2 2.7 %collective-permute-start.4 = (bf16[4,160,128]{2,1,0:T(8,128)(2,1)S(1)}, bf16[4,160,128]{2,1,0:T(8,128)(2,1)S(1)}, u32[]{:S(2)}, u32[]{:S(2)}) collective-permute-start(bf16[4,160,128]{2,1,0:T(8,128)(2,1)S(1)} %get-tuple-element.26), channel_id=1, source_target_pairs={{0,2},{2,0},{4,6},{6,4},{1,3},{3,1},{5,7},{7,5},{8,10},{10,8},{12,... | collective-permute-start | bytes 491528 | tf_op jit(solution)/shard_map/ppermute | solution.py:655
  10.9 2.6 %collective-permute-start.5 = (bf16[4,160,128]{2,1,0:T(8,128)(2,1)S(1)}, bf16[4,160,128]{2,1,0:T(8,128)(2,1)S(1)}, u32[]{:S(2)}, u32[]{:S(2)}) collective-permute-start(bf16[4,160,128]{2,1,0:T(8,128)(2,1)S(1)} %get-tuple-element.27), channel_id=1, source_target_pairs={{0,4},{2,6},{4,0},{6,2},{1,5},{3,7},{5,1},{7,3},{8,12},{10,14},{12... | collective-permute-start | bytes 491528 | tf_op jit(solution)/shard_map/ppermute | solution.py:655
  13.5 0.0 collective-permute-start.6
  13.5 5.2 %collective-permute-done.4.refs_1_.refs_5_ = bf16[4,160,128]{2,1,0:T(8,128)(2,1)S(1)} collective-permute-done((bf16[4,160,128]{2,1,0:T(8,128)(2,1)S(1)}, bf16[4,160,128]{2,1,0:T(8,128)(2,1)S(1)}, u32[]{:S(2)}, u32[]{:S(2)}) %collective-permute-start.4) | collective-permute-done | bytes 163872 | tf_op jit(solution)/shard_map/ppermute | solution.py:655
  18.7 7.3 %collective-permute-done.5.refs_2_.refs_6_ = bf16[4,160,128]{2,1,0:T(8,128)(2,1)S(1)} collective-permute-done((bf16[4,160,128]{2,1,0:T(8,128)(2,1)S(1)}, bf16[4,160,128]{2,1,0:T(8,128)(2,1)S(1)}, u32[]{:S(2)}, u32[]{:S(2)}) %collective-permute-start.5) | collective-permute-done | bytes 163872 | tf_op jit(solution)/shard_map/ppermute | solution.py:655
  26.0 0.0 collective-permute-done.6.refs_3_.refs_7_
  26.0 0.1 collective-permute-start.7
  26.1 0.0 collective-permute-done.refs_1_
  26.1 0.1 shard_map.195
  26.2 3.3 %collective-permute-start.8 = (bf16[2,2,2,80,128]{4,3,2,1,0:T(8,128)(2,1)S(1)}, bf16[2,2,2,80,128]{4,3,2,1,0:T(8,128)(2,1)S(1)}, u32[]{:S(2)}, u32[]{:S(2)}) collective-permute-start(bf16[2,2,2,80,128]{4,3,2,1,0:T(8,128)(2,1)S(1)} %get-tuple-element.32), channel_id=1, source_target_pairs={{0,2},{2,0},{4,6},{6,4},{1,3},{3,1},{5,7},{7,5},{8,10},{10,8},{12,... | collective-permute-start | bytes 491528 | tf_op jit(solution)/shard_map/ppermute | solution.py:628
  29.5 4.8 %collective-permute-done.8.refs_1_ = bf16[2,2,2,80,128]{4,3,2,1,0:T(8,128)(2,1)S(1)} collective-permute-done((bf16[2,2,2,80,128]{4,3,2,1,0:T(8,128)(2,1)S(1)}, bf16[2,2,2,80,128]{4,3,2,1,0:T(8,128)(2,1)S(1)}, u32[]{:S(2)}, u32[]{:S(2)}) %collective-permute-start.8) | collective-permute-done | bytes 163872 | tf_op jit(solution)/shard_map/ppermute | solution.py:628
  34.4 2.8 %collective-permute-start.9 = (bf16[1,2,2,80,128]{4,3,2,1,0:T(8,128)(2,1)S(1)}, bf16[1,2,2,80,128]{4,3,2,1,0:T(8,128)(2,1)S(1)}, u32[]{:S(2)}, u32[]{:S(2)}) collective-permute-start(bf16[1,2,2,80,128]{4,3,2,1,0:T(8,128)(2,1)S(1)} %get-tuple-element.34), channel_id=1, source_target_pairs={{0,4},{2,6},{4,0},{6,2},{1,5},{3,7},{5,1},{7,3},{8,12},{10,14},{12... | collective-permute-start | bytes 245768 | tf_op jit(solution)/shard_map/ppermute | solution.py:628
  37.2 2.4 %collective-permute-start.3 = (bf16[136,128]{1,0:T(8,128)(2,1)S(1)}, bf16[136,128]{1,0:T(8,128)(2,1)S(1)}, u32[]{:S(2)}, u32[]{:S(2)}) collective-permute-start(bf16[136,128]{1,0:T(8,128)(2,1)S(1)} %get-tuple-element.22.refs_2_.refs_9_), channel_id=1, source_target_pairs={{0,24},{8,16},{16,8},{24,0},{1,25},{9,17},{17,9},{25,1},{2,26},{10... | collective-permute-start | bytes 104456 | tf_op jit(solution)/shard_map/ppermute | solution.py:655
  39.6 0.5 collective-permute-start.2
  40.1 0.5 collective-permute-start.1
  40.7 1.3 %collective-permute-done.3.refs_5_.refs_12_ = bf16[136,128]{1,0:T(8,128)(2,1)S(1)} collective-permute-done((bf16[136,128]{1,0:T(8,128)(2,1)S(1)}, bf16[136,128]{1,0:T(8,128)(2,1)S(1)}, u32[]{:S(2)}, u32[]{:S(2)}) %collective-permute-start.3) | collective-permute-done | bytes 34848 | tf_op jit(solution)/shard_map/ppermute | solution.py:655
  42.0 1.5 %collective-permute-done.2.refs_4_.refs_11_ = bf16[136,128]{1,0:T(8,128)(2,1)S(1)} collective-permute-done((bf16[136,128]{1,0:T(8,128)(2,1)S(1)}, bf16[136,128]{1,0:T(8,128)(2,1)S(1)}, u32[]{:S(2)}, u32[]{:S(2)}) %collective-permute-start.2) | collective-permute-done | bytes 34848 | tf_op jit(solution)/shard_map/ppermute | solution.py:655
  43.6 0.5 collective-permute-done.1.refs_3_.refs_10_
  44.1 2.5 %shard_map.191 = (f32[2,80,256]{2,1,0:T(8,128)S(1)}, f32[2,80,256]{2,1,0:T(8,128)S(1)}) custom-call(bf16[5,2,2,80,128]{4,3,2,1,0:T(8,128)(2,1)S(1)} %get-tuple-element.20.refs_0_, bf16[5,2,2,80,128]{4,3,2,1,0:T(8,128)(2,1)S(1)} %collective-permute-done.refs_1_, bf16[136,128]{1,0:T(8,128)(2,1)S(1)} %get-tuple-element.22.refs_2_.refs_9_, ...), custom_call_target="tpu_custom_call" | custom-call | tf_op jit(solution)/shard_map/pallas_call | solution.py:369
  46.6 0.0 collective-permute-done.7.refs_8_
  46.6 0.0 copy-done.1
  46.6 0.0 copy-done.3
  46.6 0.0 copy-done.5
  46.6 0.0 copy-done.6
  46.6 0.0 copy-done.7
  46.7 1.1 %shard_map.194 = (bf16[16,2,80,128]{3,2,1,0:T(8,128)(2,1)S(1)}, f32[2,80,256]{2,1,0:T(8,128)S(1)}) custom-call(f32[2,80,256]{2,1,0:T(8,128)S(1)} %get-tuple-element.23.planes.refs_0_, s32[2,80,128]{2,1,0:T(8,128)S(1)} %copy-done.3, bf16[256,256]{1,0:T(8,128)(2,1)S(1)} %copy-done.6, bf16[256,256]{1,0:T(8,128)(2,1)S(1)} %copy-done.1, ...), custom_call_target="tpu_custom_call" | custom-call | tf_op jit(solution)/shard_map/pallas_call | solution.py:403
  47.8 0.0 collective-permute-done.9
  47.8 10.0 %shard_map.197 = bf16[8,2,80,128]{3,2,1,0:T(8,128)(2,1)S(1)} custom-call(f32[2,80,256]{2,1,0:T(8,128)S(1)} %get-tuple-element.23.planes.refs_0_, f32[2,80,256]{2,1,0:T(8,128)S(1)} %get-tuple-element.24.refs_1_, f32[2,80,256]{2,1,0:T(8,128)S(1)} %get-tuple-element.29.refs_2_, bf16[16,2,80,128]{3,2,1,0:T(8,128)(2,1)S(1)} %get-tuple-element.30.refs_3_, ...), custom_call_target="tpu_custom_call" | custom-call | tf_op jit(solution)/shard_map/pallas_call | solution.py:420
  57.8 10.2 %all_to_all.5 = bf16[8,2,80,128]{3,2,1,0:T(8,128)(2,1)S(1)} all-to-all(bf16[8,2,80,128]{3,2,1,0:T(8,128)(2,1)S(1)} %shard_map.197), channel_id=1, replica_groups=mesh['section'=4,'coil'=4,'cuts'=2] {'section','cuts'}, dimensions={0} | all-to-all | bytes 655360 | tf_op jit(solution)/shard_map/all_to_all | solution.py:682
  68.0 0.7 %copy.23 = bf16[1,2,8,40,2,128]{5,4,3,2,1,0:T(2,128)(2,1)} copy(bf16[1,2,8,40,2,128]{5,4,3,2,1,0:T(2,128)(2,1)S(1)} %bitcast.15) | data formatting | bytes 655360
  (2 shorter events, 0.1 us)
Async XLA Ops:
  0.7 0.9 %copy-start = (bf16[256,256]{1,0:T(8,128)(2,1)S(1)}, bf16[256,256]{1,0:T(8,128)(2,1)}, u32[]{:S(2)}) copy-start(bf16[256,256]{1,0:T(8,128)(2,1)} %constant.15.clone.back_z.refs_1_.refs_6_) | copy-start | bytes 393220
  1.6 0.9 %copy-start.2 = (s32[2,80,128]{2,1,0:T(8,128)S(1)}, s32[2,80,128]{2,1,0:T(8,128)}, u32[]{:S(2)}) copy-start(s32[2,80,128]{2,1,0:T(8,128)} %refs_4_.2) | copy-start | bytes 245764
  2.4 0.9 %copy-start.4 = (bf16[160,160]{1,0:T(8,128)(2,1)S(1)}, bf16[160,160]{1,0:T(8,128)(2,1)}, u32[]{:S(2)}) copy-start(bf16[160,160]{1,0:T(8,128)(2,1)} %constant.14.clone.back_y.refs_3_.refs_8_) | copy-start | bytes 153604
  6.4 40.2 %copy-start.1 = (bf16[256,256]{1,0:T(8,128)(2,1)S(1)}, bf16[256,256]{1,0:T(8,128)(2,1)}, u32[]{:S(2)}) copy-start(bf16[256,256]{1,0:T(8,128)(2,1)} %constant.15.clone.back_z.refs_1_.refs_6_) | copy-start | bytes 393220
  6.4 40.2 %copy-start.3 = (s32[2,80,128]{2,1,0:T(8,128)S(1)}, s32[2,80,128]{2,1,0:T(8,128)}, u32[]{:S(2)}) copy-start(s32[2,80,128]{2,1,0:T(8,128)} %refs_4_.2) | copy-start | bytes 245764
  6.4 40.2 %copy-start.5 = (bf16[160,160]{1,0:T(8,128)(2,1)S(1)}, bf16[160,160]{1,0:T(8,128)(2,1)}, u32[]{:S(2)}) copy-start(bf16[160,160]{1,0:T(8,128)(2,1)} %constant.14.clone.back_y.refs_3_.refs_8_) | copy-start | bytes 153604
  6.4 40.2 %copy-start.6 = (bf16[256,256]{1,0:T(8,128)(2,1)S(1)}, bf16[256,256]{1,0:T(8,128)(2,1)}, u32[]{:S(2)}) copy-start(bf16[256,256]{1,0:T(8,128)(2,1)} %constant.16.clone.refs_0_.refs_5_) | copy-start | bytes 393220
  6.4 40.2 %copy-start.7 = (bf16[160,160]{1,0:T(8,128)(2,1)S(1)}, bf16[160,160]{1,0:T(8,128)(2,1)}, u32[]{:S(2)}) copy-start(bf16[160,160]{1,0:T(8,128)(2,1)} %constant.17.clone.refs_2_.refs_7_) | copy-start | bytes 153604
  6.5 19.6 %collective-permute-start = (bf16[5,2,2,80,128]{4,3,2,1,0:T(8,128)(2,1)S(1)}, bf16[5,2,2,80,128]{4,3,2,1,0:T(8,128)(2,1)S(1)}, u32[]{:S(2)}, u32[]{:S(2)}) collective-permute-start(bf16[5,2,2,80,128]{4,3,2,1,0:T(8,128)(2,1)S(1)} %get-tuple-element.21), channel_id=1, source_target_pairs={{0,1},{1,0},{2,3},{3,2},{4,5},{5,4},{6,7},{7,6},{8,9},{9,8},{10,11... | collective-permute-start | bytes 1228808 | tf_op jit(solution)/shard_map/ppermute | solution.py:655
  8.2 10.5 %collective-permute-start.4 = (bf16[4,160,128]{2,1,0:T(8,128)(2,1)S(1)}, bf16[4,160,128]{2,1,0:T(8,128)(2,1)S(1)}, u32[]{:S(2)}, u32[]{:S(2)}) collective-permute-start(bf16[4,160,128]{2,1,0:T(8,128)(2,1)S(1)} %get-tuple-element.26), channel_id=1, source_target_pairs={{0,2},{2,0},{4,6},{6,4},{1,3},{3,1},{5,7},{7,5},{8,10},{10,8},{12,... | collective-permute-start | bytes 491528 | tf_op jit(solution)/shard_map/ppermute | solution.py:655
  10.9 15.0 %collective-permute-start.5 = (bf16[4,160,128]{2,1,0:T(8,128)(2,1)S(1)}, bf16[4,160,128]{2,1,0:T(8,128)(2,1)S(1)}, u32[]{:S(2)}, u32[]{:S(2)}) collective-permute-start(bf16[4,160,128]{2,1,0:T(8,128)(2,1)S(1)} %get-tuple-element.27), channel_id=1, source_target_pairs={{0,4},{2,6},{4,0},{6,2},{1,5},{3,7},{5,1},{7,3},{8,12},{10,14},{12... | collective-permute-start | bytes 491528 | tf_op jit(solution)/shard_map/ppermute | solution.py:655
  13.5 12.5 %collective-permute-start.6 = (bf16[4,160,128]{2,1,0:T(8,128)(2,1)S(1)}, bf16[4,160,128]{2,1,0:T(8,128)(2,1)S(1)}, u32[]{:S(2)}, u32[]{:S(2)}) collective-permute-start(bf16[4,160,128]{2,1,0:T(8,128)(2,1)S(1)} %get-tuple-element.28), channel_id=1, source_target_pairs={{0,6},{2,4},{4,2},{6,0},{1,7},{3,5},{5,3},{7,1},{8,14},{10,12},{12... | collective-permute-start | bytes 491528 | tf_op jit(solution)/shard_map/ppermute | solution.py:655
  26.0 20.6 %collective-permute-start.7 = (bf16[4,2,160,128]{3,2,1,0:T(8,128)(2,1)S(1)}, bf16[4,2,160,128]{3,2,1,0:T(8,128)(2,1)S(1)}, u32[]{:S(2)}, u32[]{:S(2)}) collective-permute-start(bf16[4,2,160,128]{3,2,1,0:T(8,128)(2,1)S(1)} %shard_map.193), channel_id=1, source_target_pairs={{0,1},{1,0},{2,3},{3,2},{4,5},{5,4},{6,7},{7,6},{8,9},{9,8},{10,11... | collective-permute-start | bytes 983048 | tf_op jit(solution)/shard_map/ppermute | solution.py:655
  26.2 8.1 %collective-permute-start.8 = (bf16[2,2,2,80,128]{4,3,2,1,0:T(8,128)(2,1)S(1)}, bf16[2,2,2,80,128]{4,3,2,1,0:T(8,128)(2,1)S(1)}, u32[]{:S(2)}, u32[]{:S(2)}) collective-permute-start(bf16[2,2,2,80,128]{4,3,2,1,0:T(8,128)(2,1)S(1)} %get-tuple-element.32), channel_id=1, source_target_pairs={{0,2},{2,0},{4,6},{6,4},{1,3},{3,1},{5,7},{7,5},{8,10},{10,8},{12,... | collective-permute-start | bytes 491528 | tf_op jit(solution)/shard_map/ppermute | solution.py:628
  34.4 13.4 %collective-permute-start.9 = (bf16[1,2,2,80,128]{4,3,2,1,0:T(8,128)(2,1)S(1)}, bf16[1,2,2,80,128]{4,3,2,1,0:T(8,128)(2,1)S(1)}, u32[]{:S(2)}, u32[]{:S(2)}) collective-permute-start(bf16[1,2,2,80,128]{4,3,2,1,0:T(8,128)(2,1)S(1)} %get-tuple-element.34), channel_id=1, source_target_pairs={{0,4},{2,6},{4,0},{6,2},{1,5},{3,7},{5,1},{7,3},{8,12},{10,14},{12... | collective-permute-start | bytes 245768 | tf_op jit(solution)/shard_map/ppermute | solution.py:628
  37.2 4.8 %collective-permute-start.3 = (bf16[136,128]{1,0:T(8,128)(2,1)S(1)}, bf16[136,128]{1,0:T(8,128)(2,1)S(1)}, u32[]{:S(2)}, u32[]{:S(2)}) collective-permute-start(bf16[136,128]{1,0:T(8,128)(2,1)S(1)} %get-tuple-element.22.refs_2_.refs_9_), channel_id=1, source_target_pairs={{0,24},{8,16},{16,8},{24,0},{1,25},{9,17},{17,9},{25,1},{2,26},{10... | collective-permute-start | bytes 104456 | tf_op jit(solution)/shard_map/ppermute | solution.py:655
  39.6 3.9 %collective-permute-start.2 = (bf16[136,128]{1,0:T(8,128)(2,1)S(1)}, bf16[136,128]{1,0:T(8,128)(2,1)S(1)}, u32[]{:S(2)}, u32[]{:S(2)}) collective-permute-start(bf16[136,128]{1,0:T(8,128)(2,1)S(1)} %get-tuple-element.22.refs_2_.refs_9_), channel_id=1, source_target_pairs={{0,16},{8,24},{16,0},{24,8},{1,17},{9,25},{17,1},{25,9},{2,18},{10... | collective-permute-start | bytes 104456 | tf_op jit(solution)/shard_map/ppermute | solution.py:655
  40.1 3.9 %collective-permute-start.1 = (bf16[136,128]{1,0:T(8,128)(2,1)S(1)}, bf16[136,128]{1,0:T(8,128)(2,1)S(1)}, u32[]{:S(2)}, u32[]{:S(2)}) collective-permute-start(bf16[136,128]{1,0:T(8,128)(2,1)S(1)} %get-tuple-element.22.refs_2_.refs_9_), channel_id=1, source_target_pairs={{0,8},{8,0},{16,24},{24,16},{1,9},{9,1},{17,25},{25,17},{2,10},{10... | collective-permute-start | bytes 104456 | tf_op jit(solution)/shard_map/ppermute | solution.py:655

commit v5 on v4

--- a/solution.py
+++ b/solution.py
@@ -223,11 +223,7 @@
     pairs = count // 2
 
     def each_pair(step):
-        if pairs <= 8:
-            for m in range(pairs):
-                step(m)
-        else:
-            lax.fori_loop(0, pairs, lambda m, _: step(m), None)
+        lax.fori_loop(0, pairs, lambda m, _: step(m), None)
 
     def sens_and_lanes(m, i):
         n, s = 2 * m + i, i % per
@@ -269,8 +265,9 @@
             gradient[0, :, lanes] -= sr * br + si * bi
             gradient[1, :, lanes] -= sr * bi - si * br
 
-    for stage in (product, forward, back, gather):
-        each_pair(stage)
+    if pairs > 8:
+        return [functools.partial(each_pair, stage) for stage in (product, forward, back, gather)]
+    return [functools.partial(stage, m) for stage in (product, forward, back, gather) for m in range(pairs)]
 
 
 def mask_of(place, mask):
@@ -301,7 +298,8 @@
                 keep(n, ref[q, s])
                 n += 1
     normal[...] = jnp.zeros(normal.shape, F32)
-    subtract_normal(planes, coil_planes, mask_of(place, mask), tables, normal, rows_y, rows_z)
+    for step in subtract_normal(planes, coil_planes, mask_of(place, mask), tables, normal, rows_y, rows_z):
+        step()
 
 
 def cascades_kernel(place, n_weights, n_data, *refs):
@@ -309,12 +307,12 @@
     tables, at = refs[5:9], 9
     weights, at = refs[at : at + n_weights], at + n_weights
     datas, at = refs[at : at + n_data], at + n_data
-    out = refs[at]
-    scratch = refs[at + 1 : -8]
+    cuts = lax.axis_size("cuts")
+    outs = refs[at : at + cuts]
+    scratch = refs[at + cuts : -8]
     refined, planes, data, gradient, rows_y, rows_z, stage, all_weights = refs[-8:]
     per, _, height, width = datas[0].shape
     cascades = len(weights)
-    cuts = out.shape[0] // cascades
     fill_ones(scratch[0])
     refined[...] = first[...]
     planes[...] = planes_in[...]
@@ -335,17 +333,20 @@
             for s in range(per):
                 stage.at[s][pl.ds(part, height, stride=2), :] = new[:, s * width : (s + 1) * width]
         block = 2 * height // cuts
-        for s in range(per):
-            for cut in range(cuts):
-                out[c * cuts + cut, s] = stage[s, cut * block : (cut + 1) * block].astype(BF16)
+        for k, (_, target, _) in enumerate(own_and_peers("cuts")):
+            for s in range(per):
+                rows = stage.at[s][pl.ds(pl.multiple_of(target * block, 16), block), :]
+                outs[k][step_to(c, "section"), s] = rows.astype(BF16)
 
         @pl.when(c + 1 < cascades)
         def _():
-            refine_into(
-                [planes[0], planes[1]], all_weights[step_to(c + 1, "section")], scratch, refined, width
-            )
+            following = all_weights[step_to(c + 1, "section")]
+            refine_into([planes[0], planes[1]], following, scratch, refined, width)
             gradient[...] = data[...]
-            subtract_normal(planes, coil_planes, weight_mask, tables, gradient, rows_y, rows_z)
+            for take in subtract_normal(
+                planes, coil_planes, weight_mask, tables, gradient, rows_y, rows_z
+            ):
+                take()
 
     lax.fori_loop(0, cascades, cascade, None)
 
@@ -419,9 +420,9 @@
     args += list(weights) + list(datas)
     return pl.pallas_call(
         functools.partial(cascades_kernel, place, len(weights), len(datas)),
-        out_shape=jax.ShapeDtypeStruct((len(weights) * cuts, per, 2 * height // cuts, width), BF16),
+        out_shape=[near_out((len(weights), per, 2 * height // cuts, width), BF16)] * cuts,
         in_specs=[VMEM] * len(args),
-        out_specs=VMEM,
+        out_specs=[VMEM] * cuts,
         scratch_shapes=refine_scratch(height, per, width, weights[0].shape[-1])
         + [pltpu.VMEM((2, height, lanes), F32)] * 4
         + pass_scratch(count, height, width)
@@ -629,6 +630,46 @@
     return [t[0] for t in terms]
 
 
+def by_section_kernel(n_in, *refs):
+    images, outs = refs[:n_in], refs[n_in:]
+    for k, (_, _, source) in enumerate(own_and_peers("cuts")):
+        for section, out in enumerate(outs):
+            out[source] = images[k][section]
+
+
+def by_section(images):
+    sections = images[0].shape[0]
+    return pl.pallas_call(
+        functools.partial(by_section_kernel, len(images)),
+        out_shape=[near_out((len(images),) + images[0].shape[1:], BF16)] * sections,
+        in_specs=[VMEM] * len(images),
+        out_specs=[VMEM] * sections,
+        compiler_params=kernel_params(),
+        interpret=INTERPRET,
+    )(*[near(x) for x in images])
+
+
+def arrange_kernel(place, *refs):
+    pieces, out = refs[:-1], refs[-1]
+    for k, (_, _, source) in enumerate(own_and_peers("section")):
+        slab = source // place.halves
+        start = source % place.halves * place.by_half // place.halves * place.run
+        for cut in range(place.cuts):
+            at = start + place.cut_block(cut) * place.per
+            out[slab, pl.ds(at, place.per)] = pieces[k][cut]
+
+
+def arrange(place, pieces):
+    return pl.pallas_call(
+        functools.partial(arrange_kernel, place),
+        out_shape=jax.ShapeDtypeStruct((place.slabs, place.owned) + pieces[0].shape[2:], BF16),
+        in_specs=[VMEM] * len(pieces),
+        out_specs=VMEM,
+        compiler_params=kernel_params(),
+        interpret=INTERPRET,
+    )(*[near(x) for x in pieces])
+
+
 class Place:
     def __init__(self, slabs, size_x):
         sections, coils, cuts = (lax.axis_size(a) for a in ("section", "coil", "cuts"))
@@ -678,10 +719,11 @@
     more = sent([None] + list(given), "cuts")[1:]
     first, planes = first_refine(terms, weights)
     coil_planes, normal = first_normal(place, planes, mask, senses, more)
-    out = run_cascades(place, planes, first, normal, coil_planes, mask, weights, datas, cuts)
-    out = lax.all_to_all(out, ("section", "cuts"), 0, 0, tiled=True)
-    out = out.reshape(slabs, place.halves, cuts, place.per, rows, 2, size_z)
-    out = out[:, :: place.halves // place.by_half, :: cuts // place.by_cut]
+    images = run_cascades(place, planes, first, normal, coil_planes, mask, weights, datas, cuts)
+    images = sent(images, "cuts")
+    pieces = by_section(images)
+    pieces = sent(pieces, "section")
+    out = arrange(place, pieces)
     return out.reshape(1, slabs, place.owned, rows, 2, size_z)
 
 

time: 69 us -> 67.8 us (0.983)
  blocking collectives: 10.2 us -> 0 us
  waiting for transfers between devices: 20.7 us -> 26 us
  starting transfers between devices: 15.5 us -> 19.2 us
  Pallas kernels: 18 us -> 18.8 us
  local copies, waits for them, and re-layouts: 3.43 us -> 2.71 us
    all_to_all x1 -> x0, blocking collectives: 10.2 us -> none  [body(): out = lax.all_to_all(out, ('section', 'cuts'), 0, 0, tiled=True)]
    ppermute x8 -> x12, waiting for transfers between devices: 15.9 us -> 21.1 us  [sent(): arrived.append(lax.ppermute(pieces[k + 1], axis, route))]
    ppermute x8 -> x12, starting transfers between devices: 9.45 us -> 13.1 us  [sent(): arrived.append(lax.ppermute(pieces[k + 1], axis, route))]
    pallas_call x0 -> x2, Pallas kernels: none -> 0.81 us  [the longest x1 0.78 us: arrange(): pl.pallas_call(functools.partial(arrange_kernel, place), out_shape=jax.Sh...]
    unnamed x17 -> x16, local copies, waits for them, and re-layouts: 3.43 us -> 2.71 us
  transfers between devices with their start and end apart: 10 -> 14, of which waited for: 6 -> 10; matrix products, arithmetic and copies ran while one was open for 0% -> 0% of each run, Pallas kernels for 7% -> 7%
where the time goes in v5:
time: 67.8 us; the launch traced here: 67.6 us
  waiting for transfers between devices  26 us (38%)
  starting transfers between devices  19.2 us (28%)
  Pallas kernels  18.8 us (28%)
  local copies, waits for them, and re-layouts  2.71 us (4%)
  between operations  0.85 us (1%)
    ppermute x12, waiting for transfers between devices, sent(): arrived.append(lax.ppermute(pieces[k + 1], axis, route))  21.1 us
    ppermute x12, starting transfers between devices, sent(): arrived.append(lax.ppermute(pieces[k + 1], axis, route))  13.1 us
    pallas_call x1, Pallas kernels, run_cascades(): pl.pallas_call(functools.partial(cascades_kernel, place, len(weights), le...  9.99 us
    ppermute x2, starting transfers between devices, sum_over_coils(): terms = [kept, lax.ppermute(given, 'coil', route)]  6.09 us
    ppermute x2, waiting for transfers between devices, sum_over_coils(): terms = [kept, lax.ppermute(given, 'coil', route)]  4.84 us
    pallas_call x1, Pallas kernels, adjoint(): pl.pallas_call(functools.partial(adjoint_kernel, place, len(small)), out_...  3.05 us
    unnamed x16, local copies, waits for them, and re-layouts  2.71 us
    pallas_call x1, Pallas kernels, first_refine(): pl.pallas_call(functools.partial(first_refine_kernel, len(pieces), len(we...  2.52 us
  transfers between devices with their start and end apart: 14, of which 10 were waited for; matrix products, arithmetic and copies ran while one was open for 0% of the time, Pallas kernels for 7%

profile of v5, /device:TPU:0, one launch (start us, length us, event | category | flops | bytes accessed | tf_op | source)
XLA Modules:
  0.0 67.6 jit_solution(14907138922527990504)
XLA Ops:
  0.7 0.0 copy-start
  0.7 0.9 %copy-done = bf16[256,256]{1,0:T(8,128)(2,1)S(1)} copy-done((bf16[256,256]{1,0:T(8,128)(2,1)S(1)}, bf16[256,256]{1,0:T(8,128)(2,1)}, u32[]{:S(2)}) %copy-start) | copy-done | bytes 131096
  1.6 0.9 %copy-done.2 = s32[2,80,128]{2,1,0:T(8,128)S(1)} copy-done((s32[2,80,128]{2,1,0:T(8,128)S(1)}, s32[2,80,128]{2,1,0:T(8,128)}, u32[]{:S(2)}) %copy-start.2) | copy-done | bytes 81944
  2.4 0.9 %copy-done.4 = bf16[160,160]{1,0:T(8,128)(2,1)S(1)} copy-done((bf16[160,160]{1,0:T(8,128)(2,1)S(1)}, bf16[160,160]{1,0:T(8,128)(2,1)}, u32[]{:S(2)}) %copy-start.4) | copy-done | bytes 51224
  3.3 3.0 %shard_map.190 = (bf16[5,2,2,80,128]{4,3,2,1,0:T(8,128)(2,1)S(1)}, bf16[5,2,2,80,128]{4,3,2,1,0:T(8,128)(2,1)S(1)}, bf16[136,128]{1,0:T(8,128)(2,1)S(1)}) custom-call(bf16[2,1,32,160,128]{4,3,2,1,0:T(8,128)(2,1)} %bitcast.14, bf16[2,1,32,160,128]{4,3,2,1,0:T(8,128)(2,1)} %bitcast.12, bf16[2,8,80,128]{3,2,1,0:T(8,128)(2,1)} %bitcast.15, ...), custom_call_target="tpu_custom_call" | custom-call | tf_op jit(solution)/shard_map/pallas_call | solution.py:574
  6.4 0.0 copy-start.1
  6.4 0.0 copy-start.3
  6.4 0.0 copy-start.5
  6.4 0.0 copy-start.6
  6.4 0.0 copy-start.7
  6.5 0.6 collective-permute-start
  7.0 1.2 %shard_map.192 = (bf16[4,160,128]{2,1,0:T(8,128)(2,1)S(1)}, bf16[4,160,128]{2,1,0:T(8,128)(2,1)S(1)}, bf16[4,160,128]{2,1,0:T(8,128)(2,1)S(1)}, bf16[4,160,128]{2,1,0:T(8,128)(2,1)S(1)}) custom-call(bf16[2,1,32,160,128]{4,3,2,1,0:T(8,128)(2,1)} %bitcast.13), custom_call_target="tpu_custom_call" | custom-call | tf_op jit(solution)/shard_map/pallas_call | solution.py:453
  8.2 2.7 %collective-permute-start.4 = (bf16[4,160,128]{2,1,0:T(8,128)(2,1)S(1)}, bf16[4,160,128]{2,1,0:T(8,128)(2,1)S(1)}, u32[]{:S(2)}, u32[]{:S(2)}) collective-permute-start(bf16[4,160,128]{2,1,0:T(8,128)(2,1)S(1)} %get-tuple-element.32), channel_id=1, source_target_pairs={{0,2},{2,0},{4,6},{6,4},{1,3},{3,1},{5,7},{7,5},{8,10},{10,8},{12,... | collective-permute-start | bytes 491528 | tf_op jit(solution)/shard_map/ppermute | solution.py:696
  10.9 2.6 %collective-permute-start.5 = (bf16[4,160,128]{2,1,0:T(8,128)(2,1)S(1)}, bf16[4,160,128]{2,1,0:T(8,128)(2,1)S(1)}, u32[]{:S(2)}, u32[]{:S(2)}) collective-permute-start(bf16[4,160,128]{2,1,0:T(8,128)(2,1)S(1)} %get-tuple-element.33), channel_id=1, source_target_pairs={{0,4},{2,6},{4,0},{6,2},{1,5},{3,7},{5,1},{7,3},{8,12},{10,14},{12... | collective-permute-start | bytes 491528 | tf_op jit(solution)/shard_map/ppermute | solution.py:696
  13.5 0.0 collective-permute-start.6
  13.5 5.2 %collective-permute-done.4.refs_1_.refs_5_ = bf16[4,160,128]{2,1,0:T(8,128)(2,1)S(1)} collective-permute-done((bf16[4,160,128]{2,1,0:T(8,128)(2,1)S(1)}, bf16[4,160,128]{2,1,0:T(8,128)(2,1)S(1)}, u32[]{:S(2)}, u32[]{:S(2)}) %collective-permute-start.4) | collective-permute-done | bytes 163872 | tf_op jit(solution)/shard_map/ppermute | solution.py:696
  18.7 7.3 %collective-permute-done.5.refs_2_.refs_6_ = bf16[4,160,128]{2,1,0:T(8,128)(2,1)S(1)} collective-permute-done((bf16[4,160,128]{2,1,0:T(8,128)(2,1)S(1)}, bf16[4,160,128]{2,1,0:T(8,128)(2,1)S(1)}, u32[]{:S(2)}, u32[]{:S(2)}) %collective-permute-start.5) | collective-permute-done | bytes 163872 | tf_op jit(solution)/shard_map/ppermute | solution.py:696
  26.0 0.0 collective-permute-done.6.refs_3_.refs_7_
  26.0 0.1 collective-permute-start.7
  26.1 0.0 collective-permute-done.refs_1_
  26.1 0.1 shard_map.195
  26.2 3.3 %collective-permute-start.8 = (bf16[2,2,2,80,128]{4,3,2,1,0:T(8,128)(2,1)S(1)}, bf16[2,2,2,80,128]{4,3,2,1,0:T(8,128)(2,1)S(1)}, u32[]{:S(2)}, u32[]{:S(2)}) collective-permute-start(bf16[2,2,2,80,128]{4,3,2,1,0:T(8,128)(2,1)S(1)} %get-tuple-element.38), channel_id=1, source_target_pairs={{0,2},{2,0},{4,6},{6,4},{1,3},{3,1},{5,7},{7,5},{8,10},{10,8},{12,... | collective-permute-start | bytes 491528 | tf_op jit(solution)/shard_map/ppermute | solution.py:629
  29.5 4.8 %collective-permute-done.8.refs_1_ = bf16[2,2,2,80,128]{4,3,2,1,0:T(8,128)(2,1)S(1)} collective-permute-done((bf16[2,2,2,80,128]{4,3,2,1,0:T(8,128)(2,1)S(1)}, bf16[2,2,2,80,128]{4,3,2,1,0:T(8,128)(2,1)S(1)}, u32[]{:S(2)}, u32[]{:S(2)}) %collective-permute-start.8) | collective-permute-done | bytes 163872 | tf_op jit(solution)/shard_map/ppermute | solution.py:629
  34.4 2.8 %collective-permute-start.9 = (bf16[1,2,2,80,128]{4,3,2,1,0:T(8,128)(2,1)S(1)}, bf16[1,2,2,80,128]{4,3,2,1,0:T(8,128)(2,1)S(1)}, u32[]{:S(2)}, u32[]{:S(2)}) collective-permute-start(bf16[1,2,2,80,128]{4,3,2,1,0:T(8,128)(2,1)S(1)} %get-tuple-element.40), channel_id=1, source_target_pairs={{0,4},{2,6},{4,0},{6,2},{1,5},{3,7},{5,1},{7,3},{8,12},{10,14},{12... | collective-permute-start | bytes 245768 | tf_op jit(solution)/shard_map/ppermute | solution.py:629
  37.2 2.4 %collective-permute-start.3 = (bf16[136,128]{1,0:T(8,128)(2,1)S(1)}, bf16[136,128]{1,0:T(8,128)(2,1)S(1)}, u32[]{:S(2)}, u32[]{:S(2)}) collective-permute-start(bf16[136,128]{1,0:T(8,128)(2,1)S(1)} %get-tuple-element.28.refs_2_.refs_9_), channel_id=1, source_target_pairs={{0,24},{8,16},{16,8},{24,0},{1,25},{9,17},{17,9},{25,1},{2,26},{10... | collective-permute-start | bytes 104456 | tf_op jit(solution)/shard_map/ppermute | solution.py:696
  39.6 0.5 collective-permute-start.2
  40.1 0.5 collective-permute-start.1
  40.7 1.3 %collective-permute-done.3.refs_5_.refs_12_ = bf16[136,128]{1,0:T(8,128)(2,1)S(1)} collective-permute-done((bf16[136,128]{1,0:T(8,128)(2,1)S(1)}, bf16[136,128]{1,0:T(8,128)(2,1)S(1)}, u32[]{:S(2)}, u32[]{:S(2)}) %collective-permute-start.3) | collective-permute-done | bytes 34848 | tf_op jit(solution)/shard_map/ppermute | solution.py:696
  42.0 1.5 %collective-permute-done.2.refs_4_.refs_11_ = bf16[136,128]{1,0:T(8,128)(2,1)S(1)} collective-permute-done((bf16[136,128]{1,0:T(8,128)(2,1)S(1)}, bf16[136,128]{1,0:T(8,128)(2,1)S(1)}, u32[]{:S(2)}, u32[]{:S(2)}) %collective-permute-start.2) | collective-permute-done | bytes 34848 | tf_op jit(solution)/shard_map/ppermute | solution.py:696
  43.6 0.5 collective-permute-done.1.refs_3_.refs_10_
  44.1 2.5 %shard_map.191 = (f32[2,80,256]{2,1,0:T(8,128)S(1)}, f32[2,80,256]{2,1,0:T(8,128)S(1)}) custom-call(bf16[5,2,2,80,128]{4,3,2,1,0:T(8,128)(2,1)S(1)} %get-tuple-element.26.refs_0_, bf16[5,2,2,80,128]{4,3,2,1,0:T(8,128)(2,1)S(1)} %collective-permute-done.refs_1_, bf16[136,128]{1,0:T(8,128)(2,1)S(1)} %get-tuple-element.28.refs_2_.refs_9_, ...), custom_call_target="tpu_custom_call" | custom-call | tf_op jit(solution)/shard_map/pallas_call | solution.py:370
  46.6 0.0 collective-permute-done.7.refs_8_
  46.6 0.0 copy-done.1
  46.6 0.0 copy-done.3
  46.6 0.0 copy-done.5
  46.6 0.0 copy-done.6
  46.7 1.1 %shard_map.194 = (bf16[16,2,80,128]{3,2,1,0:T(8,128)(2,1)S(1)}, f32[2,80,256]{2,1,0:T(8,128)S(1)}) custom-call(f32[2,80,256]{2,1,0:T(8,128)S(1)} %get-tuple-element.29.planes.refs_0_, s32[2,80,128]{2,1,0:T(8,128)S(1)} %copy-done.3, bf16[256,256]{1,0:T(8,128)(2,1)S(1)} %copy-done.6, bf16[256,256]{1,0:T(8,128)(2,1)S(1)} %copy-done.1, ...), custom_call_target="tpu_custom_call" | custom-call | tf_op jit(solution)/shard_map/pallas_call | solution.py:404
  47.8 0.0 collective-permute-done.9
  47.8 10.0 %shard_map.197 = (bf16[4,2,80,128]{3,2,1,0:T(8,128)(2,1)S(1)}, bf16[4,2,80,128]{3,2,1,0:T(8,128)(2,1)S(1)}) custom-call(f32[2,80,256]{2,1,0:T(8,128)S(1)} %get-tuple-element.29.planes.refs_0_, f32[2,80,256]{2,1,0:T(8,128)S(1)} %get-tuple-element.30.refs_1_, f32[2,80,256]{2,1,0:T(8,128)S(1)} %get-tuple-element.35.refs_2_, ...), custom_call_target="tpu_custom_call" | custom-call | tf_op jit(solution)/shard_map/pallas_call | solution.py:421
  57.8 0.1 collective-permute-start.10
  57.9 1.4 %collective-permute-done.10.refs_1_ = bf16[4,2,80,128]{3,2,1,0:T(8,128)(2,1)S(1)} collective-permute-done((bf16[4,2,80,128]{3,2,1,0:T(8,128)(2,1)S(1)}, bf16[4,2,80,128]{3,2,1,0:T(8,128)(2,1)S(1)}, u32[]{:S(2)}, u32[]{:S(2)}) %collective-permute-start.10) | collective-permute-done | bytes 163872 | tf_op jit(solution)/shard_map/ppermute | solution.py:696
  59.3 0.6 collective-permute-start.11
  59.9 1.5 %collective-permute-start.12 = (bf16[2,2,80,128]{3,2,1,0:T(8,128)(2,1)S(1)}, bf16[2,2,80,128]{3,2,1,0:T(8,128)(2,1)S(1)}, u32[]{:S(2)}, u32[]{:S(2)}) collective-permute-start(bf16[2,2,80,128]{3,2,1,0:T(8,128)(2,1)S(1)} %get-tuple-element.45), channel_id=1, source_target_pairs={{0,16},{8,24},{16,0},{24,8},{1,17},{9,25},{17,1},{25,9},{2,18},{10... | collective-permute-start | bytes 245768 | tf_op jit(solution)/shard_map/ppermute | solution.py:696
  61.4 1.4 %collective-permute-start.13 = (bf16[2,2,80,128]{3,2,1,0:T(8,128)(2,1)S(1)}, bf16[2,2,80,128]{3,2,1,0:T(8,128)(2,1)S(1)}, u32[]{:S(2)}, u32[]{:S(2)}) collective-permute-start(bf16[2,2,80,128]{3,2,1,0:T(8,128)(2,1)S(1)} %get-tuple-element.46), channel_id=1, source_target_pairs={{0,24},{8,16},{16,8},{24,0},{1,25},{9,17},{17,9},{25,1},{2,26},{10... | collective-permute-start | bytes 245768 | tf_op jit(solution)/shard_map/ppermute | solution.py:696
  62.9 1.3 %collective-permute-done.11.refs_1_ = bf16[2,2,80,128]{3,2,1,0:T(8,128)(2,1)S(1)} collective-permute-done((bf16[2,2,80,128]{3,2,1,0:T(8,128)(2,1)S(1)}, bf16[2,2,80,128]{3,2,1,0:T(8,128)(2,1)S(1)}, u32[]{:S(2)}, u32[]{:S(2)}) %collective-permute-start.11) | collective-permute-done | bytes 81952 | tf_op jit(solution)/shard_map/ppermute | solution.py:696
  64.2 1.0 %collective-permute-done.12.refs_2_ = bf16[2,2,80,128]{3,2,1,0:T(8,128)(2,1)S(1)} collective-permute-done((bf16[2,2,80,128]{3,2,1,0:T(8,128)(2,1)S(1)}, bf16[2,2,80,128]{3,2,1,0:T(8,128)(2,1)S(1)}, u32[]{:S(2)}, u32[]{:S(2)}) %collective-permute-start.12) | collective-permute-done | bytes 81952 | tf_op jit(solution)/shard_map/ppermute | solution.py:696
  65.2 1.6 %collective-permute-done.13.refs_3_ = bf16[2,2,80,128]{3,2,1,0:T(8,128)(2,1)S(1)} collective-permute-done((bf16[2,2,80,128]{3,2,1,0:T(8,128)(2,1)S(1)}, bf16[2,2,80,128]{3,2,1,0:T(8,128)(2,1)S(1)}, u32[]{:S(2)}, u32[]{:S(2)}) %collective-permute-start.13) | collective-permute-done | bytes 81952 | tf_op jit(solution)/shard_map/ppermute | solution.py:696
  66.8 0.8 %shard_map.199 = bf16[2,8,80,128]{3,2,1,0:T(8,128)(2,1)} custom-call(bf16[2,2,80,128]{3,2,1,0:T(8,128)(2,1)S(1)} %get-tuple-element.43.refs_0_, bf16[2,2,80,128]{3,2,1,0:T(8,128)(2,1)S(1)} %collective-permute-done.11.refs_1_, bf16[2,2,80,128]{3,2,1,0:T(8,128)(2,1)S(1)} %collective-permute-done.12.refs_2_, ...), custom_call_target="tpu_custom_call" | custom-call | tf_op jit(solution)/shard_map/pallas_call | solution.py:663
  (6 shorter events, 0.1 us)
Async XLA Ops:
  0.7 0.9 %copy-start = (bf16[256,256]{1,0:T(8,128)(2,1)S(1)}, bf16[256,256]{1,0:T(8,128)(2,1)}, u32[]{:S(2)}) copy-start(bf16[256,256]{1,0:T(8,128)(2,1)} %constant.15.clone.back_z.refs_1_.refs_6_) | copy-start | bytes 393220
  1.6 0.9 %copy-start.2 = (s32[2,80,128]{2,1,0:T(8,128)S(1)}, s32[2,80,128]{2,1,0:T(8,128)}, u32[]{:S(2)}) copy-start(s32[2,80,128]{2,1,0:T(8,128)} %refs_4_.2) | copy-start | bytes 245764
  2.4 0.9 %copy-start.4 = (bf16[160,160]{1,0:T(8,128)(2,1)S(1)}, bf16[160,160]{1,0:T(8,128)(2,1)}, u32[]{:S(2)}) copy-start(bf16[160,160]{1,0:T(8,128)(2,1)} %constant.14.clone.back_y.refs_3_.refs_8_) | copy-start | bytes 153604
  6.4 40.2 %copy-start.1 = (bf16[256,256]{1,0:T(8,128)(2,1)S(1)}, bf16[256,256]{1,0:T(8,128)(2,1)}, u32[]{:S(2)}) copy-start(bf16[256,256]{1,0:T(8,128)(2,1)} %constant.15.clone.back_z.refs_1_.refs_6_) | copy-start | bytes 393220
  6.4 40.2 %copy-start.3 = (s32[2,80,128]{2,1,0:T(8,128)S(1)}, s32[2,80,128]{2,1,0:T(8,128)}, u32[]{:S(2)}) copy-start(s32[2,80,128]{2,1,0:T(8,128)} %refs_4_.2) | copy-start | bytes 245764
  6.4 40.2 %copy-start.5 = (bf16[160,160]{1,0:T(8,128)(2,1)S(1)}, bf16[160,160]{1,0:T(8,128)(2,1)}, u32[]{:S(2)}) copy-start(bf16[160,160]{1,0:T(8,128)(2,1)} %constant.14.clone.back_y.refs_3_.refs_8_) | copy-start | bytes 153604
  6.4 40.2 %copy-start.6 = (bf16[256,256]{1,0:T(8,128)(2,1)S(1)}, bf16[256,256]{1,0:T(8,128)(2,1)}, u32[]{:S(2)}) copy-start(bf16[256,256]{1,0:T(8,128)(2,1)} %constant.16.clone.refs_0_.refs_5_) | copy-start | bytes 393220
  6.4 40.2 %copy-start.7 = (bf16[160,160]{1,0:T(8,128)(2,1)S(1)}, bf16[160,160]{1,0:T(8,128)(2,1)}, u32[]{:S(2)}) copy-start(bf16[160,160]{1,0:T(8,128)(2,1)} %constant.17.clone.refs_2_.refs_7_) | copy-start | bytes 153604
  6.5 19.6 %collective-permute-start = (bf16[5,2,2,80,128]{4,3,2,1,0:T(8,128)(2,1)S(1)}, bf16[5,2,2,80,128]{4,3,2,1,0:T(8,128)(2,1)S(1)}, u32[]{:S(2)}, u32[]{:S(2)}) collective-permute-start(bf16[5,2,2,80,128]{4,3,2,1,0:T(8,128)(2,1)S(1)} %get-tuple-element.27), channel_id=1, source_target_pairs={{0,1},{1,0},{2,3},{3,2},{4,5},{5,4},{6,7},{7,6},{8,9},{9,8},{10,11... | collective-permute-start | bytes 1228808 | tf_op jit(solution)/shard_map/ppermute | solution.py:696
  8.2 10.5 %collective-permute-start.4 = (bf16[4,160,128]{2,1,0:T(8,128)(2,1)S(1)}, bf16[4,160,128]{2,1,0:T(8,128)(2,1)S(1)}, u32[]{:S(2)}, u32[]{:S(2)}) collective-permute-start(bf16[4,160,128]{2,1,0:T(8,128)(2,1)S(1)} %get-tuple-element.32), channel_id=1, source_target_pairs={{0,2},{2,0},{4,6},{6,4},{1,3},{3,1},{5,7},{7,5},{8,10},{10,8},{12,... | collective-permute-start | bytes 491528 | tf_op jit(solution)/shard_map/ppermute | solution.py:696
  10.9 15.0 %collective-permute-start.5 = (bf16[4,160,128]{2,1,0:T(8,128)(2,1)S(1)}, bf16[4,160,128]{2,1,0:T(8,128)(2,1)S(1)}, u32[]{:S(2)}, u32[]{:S(2)}) collective-permute-start(bf16[4,160,128]{2,1,0:T(8,128)(2,1)S(1)} %get-tuple-element.33), channel_id=1, source_target_pairs={{0,4},{2,6},{4,0},{6,2},{1,5},{3,7},{5,1},{7,3},{8,12},{10,14},{12... | collective-permute-start | bytes 491528 | tf_op jit(solution)/shard_map/ppermute | solution.py:696
  13.5 12.5 %collective-permute-start.6 = (bf16[4,160,128]{2,1,0:T(8,128)(2,1)S(1)}, bf16[4,160,128]{2,1,0:T(8,128)(2,1)S(1)}, u32[]{:S(2)}, u32[]{:S(2)}) collective-permute-start(bf16[4,160,128]{2,1,0:T(8,128)(2,1)S(1)} %get-tuple-element.34), channel_id=1, source_target_pairs={{0,6},{2,4},{4,2},{6,0},{1,7},{3,5},{5,3},{7,1},{8,14},{10,12},{12... | collective-permute-start | bytes 491528 | tf_op jit(solution)/shard_map/ppermute | solution.py:696
  26.0 20.6 %collective-permute-start.7 = (bf16[4,2,160,128]{3,2,1,0:T(8,128)(2,1)S(1)}, bf16[4,2,160,128]{3,2,1,0:T(8,128)(2,1)S(1)}, u32[]{:S(2)}, u32[]{:S(2)}) collective-permute-start(bf16[4,2,160,128]{3,2,1,0:T(8,128)(2,1)S(1)} %shard_map.193), channel_id=1, source_target_pairs={{0,1},{1,0},{2,3},{3,2},{4,5},{5,4},{6,7},{7,6},{8,9},{9,8},{10,11... | collective-permute-start | bytes 983048 | tf_op jit(solution)/shard_map/ppermute | solution.py:696
  26.2 8.1 %collective-permute-start.8 = (bf16[2,2,2,80,128]{4,3,2,1,0:T(8,128)(2,1)S(1)}, bf16[2,2,2,80,128]{4,3,2,1,0:T(8,128)(2,1)S(1)}, u32[]{:S(2)}, u32[]{:S(2)}) collective-permute-start(bf16[2,2,2,80,128]{4,3,2,1,0:T(8,128)(2,1)S(1)} %get-tuple-element.38), channel_id=1, source_target_pairs={{0,2},{2,0},{4,6},{6,4},{1,3},{3,1},{5,7},{7,5},{8,10},{10,8},{12,... | collective-permute-start | bytes 491528 | tf_op jit(solution)/shard_map/ppermute | solution.py:629
  34.4 13.4 %collective-permute-start.9 = (bf16[1,2,2,80,128]{4,3,2,1,0:T(8,128)(2,1)S(1)}, bf16[1,2,2,80,128]{4,3,2,1,0:T(8,128)(2,1)S(1)}, u32[]{:S(2)}, u32[]{:S(2)}) collective-permute-start(bf16[1,2,2,80,128]{4,3,2,1,0:T(8,128)(2,1)S(1)} %get-tuple-element.40), channel_id=1, source_target_pairs={{0,4},{2,6},{4,0},{6,2},{1,5},{3,7},{5,1},{7,3},{8,12},{10,14},{12... | collective-permute-start | bytes 245768 | tf_op jit(solution)/shard_map/ppermute | solution.py:629
  37.2 4.8 %collective-permute-start.3 = (bf16[136,128]{1,0:T(8,128)(2,1)S(1)}, bf16[136,128]{1,0:T(8,128)(2,1)S(1)}, u32[]{:S(2)}, u32[]{:S(2)}) collective-permute-start(bf16[136,128]{1,0:T(8,128)(2,1)S(1)} %get-tuple-element.28.refs_2_.refs_9_), channel_id=1, source_target_pairs={{0,24},{8,16},{16,8},{24,0},{1,25},{9,17},{17,9},{25,1},{2,26},{10... | collective-permute-start | bytes 104456 | tf_op jit(solution)/shard_map/ppermute | solution.py:696
  39.6 3.9 %collective-permute-start.2 = (bf16[136,128]{1,0:T(8,128)(2,1)S(1)}, bf16[136,128]{1,0:T(8,128)(2,1)S(1)}, u32[]{:S(2)}, u32[]{:S(2)}) collective-permute-start(bf16[136,128]{1,0:T(8,128)(2,1)S(1)} %get-tuple-element.28.refs_2_.refs_9_), channel_id=1, source_target_pairs={{0,16},{8,24},{16,0},{24,8},{1,17},{9,25},{17,1},{25,9},{2,18},{10... | collective-permute-start | bytes 104456 | tf_op jit(solution)/shard_map/ppermute | solution.py:696
  40.1 3.9 %collective-permute-start.1 = (bf16[136,128]{1,0:T(8,128)(2,1)S(1)}, bf16[136,128]{1,0:T(8,128)(2,1)S(1)}, u32[]{:S(2)}, u32[]{:S(2)}) collective-permute-start(bf16[136,128]{1,0:T(8,128)(2,1)S(1)} %get-tuple-element.28.refs_2_.refs_9_), channel_id=1, source_target_pairs={{0,8},{8,0},{16,24},{24,16},{1,9},{9,1},{17,25},{25,17},{2,10},{10... | collective-permute-start | bytes 104456 | tf_op jit(solution)/shard_map/ppermute | solution.py:696
  57.8 1.5 %collective-permute-start.10 = (bf16[4,2,80,128]{3,2,1,0:T(8,128)(2,1)S(1)}, bf16[4,2,80,128]{3,2,1,0:T(8,128)(2,1)S(1)}, u32[]{:S(2)}, u32[]{:S(2)}) collective-permute-start(bf16[4,2,80,128]{3,2,1,0:T(8,128)(2,1)S(1)} %get-tuple-element.42), channel_id=1, source_target_pairs={{0,1},{1,0},{2,3},{3,2},{4,5},{5,4},{6,7},{7,6},{8,9},{9,8},{10,11... | collective-permute-start | bytes 491528 | tf_op jit(solution)/shard_map/ppermute | solution.py:696
  59.3 4.9 %collective-permute-start.11 = (bf16[2,2,80,128]{3,2,1,0:T(8,128)(2,1)S(1)}, bf16[2,2,80,128]{3,2,1,0:T(8,128)(2,1)S(1)}, u32[]{:S(2)}, u32[]{:S(2)}) collective-permute-start(bf16[2,2,80,128]{3,2,1,0:T(8,128)(2,1)S(1)} %get-tuple-element.44), channel_id=1, source_target_pairs={{0,8},{8,0},{16,24},{24,16},{1,9},{9,1},{17,25},{25,17},{2,10},{10... | collective-permute-start | bytes 245768 | tf_op jit(solution)/shard_map/ppermute | solution.py:696
  59.9 5.3 %collective-permute-start.12 = (bf16[2,2,80,128]{3,2,1,0:T(8,128)(2,1)S(1)}, bf16[2,2,80,128]{3,2,1,0:T(8,128)(2,1)S(1)}, u32[]{:S(2)}, u32[]{:S(2)}) collective-permute-start(bf16[2,2,80,128]{3,2,1,0:T(8,128)(2,1)S(1)} %get-tuple-element.45), channel_id=1, source_target_pairs={{0,16},{8,24},{16,0},{24,8},{1,17},{9,25},{17,1},{25,9},{2,18},{10... | collective-permute-start | bytes 245768 | tf_op jit(solution)/shard_map/ppermute | solution.py:696
  61.4 5.3 %collective-permute-start.13 = (bf16[2,2,80,128]{3,2,1,0:T(8,128)(2,1)S(1)}, bf16[2,2,80,128]{3,2,1,0:T(8,128)(2,1)S(1)}, u32[]{:S(2)}, u32[]{:S(2)}) collective-permute-start(bf16[2,2,80,128]{3,2,1,0:T(8,128)(2,1)S(1)} %get-tuple-element.46), channel_id=1, source_target_pairs={{0,24},{8,16},{16,8},{24,0},{1,25},{9,17},{17,9},{25,1},{2,26},{10... | collective-permute-start | bytes 245768 | tf_op jit(solution)/shard_map/ppermute | solution.py:696

commit v6 on v5

--- a/solution.py
+++ b/solution.py
@@ -227,7 +227,7 @@
 
     def sens_and_lanes(m, i):
         n, s = 2 * m + i, i % per
-        sens = coil_planes[n, 0].astype(F32), coil_planes[n, 1].astype(F32)
+        sens = coil_planes[n, 0], coil_planes[n, 1]
         return *sens, slice(s * width, (s + 1) * width)
 
     def product(m):
@@ -284,7 +284,7 @@
         slot = stage.at[n % stage.shape[0]]
         slot[...] = rows.astype(F32)
         for part in range(2):
-            coil_planes[n, part] = slot[pl.ds(part, height, stride=2), :].astype(BF16)
+            coil_planes[n, part] = slot[pl.ds(part, height, stride=2), :]
 
     start = place.cut_block(lax.axis_index("cuts")) * place.per
     n = 0
@@ -403,7 +403,7 @@
     args = [planes, mask] + pass_tables(height, width) + list(senses) + list(more)
     return pl.pallas_call(
         functools.partial(first_normal_kernel, place, len(senses)),
-        out_shape=[near_out((count, 2, height, width), BF16), near_out((2, height, lanes), F32)],
+        out_shape=[near_out((count, 2, height, width), F32), near_out((2, height, lanes), F32)],
         in_specs=[VMEM] * len(args),
         out_specs=[VMEM] * 2,
         scratch_shapes=pass_scratch(count, height, width) + [pltpu.VMEM((4, 2 * height, width), F32)],

time: 67.8 us -> 67.6 us (level)
  no operation moved by 1% of the time
where the time goes in v6:
time: 67.6 us; the launch traced here: 67.3 us
  waiting for transfers between devices  26 us (38%)
  starting transfers between devices  19.2 us (28%)
  Pallas kernels  18.6 us (28%)
  local copies, waits for them, and re-layouts  2.71 us (4%)
  between operations  0.85 us (1%)
    ppermute x12, waiting for transfers between devices, sent(): arrived.append(lax.ppermute(pieces[k + 1], axis, route))  21.2 us
    ppermute x12, starting transfers between devices, sent(): arrived.append(lax.ppermute(pieces[k + 1], axis, route))  13.1 us
    pallas_call x1, Pallas kernels, run_cascades(): pl.pallas_call(functools.partial(cascades_kernel, place, len(weights), le...  9.82 us
    ppermute x2, starting transfers between devices, sum_over_coils(): terms = [kept, lax.ppermute(given, 'coil', route)]  6.09 us
    ppermute x2, waiting for transfers between devices, sum_over_coils(): terms = [kept, lax.ppermute(given, 'coil', route)]  4.84 us
    pallas_call x1, Pallas kernels, adjoint(): pl.pallas_call(functools.partial(adjoint_kernel, place, len(small)), out_...  3.05 us
    unnamed x16, local copies, waits for them, and re-layouts  2.71 us
    pallas_call x1, Pallas kernels, first_refine(): pl.pallas_call(functools.partial(first_refine_kernel, len(pieces), len(we...  2.52 us
  transfers between devices with their start and end apart: 14, of which 10 were waited for; matrix products, arithmetic and copies ran while one was open for 0% of the time, Pallas kernels for 7%

profile of v6, /device:TPU:0, one launch (start us, length us, event | category | flops | bytes accessed | tf_op | source)
XLA Modules:
  0.0 67.3 jit_solution(987821961139517520)
XLA Ops:
  0.7 0.0 copy-start
  0.7 0.9 %copy-done = bf16[256,256]{1,0:T(8,128)(2,1)S(1)} copy-done((bf16[256,256]{1,0:T(8,128)(2,1)S(1)}, bf16[256,256]{1,0:T(8,128)(2,1)}, u32[]{:S(2)}) %copy-start) | copy-done | bytes 131096
  1.6 0.9 %copy-done.2 = s32[2,80,128]{2,1,0:T(8,128)S(1)} copy-done((s32[2,80,128]{2,1,0:T(8,128)S(1)}, s32[2,80,128]{2,1,0:T(8,128)}, u32[]{:S(2)}) %copy-start.2) | copy-done | bytes 81944
  2.4 0.9 %copy-done.4 = bf16[160,160]{1,0:T(8,128)(2,1)S(1)} copy-done((bf16[160,160]{1,0:T(8,128)(2,1)S(1)}, bf16[160,160]{1,0:T(8,128)(2,1)}, u32[]{:S(2)}) %copy-start.4) | copy-done | bytes 51224
  3.3 3.0 %shard_map.190 = (bf16[5,2,2,80,128]{4,3,2,1,0:T(8,128)(2,1)S(1)}, bf16[5,2,2,80,128]{4,3,2,1,0:T(8,128)(2,1)S(1)}, bf16[136,128]{1,0:T(8,128)(2,1)S(1)}) custom-call(bf16[2,1,32,160,128]{4,3,2,1,0:T(8,128)(2,1)} %bitcast.14, bf16[2,1,32,160,128]{4,3,2,1,0:T(8,128)(2,1)} %bitcast.12, bf16[2,8,80,128]{3,2,1,0:T(8,128)(2,1)} %bitcast.15, ...), custom_call_target="tpu_custom_call" | custom-call | tf_op jit(solution)/shard_map/pallas_call | solution.py:574
  6.4 0.0 copy-start.1
  6.4 0.0 copy-start.3
  6.4 0.0 copy-start.5
  6.4 0.0 copy-start.6
  6.4 0.0 copy-start.7
  6.5 0.6 collective-permute-start
  7.0 1.2 %shard_map.192 = (bf16[4,160,128]{2,1,0:T(8,128)(2,1)S(1)}, bf16[4,160,128]{2,1,0:T(8,128)(2,1)S(1)}, bf16[4,160,128]{2,1,0:T(8,128)(2,1)S(1)}, bf16[4,160,128]{2,1,0:T(8,128)(2,1)S(1)}) custom-call(bf16[2,1,32,160,128]{4,3,2,1,0:T(8,128)(2,1)} %bitcast.13), custom_call_target="tpu_custom_call" | custom-call | tf_op jit(solution)/shard_map/pallas_call | solution.py:453
  8.2 2.7 %collective-permute-start.4 = (bf16[4,160,128]{2,1,0:T(8,128)(2,1)S(1)}, bf16[4,160,128]{2,1,0:T(8,128)(2,1)S(1)}, u32[]{:S(2)}, u32[]{:S(2)}) collective-permute-start(bf16[4,160,128]{2,1,0:T(8,128)(2,1)S(1)} %get-tuple-element.32), channel_id=1, source_target_pairs={{0,2},{2,0},{4,6},{6,4},{1,3},{3,1},{5,7},{7,5},{8,10},{10,8},{12,... | collective-permute-start | bytes 491528 | tf_op jit(solution)/shard_map/ppermute | solution.py:696
  10.9 2.6 %collective-permute-start.5 = (bf16[4,160,128]{2,1,0:T(8,128)(2,1)S(1)}, bf16[4,160,128]{2,1,0:T(8,128)(2,1)S(1)}, u32[]{:S(2)}, u32[]{:S(2)}) collective-permute-start(bf16[4,160,128]{2,1,0:T(8,128)(2,1)S(1)} %get-tuple-element.33), channel_id=1, source_target_pairs={{0,4},{2,6},{4,0},{6,2},{1,5},{3,7},{5,1},{7,3},{8,12},{10,14},{12... | collective-permute-start | bytes 491528 | tf_op jit(solution)/shard_map/ppermute | solution.py:696
  13.5 0.0 collective-permute-start.6
  13.5 5.2 %collective-permute-done.4.refs_1_.refs_5_ = bf16[4,160,128]{2,1,0:T(8,128)(2,1)S(1)} collective-permute-done((bf16[4,160,128]{2,1,0:T(8,128)(2,1)S(1)}, bf16[4,160,128]{2,1,0:T(8,128)(2,1)S(1)}, u32[]{:S(2)}, u32[]{:S(2)}) %collective-permute-start.4) | collective-permute-done | bytes 163872 | tf_op jit(solution)/shard_map/ppermute | solution.py:696
  18.7 7.3 %collective-permute-done.5.refs_2_.refs_6_ = bf16[4,160,128]{2,1,0:T(8,128)(2,1)S(1)} collective-permute-done((bf16[4,160,128]{2,1,0:T(8,128)(2,1)S(1)}, bf16[4,160,128]{2,1,0:T(8,128)(2,1)S(1)}, u32[]{:S(2)}, u32[]{:S(2)}) %collective-permute-start.5) | collective-permute-done | bytes 163872 | tf_op jit(solution)/shard_map/ppermute | solution.py:696
  26.0 0.0 collective-permute-done.6.refs_3_.refs_7_
  26.0 0.1 collective-permute-start.7
  26.1 0.0 collective-permute-done.refs_1_
  26.1 0.1 shard_map.195
  26.2 3.3 %collective-permute-start.8 = (bf16[2,2,2,80,128]{4,3,2,1,0:T(8,128)(2,1)S(1)}, bf16[2,2,2,80,128]{4,3,2,1,0:T(8,128)(2,1)S(1)}, u32[]{:S(2)}, u32[]{:S(2)}) collective-permute-start(bf16[2,2,2,80,128]{4,3,2,1,0:T(8,128)(2,1)S(1)} %get-tuple-element.38), channel_id=1, source_target_pairs={{0,2},{2,0},{4,6},{6,4},{1,3},{3,1},{5,7},{7,5},{8,10},{10,8},{12,... | collective-permute-start | bytes 491528 | tf_op jit(solution)/shard_map/ppermute | solution.py:629
  29.5 4.8 %collective-permute-done.8.refs_1_ = bf16[2,2,2,80,128]{4,3,2,1,0:T(8,128)(2,1)S(1)} collective-permute-done((bf16[2,2,2,80,128]{4,3,2,1,0:T(8,128)(2,1)S(1)}, bf16[2,2,2,80,128]{4,3,2,1,0:T(8,128)(2,1)S(1)}, u32[]{:S(2)}, u32[]{:S(2)}) %collective-permute-start.8) | collective-permute-done | bytes 163872 | tf_op jit(solution)/shard_map/ppermute | solution.py:629
  34.4 2.8 %collective-permute-start.9 = (bf16[1,2,2,80,128]{4,3,2,1,0:T(8,128)(2,1)S(1)}, bf16[1,2,2,80,128]{4,3,2,1,0:T(8,128)(2,1)S(1)}, u32[]{:S(2)}, u32[]{:S(2)}) collective-permute-start(bf16[1,2,2,80,128]{4,3,2,1,0:T(8,128)(2,1)S(1)} %get-tuple-element.40), channel_id=1, source_target_pairs={{0,4},{2,6},{4,0},{6,2},{1,5},{3,7},{5,1},{7,3},{8,12},{10,14},{12... | collective-permute-start | bytes 245768 | tf_op jit(solution)/shard_map/ppermute | solution.py:629
  37.2 2.4 %collective-permute-start.3 = (bf16[136,128]{1,0:T(8,128)(2,1)S(1)}, bf16[136,128]{1,0:T(8,128)(2,1)S(1)}, u32[]{:S(2)}, u32[]{:S(2)}) collective-permute-start(bf16[136,128]{1,0:T(8,128)(2,1)S(1)} %get-tuple-element.28.refs_2_.refs_9_), channel_id=1, source_target_pairs={{0,24},{8,16},{16,8},{24,0},{1,25},{9,17},{17,9},{25,1},{2,26},{10... | collective-permute-start | bytes 104456 | tf_op jit(solution)/shard_map/ppermute | solution.py:696
  39.6 0.5 collective-permute-start.2
  40.1 0.5 collective-permute-start.1
  40.7 1.3 %collective-permute-done.3.refs_5_.refs_12_ = bf16[136,128]{1,0:T(8,128)(2,1)S(1)} collective-permute-done((bf16[136,128]{1,0:T(8,128)(2,1)S(1)}, bf16[136,128]{1,0:T(8,128)(2,1)S(1)}, u32[]{:S(2)}, u32[]{:S(2)}) %collective-permute-start.3) | collective-permute-done | bytes 34848 | tf_op jit(solution)/shard_map/ppermute | solution.py:696
  42.0 1.5 %collective-permute-done.2.refs_4_.refs_11_ = bf16[136,128]{1,0:T(8,128)(2,1)S(1)} collective-permute-done((bf16[136,128]{1,0:T(8,128)(2,1)S(1)}, bf16[136,128]{1,0:T(8,128)(2,1)S(1)}, u32[]{:S(2)}, u32[]{:S(2)}) %collective-permute-start.2) | collective-permute-done | bytes 34848 | tf_op jit(solution)/shard_map/ppermute | solution.py:696
  43.6 0.5 collective-permute-done.1.refs_3_.refs_10_
  44.1 2.5 %shard_map.191 = (f32[2,80,256]{2,1,0:T(8,128)S(1)}, f32[2,80,256]{2,1,0:T(8,128)S(1)}) custom-call(bf16[5,2,2,80,128]{4,3,2,1,0:T(8,128)(2,1)S(1)} %get-tuple-element.26.refs_0_, bf16[5,2,2,80,128]{4,3,2,1,0:T(8,128)(2,1)S(1)} %collective-permute-done.refs_1_, bf16[136,128]{1,0:T(8,128)(2,1)S(1)} %get-tuple-element.28.refs_2_.refs_9_, ...), custom_call_target="tpu_custom_call" | custom-call | tf_op jit(solution)/shard_map/pallas_call | solution.py:370
  46.6 0.0 collective-permute-done.7.refs_8_
  46.6 0.0 copy-done.1
  46.6 0.0 copy-done.3
  46.6 0.0 copy-done.5
  46.6 0.0 copy-done.6
  46.7 1.1 %shard_map.194 = (f32[16,2,80,128]{3,2,1,0:T(8,128)S(1)}, f32[2,80,256]{2,1,0:T(8,128)S(1)}) custom-call(f32[2,80,256]{2,1,0:T(8,128)S(1)} %get-tuple-element.29.planes.refs_0_, s32[2,80,128]{2,1,0:T(8,128)S(1)} %copy-done.3, bf16[256,256]{1,0:T(8,128)(2,1)S(1)} %copy-done.6, bf16[256,256]{1,0:T(8,128)(2,1)S(1)} %copy-done.1, ...), custom_call_target="tpu_custom_call" | custom-call | tf_op jit(solution)/shard_map/pallas_call | solution.py:404
  47.7 0.0 collective-permute-done.9
  47.7 9.8 %shard_map.197 = (bf16[4,2,80,128]{3,2,1,0:T(8,128)(2,1)S(1)}, bf16[4,2,80,128]{3,2,1,0:T(8,128)(2,1)S(1)}) custom-call(f32[2,80,256]{2,1,0:T(8,128)S(1)} %get-tuple-element.29.planes.refs_0_, f32[2,80,256]{2,1,0:T(8,128)S(1)} %get-tuple-element.30.refs_1_, f32[2,80,256]{2,1,0:T(8,128)S(1)} %get-tuple-element.35.refs_2_, ...), custom_call_target="tpu_custom_call" | custom-call | tf_op jit(solution)/shard_map/pallas_call | solution.py:421
  57.6 0.1 collective-permute-start.10
  57.6 1.4 %collective-permute-done.10.refs_1_ = bf16[4,2,80,128]{3,2,1,0:T(8,128)(2,1)S(1)} collective-permute-done((bf16[4,2,80,128]{3,2,1,0:T(8,128)(2,1)S(1)}, bf16[4,2,80,128]{3,2,1,0:T(8,128)(2,1)S(1)}, u32[]{:S(2)}, u32[]{:S(2)}) %collective-permute-start.10) | collective-permute-done | bytes 163872 | tf_op jit(solution)/shard_map/ppermute | solution.py:696
  59.1 0.6 collective-permute-start.11
  59.7 1.5 %collective-permute-start.12 = (bf16[2,2,80,128]{3,2,1,0:T(8,128)(2,1)S(1)}, bf16[2,2,80,128]{3,2,1,0:T(8,128)(2,1)S(1)}, u32[]{:S(2)}, u32[]{:S(2)}) collective-permute-start(bf16[2,2,80,128]{3,2,1,0:T(8,128)(2,1)S(1)} %get-tuple-element.45), channel_id=1, source_target_pairs={{0,16},{8,24},{16,0},{24,8},{1,17},{9,25},{17,1},{25,9},{2,18},{10... | collective-permute-start | bytes 245768 | tf_op jit(solution)/shard_map/ppermute | solution.py:696
  61.2 1.4 %collective-permute-start.13 = (bf16[2,2,80,128]{3,2,1,0:T(8,128)(2,1)S(1)}, bf16[2,2,80,128]{3,2,1,0:T(8,128)(2,1)S(1)}, u32[]{:S(2)}, u32[]{:S(2)}) collective-permute-start(bf16[2,2,80,128]{3,2,1,0:T(8,128)(2,1)S(1)} %get-tuple-element.46), channel_id=1, source_target_pairs={{0,24},{8,16},{16,8},{24,0},{1,25},{9,17},{17,9},{25,1},{2,26},{10... | collective-permute-start | bytes 245768 | tf_op jit(solution)/shard_map/ppermute | solution.py:696
  62.6 1.3 %collective-permute-done.11.refs_1_ = bf16[2,2,80,128]{3,2,1,0:T(8,128)(2,1)S(1)} collective-permute-done((bf16[2,2,80,128]{3,2,1,0:T(8,128)(2,1)S(1)}, bf16[2,2,80,128]{3,2,1,0:T(8,128)(2,1)S(1)}, u32[]{:S(2)}, u32[]{:S(2)}) %collective-permute-start.11) | collective-permute-done | bytes 81952 | tf_op jit(solution)/shard_map/ppermute | solution.py:696
  63.9 1.0 %collective-permute-done.12.refs_2_ = bf16[2,2,80,128]{3,2,1,0:T(8,128)(2,1)S(1)} collective-permute-done((bf16[2,2,80,128]{3,2,1,0:T(8,128)(2,1)S(1)}, bf16[2,2,80,128]{3,2,1,0:T(8,128)(2,1)S(1)}, u32[]{:S(2)}, u32[]{:S(2)}) %collective-permute-start.12) | collective-permute-done | bytes 81952 | tf_op jit(solution)/shard_map/ppermute | solution.py:696
  64.9 1.6 %collective-permute-done.13.refs_3_ = bf16[2,2,80,128]{3,2,1,0:T(8,128)(2,1)S(1)} collective-permute-done((bf16[2,2,80,128]{3,2,1,0:T(8,128)(2,1)S(1)}, bf16[2,2,80,128]{3,2,1,0:T(8,128)(2,1)S(1)}, u32[]{:S(2)}, u32[]{:S(2)}) %collective-permute-start.13) | collective-permute-done | bytes 81952 | tf_op jit(solution)/shard_map/ppermute | solution.py:696
  66.5 0.8 %shard_map.199 = bf16[2,8,80,128]{3,2,1,0:T(8,128)(2,1)} custom-call(bf16[2,2,80,128]{3,2,1,0:T(8,128)(2,1)S(1)} %get-tuple-element.43.refs_0_, bf16[2,2,80,128]{3,2,1,0:T(8,128)(2,1)S(1)} %collective-permute-done.11.refs_1_, bf16[2,2,80,128]{3,2,1,0:T(8,128)(2,1)S(1)} %collective-permute-done.12.refs_2_, ...), custom_call_target="tpu_custom_call" | custom-call | tf_op jit(solution)/shard_map/pallas_call | solution.py:663
  (6 shorter events, 0.1 us)
Async XLA Ops:
  0.7 0.9 %copy-start = (bf16[256,256]{1,0:T(8,128)(2,1)S(1)}, bf16[256,256]{1,0:T(8,128)(2,1)}, u32[]{:S(2)}) copy-start(bf16[256,256]{1,0:T(8,128)(2,1)} %constant.15.clone.back_z.refs_1_.refs_6_) | copy-start | bytes 393220
  1.6 0.9 %copy-start.2 = (s32[2,80,128]{2,1,0:T(8,128)S(1)}, s32[2,80,128]{2,1,0:T(8,128)}, u32[]{:S(2)}) copy-start(s32[2,80,128]{2,1,0:T(8,128)} %refs_4_.2) | copy-start | bytes 245764
  2.4 0.9 %copy-start.4 = (bf16[160,160]{1,0:T(8,128)(2,1)S(1)}, bf16[160,160]{1,0:T(8,128)(2,1)}, u32[]{:S(2)}) copy-start(bf16[160,160]{1,0:T(8,128)(2,1)} %constant.14.clone.back_y.refs_3_.refs_8_) | copy-start | bytes 153604
  6.4 40.2 %copy-start.1 = (bf16[256,256]{1,0:T(8,128)(2,1)S(1)}, bf16[256,256]{1,0:T(8,128)(2,1)}, u32[]{:S(2)}) copy-start(bf16[256,256]{1,0:T(8,128)(2,1)} %constant.15.clone.back_z.refs_1_.refs_6_) | copy-start | bytes 393220
  6.4 40.2 %copy-start.3 = (s32[2,80,128]{2,1,0:T(8,128)S(1)}, s32[2,80,128]{2,1,0:T(8,128)}, u32[]{:S(2)}) copy-start(s32[2,80,128]{2,1,0:T(8,128)} %refs_4_.2) | copy-start | bytes 245764
  6.4 40.2 %copy-start.5 = (bf16[160,160]{1,0:T(8,128)(2,1)S(1)}, bf16[160,160]{1,0:T(8,128)(2,1)}, u32[]{:S(2)}) copy-start(bf16[160,160]{1,0:T(8,128)(2,1)} %constant.14.clone.back_y.refs_3_.refs_8_) | copy-start | bytes 153604
  6.4 40.2 %copy-start.6 = (bf16[256,256]{1,0:T(8,128)(2,1)S(1)}, bf16[256,256]{1,0:T(8,128)(2,1)}, u32[]{:S(2)}) copy-start(bf16[256,256]{1,0:T(8,128)(2,1)} %constant.16.clone.refs_0_.refs_5_) | copy-start | bytes 393220
  6.4 40.2 %copy-start.7 = (bf16[160,160]{1,0:T(8,128)(2,1)S(1)}, bf16[160,160]{1,0:T(8,128)(2,1)}, u32[]{:S(2)}) copy-start(bf16[160,160]{1,0:T(8,128)(2,1)} %constant.17.clone.refs_2_.refs_7_) | copy-start | bytes 153604
  6.5 19.6 %collective-permute-start = (bf16[5,2,2,80,128]{4,3,2,1,0:T(8,128)(2,1)S(1)}, bf16[5,2,2,80,128]{4,3,2,1,0:T(8,128)(2,1)S(1)}, u32[]{:S(2)}, u32[]{:S(2)}) collective-permute-start(bf16[5,2,2,80,128]{4,3,2,1,0:T(8,128)(2,1)S(1)} %get-tuple-element.27), channel_id=1, source_target_pairs={{0,1},{1,0},{2,3},{3,2},{4,5},{5,4},{6,7},{7,6},{8,9},{9,8},{10,11... | collective-permute-start | bytes 1228808 | tf_op jit(solution)/shard_map/ppermute | solution.py:696
  8.2 10.5 %collective-permute-start.4 = (bf16[4,160,128]{2,1,0:T(8,128)(2,1)S(1)}, bf16[4,160,128]{2,1,0:T(8,128)(2,1)S(1)}, u32[]{:S(2)}, u32[]{:S(2)}) collective-permute-start(bf16[4,160,128]{2,1,0:T(8,128)(2,1)S(1)} %get-tuple-element.32), channel_id=1, source_target_pairs={{0,2},{2,0},{4,6},{6,4},{1,3},{3,1},{5,7},{7,5},{8,10},{10,8},{12,... | collective-permute-start | bytes 491528 | tf_op jit(solution)/shard_map/ppermute | solution.py:696
  10.9 15.0 %collective-permute-start.5 = (bf16[4,160,128]{2,1,0:T(8,128)(2,1)S(1)}, bf16[4,160,128]{2,1,0:T(8,128)(2,1)S(1)}, u32[]{:S(2)}, u32[]{:S(2)}) collective-permute-start(bf16[4,160,128]{2,1,0:T(8,128)(2,1)S(1)} %get-tuple-element.33), channel_id=1, source_target_pairs={{0,4},{2,6},{4,0},{6,2},{1,5},{3,7},{5,1},{7,3},{8,12},{10,14},{12... | collective-permute-start | bytes 491528 | tf_op jit(solution)/shard_map/ppermute | solution.py:696
  13.5 12.5 %collective-permute-start.6 = (bf16[4,160,128]{2,1,0:T(8,128)(2,1)S(1)}, bf16[4,160,128]{2,1,0:T(8,128)(2,1)S(1)}, u32[]{:S(2)}, u32[]{:S(2)}) collective-permute-start(bf16[4,160,128]{2,1,0:T(8,128)(2,1)S(1)} %get-tuple-element.34), channel_id=1, source_target_pairs={{0,6},{2,4},{4,2},{6,0},{1,7},{3,5},{5,3},{7,1},{8,14},{10,12},{12... | collective-permute-start | bytes 491528 | tf_op jit(solution)/shard_map/ppermute | solution.py:696
  26.0 20.6 %collective-permute-start.7 = (bf16[4,2,160,128]{3,2,1,0:T(8,128)(2,1)S(1)}, bf16[4,2,160,128]{3,2,1,0:T(8,128)(2,1)S(1)}, u32[]{:S(2)}, u32[]{:S(2)}) collective-permute-start(bf16[4,2,160,128]{3,2,1,0:T(8,128)(2,1)S(1)} %shard_map.193), channel_id=1, source_target_pairs={{0,1},{1,0},{2,3},{3,2},{4,5},{5,4},{6,7},{7,6},{8,9},{9,8},{10,11... | collective-permute-start | bytes 983048 | tf_op jit(solution)/shard_map/ppermute | solution.py:696
  26.2 8.1 %collective-permute-start.8 = (bf16[2,2,2,80,128]{4,3,2,1,0:T(8,128)(2,1)S(1)}, bf16[2,2,2,80,128]{4,3,2,1,0:T(8,128)(2,1)S(1)}, u32[]{:S(2)}, u32[]{:S(2)}) collective-permute-start(bf16[2,2,2,80,128]{4,3,2,1,0:T(8,128)(2,1)S(1)} %get-tuple-element.38), channel_id=1, source_target_pairs={{0,2},{2,0},{4,6},{6,4},{1,3},{3,1},{5,7},{7,5},{8,10},{10,8},{12,... | collective-permute-start | bytes 491528 | tf_op jit(solution)/shard_map/ppermute | solution.py:629
  34.4 13.4 %collective-permute-start.9 = (bf16[1,2,2,80,128]{4,3,2,1,0:T(8,128)(2,1)S(1)}, bf16[1,2,2,80,128]{4,3,2,1,0:T(8,128)(2,1)S(1)}, u32[]{:S(2)}, u32[]{:S(2)}) collective-permute-start(bf16[1,2,2,80,128]{4,3,2,1,0:T(8,128)(2,1)S(1)} %get-tuple-element.40), channel_id=1, source_target_pairs={{0,4},{2,6},{4,0},{6,2},{1,5},{3,7},{5,1},{7,3},{8,12},{10,14},{12... | collective-permute-start | bytes 245768 | tf_op jit(solution)/shard_map/ppermute | solution.py:629
  37.2 4.8 %collective-permute-start.3 = (bf16[136,128]{1,0:T(8,128)(2,1)S(1)}, bf16[136,128]{1,0:T(8,128)(2,1)S(1)}, u32[]{:S(2)}, u32[]{:S(2)}) collective-permute-start(bf16[136,128]{1,0:T(8,128)(2,1)S(1)} %get-tuple-element.28.refs_2_.refs_9_), channel_id=1, source_target_pairs={{0,24},{8,16},{16,8},{24,0},{1,25},{9,17},{17,9},{25,1},{2,26},{10... | collective-permute-start | bytes 104456 | tf_op jit(solution)/shard_map/ppermute | solution.py:696
  39.6 3.9 %collective-permute-start.2 = (bf16[136,128]{1,0:T(8,128)(2,1)S(1)}, bf16[136,128]{1,0:T(8,128)(2,1)S(1)}, u32[]{:S(2)}, u32[]{:S(2)}) collective-permute-start(bf16[136,128]{1,0:T(8,128)(2,1)S(1)} %get-tuple-element.28.refs_2_.refs_9_), channel_id=1, source_target_pairs={{0,16},{8,24},{16,0},{24,8},{1,17},{9,25},{17,1},{25,9},{2,18},{10... | collective-permute-start | bytes 104456 | tf_op jit(solution)/shard_map/ppermute | solution.py:696
  40.1 3.9 %collective-permute-start.1 = (bf16[136,128]{1,0:T(8,128)(2,1)S(1)}, bf16[136,128]{1,0:T(8,128)(2,1)S(1)}, u32[]{:S(2)}, u32[]{:S(2)}) collective-permute-start(bf16[136,128]{1,0:T(8,128)(2,1)S(1)} %get-tuple-element.28.refs_2_.refs_9_), channel_id=1, source_target_pairs={{0,8},{8,0},{16,24},{24,16},{1,9},{9,1},{17,25},{25,17},{2,10},{10... | collective-permute-start | bytes 104456 | tf_op jit(solution)/shard_map/ppermute | solution.py:696
  57.6 1.5 %collective-permute-start.10 = (bf16[4,2,80,128]{3,2,1,0:T(8,128)(2,1)S(1)}, bf16[4,2,80,128]{3,2,1,0:T(8,128)(2,1)S(1)}, u32[]{:S(2)}, u32[]{:S(2)}) collective-permute-start(bf16[4,2,80,128]{3,2,1,0:T(8,128)(2,1)S(1)} %get-tuple-element.42), channel_id=1, source_target_pairs={{0,1},{1,0},{2,3},{3,2},{4,5},{5,4},{6,7},{7,6},{8,9},{9,8},{10,11... | collective-permute-start | bytes 491528 | tf_op jit(solution)/shard_map/ppermute | solution.py:696
  59.1 4.9 %collective-permute-start.11 = (bf16[2,2,80,128]{3,2,1,0:T(8,128)(2,1)S(1)}, bf16[2,2,80,128]{3,2,1,0:T(8,128)(2,1)S(1)}, u32[]{:S(2)}, u32[]{:S(2)}) collective-permute-start(bf16[2,2,80,128]{3,2,1,0:T(8,128)(2,1)S(1)} %get-tuple-element.44), channel_id=1, source_target_pairs={{0,8},{8,0},{16,24},{24,16},{1,9},{9,1},{17,25},{25,17},{2,10},{10... | collective-permute-start | bytes 245768 | tf_op jit(solution)/shard_map/ppermute | solution.py:696
  59.7 5.3 %collective-permute-start.12 = (bf16[2,2,80,128]{3,2,1,0:T(8,128)(2,1)S(1)}, bf16[2,2,80,128]{3,2,1,0:T(8,128)(2,1)S(1)}, u32[]{:S(2)}, u32[]{:S(2)}) collective-permute-start(bf16[2,2,80,128]{3,2,1,0:T(8,128)(2,1)S(1)} %get-tuple-element.45), channel_id=1, source_target_pairs={{0,16},{8,24},{16,0},{24,8},{1,17},{9,25},{17,1},{25,9},{2,18},{10... | collective-permute-start | bytes 245768 | tf_op jit(solution)/shard_map/ppermute | solution.py:696
  61.2 5.3 %collective-permute-start.13 = (bf16[2,2,80,128]{3,2,1,0:T(8,128)(2,1)S(1)}, bf16[2,2,80,128]{3,2,1,0:T(8,128)(2,1)S(1)}, u32[]{:S(2)}, u32[]{:S(2)}) collective-permute-start(bf16[2,2,80,128]{3,2,1,0:T(8,128)(2,1)S(1)} %get-tuple-element.46), channel_id=1, source_target_pairs={{0,24},{8,16},{16,8},{24,0},{1,25},{9,17},{17,9},{25,1},{2,26},{10... | collective-permute-start | bytes 245768 | tf_op jit(solution)/shard_map/ppermute | solution.py:696
